TPU v7x, 128 devices: a whole 4x4x4 slice. The times are simulated.
128 devices in a mesh: ctx: 128 (over y, z, x, core).
Axes of the slice: x: 4, y: 4, z: 4, core: 2. Of those that a mesh axis runs over, the one named last changes fastest.
Arguments:
- queries: bfloat16 [131072, 2048], P('ctx'), may hold values from -6 to 6
- keys: bfloat16 [131072, 2048], P('ctx'), may hold values from -6 to 6
- values: bfloat16 [131072, 2048], P('ctx'), may hold values from -6 to 6
- level_gate: bfloat16 [131072, 128], P('ctx'), may hold values from 0.19921875 to 2
- norm_gain: float32 [2048], replicated, may hold values from 0.5 to 1.5
- out_weight: bfloat16 [2048, 2048], P('ctx'), may hold values from -0.125 to 0.125
Outputs:
- layer_out: bfloat16 [131072, 2048], P('ctx')
All inputs are finite; a program needn't handle non-finite values.
Results may differ from a plain program's by a relative error of at most 0.0057.
Values may be sent and summed in bfloat16 or wider, within the bound.
No kernel may reach another device: no remote copies, remote signals or barrier semaphores. Data moves between devices by JAX's collectives and lax.ppermute only.
A program may use at most 192 MiB of HBM per device.

v0:
```python
import jax
import jax.numpy as jnp
from jax import lax
from jax.sharding import PartitionSpec as P

HEADS = 16
HEAD = 128
GATES = 8


EPSILON = 1e-06


def from_partner(value, axis, bit):
    mask = 2**bit
    pairs = [(source, source ^ mask) for source in range(lax.axis_size(axis))]
    return lax.ppermute(value, axis, pairs)


def shards(queries, keys, values, level_gate, norm_gain, out_weight):
    rows_here = queries.shape[0]
    query_heads = queries.reshape(rows_here, HEADS, HEAD)
    key_heads = keys.reshape(rows_here, HEADS, HEAD)
    value_heads = values.reshape(rows_here, HEADS, HEAD)
    level_weights = level_gate.reshape(rows_here, GATES, HEADS).astype(jnp.float32)
    scores = jnp.einsum("thd,shd->hts", query_heads, key_heads, preferred_element_type=jnp.float32)
    positions = jnp.arange(rows_here, dtype=jnp.int32)
    causal = positions[:, None] >= positions[None, :]
    weighted = jnp.where(causal[None], scores, jnp.float32(0.0)).astype(jnp.bfloat16)
    summed = jnp.einsum("hts,shd->thd", weighted, value_heads, preferred_element_type=jnp.float32)
    summed = summed * level_weights[:, 0, :, None]
    own_state = jnp.einsum(
        "shd,she->hde", key_heads, value_heads, preferred_element_type=jnp.float32
    )
    position = lax.axis_index("ctx")
    levels = lax.axis_size("ctx").bit_length() - 1
    running = own_state
    for level_index in range(levels):
        partner = from_partner(running, "ctx", level_index)
        upper_half = position >> level_index & 1 == 1
        bucket = jnp.where(upper_half, partner, jnp.float32(0.0)).astype(jnp.bfloat16)
        product = jnp.einsum(
            "thd,hde->the", query_heads, bucket, preferred_element_type=jnp.float32
        )
        summed = summed + level_weights[:, level_index + 1, :, None] * product
        if level_index + 1 < levels:
            running = running + partner
    squares = jnp.mean(summed * summed, axis=-1, keepdims=True)
    normed = summed * lax.rsqrt(squares + EPSILON) * norm_gain.reshape(HEADS, HEAD)
    normed = normed.reshape(rows_here, HEADS * HEAD).astype(jnp.bfloat16)
    whole_weight = lax.all_gather(out_weight, "ctx", axis=0, tiled=True)
    projected = jnp.dot(normed, whole_weight, preferred_element_type=jnp.float32)
    return projected.astype(jnp.bfloat16)


def solution(mesh):
    placed = (P("ctx", None), P("ctx", None), P("ctx", None), P("ctx", None), P(), P("ctx", None))
    return jax.shard_map(
        shards, mesh=mesh, in_specs=placed, out_specs=P("ctx", None), check_vma=False
    )
```

profile of v0, /device:TPU:1, one launch (start us, length us, event | category | flops | bytes accessed | tf_op | source)
XLA Modules:
  0.0 219.7 jit_solution(17310514026195994322)
XLA Ops:
  6.5 0.7 all-gather.2.cloned.1.call-update
  7.3 6.4 %copy.57 = bf16[1024,2048]{0,1:T(8,128)(2,1)} copy(bf16[1024,2048]{1,0:T(8,128)(2,1)} %param.7) | data formatting | bytes 8388608 | tf_op jit(solution)/shard_map/reshape | solution.py:23
  13.7 4.8 %fusion.13 = f32[16,128,128]{2,1,0:T(8,128)S(1)} fusion(bf16[1024,16,128]{0,2,1:T(8,128)(2,1)} %bitcast.129, bf16[1024,2048]{1,0:T(8,128)(2,1)} %param.8), kind=kOutput, calls=%fused_computation.23 | convolution fusion | flops 536870912 | bytes 9437184 | tf_op jit(solution)/shard_map/shd,she->hde/dot_general | solution.py:32
  18.5 1.5 collective-permute-start
  20.0 2.3 %collective-permute-done = f32[16,128,128]{2,1,0:T(8,128)S(1)} collective-permute-done((f32[16,128,128]{2,1,0:T(8,128)S(1)}, f32[16,128,128]{2,1,0:T(8,128)S(1)}, u32[]{:S(2)}, u32[]{:S(2)}) %collective-permute-start) | collective-permute-done | bytes 1048608 | tf_op jit(solution)/shard_map/ppermute | solution.py:17
  22.4 1.4 collective-permute-start.1
  23.8 24.8 %collective-permute-done.1 = f32[16,128,128]{2,1,0:T(8,128)S(1)} collective-permute-done((f32[16,128,128]{2,1,0:T(8,128)S(1)}, f32[16,128,128]{2,1,0:T(8,128)S(1)}, u32[]{:S(2)}, u32[]{:S(2)}) %collective-permute-start.1) | collective-permute-done | bytes 1048608 | tf_op jit(solution)/shard_map/ppermute | solution.py:17
  48.5 0.1 add.53
  48.7 2.9 %collective-permute-start.2 = (f32[16,128,128]{2,1,0:T(8,128)S(1)}, f32[16,128,128]{2,1,0:T(8,128)S(1)}, u32[]{:S(2)}, u32[]{:S(2)}) collective-permute-start(f32[16,128,128]{2,1,0:T(8,128)S(1)} %add.53), channel_id=1, source_target_pairs={{0,4},{1,5},{2,6},{3,7},{4,0},{5,1},{6,2},{7,3},{8,12},{9,13},{10,... | collective-permute-start | bytes 3145736 | tf_op jit(solution)/shard_map/ppermute | solution.py:17
  51.6 0.3 iota_compare_fusion
  51.9 23.8 %collective-permute-done.2 = f32[16,128,128]{2,1,0:T(8,128)S(1)} collective-permute-done((f32[16,128,128]{2,1,0:T(8,128)S(1)}, f32[16,128,128]{2,1,0:T(8,128)S(1)}, u32[]{:S(2)}, u32[]{:S(2)}) %collective-permute-start.2) | collective-permute-done | bytes 1048608 | tf_op jit(solution)/shard_map/ppermute | solution.py:17
  75.8 0.9 copy-done.4
  76.8 1.2 collective-permute-start.3
  77.9 23.5 %fusion = f32[16,1024,128]{1,2,0:T(8,128)} fusion(pred[1024,1024]{1,0:T(8,128)(4,1)S(1)} %iota_compare_fusion, bf16[1024,16,128]{0,2,1:T(8,128)(2,1)} %bitcast.130, bf16[1024,2048]{1,0:T(8,128)(2,1)} %param.8, bf16[1024,2048]{1,0:T(8,128)(2,1)} %param.6), kind=kOutput, calls=%fused_computation.1 | convolution fusion | flops 8623489024 | bytes 22020096 | tf_op jit(solution)/shard_map/hts,shd->thd/dot_general | solution.py:30
  101.4 0.1 copy.33
  101.7 4.2 %fusion.29 = f32[16,128,1024]{2,1,0:T(8,128)S(1)} fusion(f32[16,128,128]{2,1,0:T(8,128)} %copy-done.3, pred[]{:T(512)S(6)} %eq.21, bf16[1024,2048]{1,0:T(8,128)(2,1)} %param.6), kind=kOutput, calls=%fused_computation.38 | convolution fusion | flops 537133056 | bytes 13631489 | tf_op jit(solution)/shard_map/thd,hde->the/dot_general | solution.py:42
  105.9 5.7 %collective-permute-done.3 = f32[16,128,128]{2,1,0:T(8,128)} collective-permute-done((f32[16,128,128]{2,1,0:T(8,128)S(1)}, f32[16,128,128]{2,1,0:T(8,128)}, u32[]{:S(2)}, u32[]{:S(2)}) %collective-permute-start.3) | collective-permute-done | bytes 1048608 | tf_op jit(solution)/shard_map/ppermute | solution.py:17
  111.6 1.3 add.57
  113.0 3.0 %collective-permute-start.4 = (f32[16,128,128]{2,1,0:T(8,128)S(1)}, f32[16,128,128]{2,1,0:T(8,128)S(1)}, u32[]{:S(2)}, u32[]{:S(2)}) collective-permute-start(f32[16,128,128]{2,1,0:T(8,128)S(1)} %add.57), channel_id=1, source_target_pairs={{0,16},{1,17},{2,18},{3,19},{4,20},{5,21},{6,22},{7,23},{8,24},{9,... | collective-permute-start | bytes 3145736 | tf_op jit(solution)/shard_map/ppermute | solution.py:17
  116.0 4.6 %fusion.25 = f32[16,128,1024]{2,1,0:T(8,128)} fusion(f32[16,128,128]{2,1,0:T(8,128)S(1)} %copy-done.2, pred[]{:T(512)S(6)} %eq.22, bf16[1024,2048]{1,0:T(8,128)(2,1)S(1)} %copy-done), kind=kOutput, calls=%fused_computation.35 | convolution fusion | flops 537133056 | bytes 13631489 | tf_op jit(solution)/shard_map/thd,hde->the/dot_general | solution.py:42
  120.6 4.6 %fusion.23 = f32[16,128,1024]{2,1,0:T(8,128)} fusion(f32[16,128,128]{2,1,0:T(8,128)S(1)} %copy-done.5, pred[]{:T(512)S(6)} %eq.23, bf16[1024,2048]{1,0:T(8,128)(2,1)S(1)} %copy-done), kind=kOutput, calls=%fused_computation.33 | convolution fusion | flops 537133056 | bytes 13631489 | tf_op jit(solution)/shard_map/thd,hde->the/dot_general | solution.py:42
  125.2 11.9 %collective-permute-done.4 = f32[16,128,128]{2,1,0:T(8,128)S(1)} collective-permute-done((f32[16,128,128]{2,1,0:T(8,128)S(1)}, f32[16,128,128]{2,1,0:T(8,128)S(1)}, u32[]{:S(2)}, u32[]{:S(2)}) %collective-permute-start.4) | collective-permute-done | bytes 1048608 | tf_op jit(solution)/shard_map/ppermute | solution.py:17
  137.2 1.6 collective-permute-start.5
  138.8 4.6 %fusion.21 = f32[16,128,1024]{2,1,0:T(8,128)} fusion(f32[16,128,128]{2,1,0:T(8,128)} %collective-permute-done.3, pred[]{:T(512)S(6)} %eq.24, bf16[1024,2048]{1,0:T(8,128)(2,1)S(1)} %copy-done), kind=kOutput, calls=%fused_computation.31 | convolution fusion | flops 537133056 | bytes 13631489 | tf_op jit(solution)/shard_map/thd,hde->the/dot_general | solution.py:42
  143.4 4.6 %fusion.19 = f32[16,128,1024]{2,1,0:T(8,128)} fusion(f32[16,128,128]{2,1,0:T(8,128)S(1)} %collective-permute-done.4, pred[]{:T(512)S(6)} %eq.25, bf16[1024,2048]{1,0:T(8,128)(2,1)S(1)} %copy-done), kind=kOutput, calls=%fused_computation.29 | convolution fusion | flops 537133056 | bytes 13631489 | tf_op jit(solution)/shard_map/thd,hde->the/dot_general | solution.py:42
  148.0 10.8 %collective-permute-done.5 = f32[16,128,128]{2,1,0:T(8,128)S(1)} collective-permute-done((f32[16,128,128]{2,1,0:T(8,128)S(1)}, f32[16,128,128]{2,1,0:T(8,128)S(1)}, u32[]{:S(2)}, u32[]{:S(2)}) %collective-permute-start.5) | collective-permute-done | bytes 1048608 | tf_op jit(solution)/shard_map/ppermute | solution.py:17
  159.0 4.8 %collective-permute-start.6 = (bf16[16,128,128]{2,1,0:T(8,128)(2,1)S(1)}, bf16[16,128,128]{2,1,0:T(8,128)(2,1)S(1)}, u32[]{:S(2)}, u32[]{:S(2)}) collective-permute-start(bf16[16,128,128]{2,1,0:T(8,128)(2,1)S(1)} %add.61), channel_id=1, source_target_pairs={{0,64},{1,65},{2,66},{3,67},{4,68},{5,69},{6,70},{7,71},{8,72},{9,... | collective-permute-start | bytes 1572872 | tf_op jit(solution)/shard_map/ppermute | solution.py:17
  163.8 4.6 %fusion.17 = f32[16,128,1024]{2,1,0:T(8,128)} fusion(f32[16,128,128]{2,1,0:T(8,128)S(1)} %collective-permute-done.5, pred[]{:T(512)S(6)} %eq.26, bf16[1024,2048]{1,0:T(8,128)(2,1)S(1)} %copy-done), kind=kOutput, calls=%fused_computation.27 | convolution fusion | flops 537133056 | bytes 13631489 | tf_op jit(solution)/shard_map/thd,hde->the/dot_general | solution.py:42
  168.4 4.3 %collective-permute-done.6 = bf16[16,128,128]{2,1,0:T(8,128)(2,1)S(1)} collective-permute-done((bf16[16,128,128]{2,1,0:T(8,128)(2,1)S(1)}, bf16[16,128,128]{2,1,0:T(8,128)(2,1)S(1)}, u32[]{:S(2)}, u32[]{:S(2)}) %collective-permute-start.6) | collective-permute-done | bytes 524320 | tf_op jit(solution)/shard_map/ppermute | solution.py:17
  172.8 20.8 %multiply_reduce_fusion = (f32[1024,16]{0,1:T(8,128)S(1)}, f32[1024,16,128]{0,2,1:T(8,128)}) fusion(bf16[16,128,128]{2,1,0:T(8,128)(2,1)S(1)} %collective-permute-done.6, pred[]{:T(512)S(6)} %eq.27, f32[1024,16]{0,1:T(8,128)S(1)} %get-tuple-element.6, f32[16,128,1024]{2,1,0:T(8,128)} %fusion.17, f32[1024,16]{0,1:T(8,128)S(1)} %get-tuple-element.7, ...), kind=kOutput, calls=%fused_computation.21 | convolution fusion | flops 572768256 | bytes 72417280 | tf_op jit(solution)/shard_map/thd,hde->the/dot_general | solution.py:42
  193.6 5.3 %multiply_convert_fusion = bf16[1024,16,128]{0,2,1:T(8,128)(2,1)} fusion(f32[1024,16,128]{0,2,1:T(8,128)} %get-tuple-element.14, f32[16,128]{1,0:T(8,128)S(1)} %bitcast.133, f32[1024,16]{0,1:T(8,128)S(1)} %add_rsqrt_fusion), kind=kLoop, calls=%fused_computation.20 | loop fusion | flops 6291456 | bytes 12656640 | tf_op jit(solution)/shard_map/convert_element_type | solution.py:50
  198.9 14.0 %convolution_convert_fusion = bf16[1024,2048]{1,0:T(8,128)(2,1)} fusion(bf16[1024,2048]{0,1:T(8,128)(2,1)} %bitcast.131, bf16[2048,2048]{1,0:T(8,128)(2,1)} %all-gather.2.cloned.1.call-done), kind=kOutput, calls=%fused_computation.41 | convolution fusion | flops 8592031744 | bytes 16777216 | tf_op jit(solution)/shard_map/dot_general | solution.py:52
  (24 shorter events, 0.6 us)
Async XLA Ops:
  6.5 192.4 %all-gather.2.cloned.1.call-start = ((), (), s32[]{:S(2)}) async-start(), calls=%async_computation | async-start | bytes 8454144 | tf_op jit(solution)/shard_map/all_gather | solution.py:51
  18.5 3.7 %collective-permute-start = (f32[16,128,128]{2,1,0:T(8,128)S(1)}, f32[16,128,128]{2,1,0:T(8,128)S(1)}, u32[]{:S(2)}, u32[]{:S(2)}) collective-permute-start(f32[16,128,128]{2,1,0:T(8,128)S(1)} %fusion.13), channel_id=1, source_target_pairs={{0,1},{1,0},{2,3},{3,2},{4,5},{5,4},{6,7},{7,6},{8,9},{9,8},{10,11... | collective-permute-start | bytes 3145736 | tf_op jit(solution)/shard_map/ppermute | solution.py:17
  22.2 1.5 copy-start.3
  22.4 26.2 %collective-permute-start.1 = (f32[16,128,128]{2,1,0:T(8,128)S(1)}, f32[16,128,128]{2,1,0:T(8,128)S(1)}, u32[]{:S(2)}, u32[]{:S(2)}) collective-permute-start(f32[16,128,128]{2,1,0:T(8,128)S(1)} %add.51), channel_id=1, source_target_pairs={{0,2},{1,3},{2,0},{3,1},{4,6},{5,7},{6,4},{7,5},{8,10},{9,11},{10,... | collective-permute-start | bytes 3145736 | tf_op jit(solution)/shard_map/ppermute | solution.py:17
  48.5 27.3 %copy-start.1 = (f32[16,128,128]{2,1,0:T(8,128)}, f32[16,128,128]{2,1,0:T(8,128)S(1)}, u32[]{:S(2)}) copy-start(f32[16,128,128]{2,1,0:T(8,128)S(1)} %collective-permute-done.1) | copy-start | bytes 3145732
  48.7 27.0 %collective-permute-start.2 = (f32[16,128,128]{2,1,0:T(8,128)S(1)}, f32[16,128,128]{2,1,0:T(8,128)S(1)}, u32[]{:S(2)}, u32[]{:S(2)}) collective-permute-start(f32[16,128,128]{2,1,0:T(8,128)S(1)} %add.53), channel_id=1, source_target_pairs={{0,4},{1,5},{2,6},{3,7},{4,0},{5,1},{6,2},{7,3},{8,12},{9,13},{10,... | collective-permute-start | bytes 3145736 | tf_op jit(solution)/shard_map/ppermute | solution.py:17
  75.7 1.1 copy-start.4
  76.7 24.7 %copy-start.6 = (bf16[1024,128]{1,0:T(8,128)(2,1)S(1)}, bf16[1024,128]{1,0:T(8,128)(2,1)}, u32[]{:S(2)}) copy-start(bf16[1024,128]{1,0:T(8,128)(2,1)} %param.9) | copy-start | bytes 786436
  76.8 34.9 %collective-permute-start.3 = (f32[16,128,128]{2,1,0:T(8,128)S(1)}, f32[16,128,128]{2,1,0:T(8,128)}, u32[]{:S(2)}, u32[]{:S(2)}) collective-permute-start(f32[16,128,128]{2,1,0:T(8,128)S(1)} %add.55), channel_id=1, source_target_pairs={{0,8},{1,9},{2,10},{3,11},{4,12},{5,13},{6,14},{7,15},{8,0},{9,1},... | collective-permute-start | bytes 3145736 | tf_op jit(solution)/shard_map/ppermute | solution.py:17
  101.7 14.3 %copy-start = (bf16[1024,2048]{1,0:T(8,128)(2,1)S(1)}, bf16[1024,2048]{1,0:T(8,128)(2,1)}, u32[]{:S(2)}) copy-start(bf16[1024,2048]{1,0:T(8,128)(2,1)} %param.6) | copy-start | bytes 12582916
  101.7 14.3 %copy-start.2 = (f32[16,128,128]{2,1,0:T(8,128)S(1)}, f32[16,128,128]{2,1,0:T(8,128)}, u32[]{:S(2)}) copy-start(f32[16,128,128]{2,1,0:T(8,128)} %copy-done.1) | copy-start | bytes 3145732
  113.0 7.6 %copy-start.5 = (f32[16,128,128]{2,1,0:T(8,128)S(1)}, f32[16,128,128]{2,1,0:T(8,128)}, u32[]{:S(2)}) copy-start(f32[16,128,128]{2,1,0:T(8,128)} %copy-done.4) | copy-start | bytes 3145732
  113.0 24.1 %collective-permute-start.4 = (f32[16,128,128]{2,1,0:T(8,128)S(1)}, f32[16,128,128]{2,1,0:T(8,128)S(1)}, u32[]{:S(2)}, u32[]{:S(2)}) collective-permute-start(f32[16,128,128]{2,1,0:T(8,128)S(1)} %add.57), channel_id=1, source_target_pairs={{0,16},{1,17},{2,18},{3,19},{4,20},{5,21},{6,22},{7,23},{8,24},{9,... | collective-permute-start | bytes 3145736 | tf_op jit(solution)/shard_map/ppermute | solution.py:17
  137.2 21.6 %collective-permute-start.5 = (f32[16,128,128]{2,1,0:T(8,128)S(1)}, f32[16,128,128]{2,1,0:T(8,128)S(1)}, u32[]{:S(2)}, u32[]{:S(2)}) collective-permute-start(f32[16,128,128]{2,1,0:T(8,128)S(1)} %add.59), channel_id=1, source_target_pairs={{0,32},{1,33},{2,34},{3,35},{4,36},{5,37},{6,38},{7,39},{8,40},{9,... | collective-permute-start | bytes 3145736 | tf_op jit(solution)/shard_map/ppermute | solution.py:17
  159.0 13.8 %collective-permute-start.6 = (bf16[16,128,128]{2,1,0:T(8,128)(2,1)S(1)}, bf16[16,128,128]{2,1,0:T(8,128)(2,1)S(1)}, u32[]{:S(2)}, u32[]{:S(2)}) collective-permute-start(bf16[16,128,128]{2,1,0:T(8,128)(2,1)S(1)} %add.61), channel_id=1, source_target_pairs={{0,64},{1,65},{2,66},{3,67},{4,68},{5,69},{6,70},{7,71},{8,72},{9,... | collective-permute-start | bytes 1572872 | tf_op jit(solution)/shard_map/ppermute | solution.py:17
  172.7 20.9 %copy-start.7 = (f32[2048]{0:T(1024)S(1)}, f32[2048]{0:T(1024)}, u32[]{:S(2)}) copy-start(f32[2048]{0:T(1024)} %param.10) | copy-start | bytes 24580
Sparse Core Ops, SparseCore 0:
  10.3 101.7 all-gather.1
where the time goes:
time: 223 us; the launch traced here: 220 us
  matrix products  90.4 us (41%)
  waiting for transfers between devices  84.3 us (38%)
  starting transfers between devices  16.3 us (7%)
  between operations  13.5 us (6%)
  other arithmetic  7.6 us (3%)
  local copies, waits for them, and re-layouts  7.53 us (3%)
    ppermute x7, waiting for transfers between devices, from_partner(): return lax.ppermute(value, axis, pairs)  83.6 us
    dot_general x7, matrix products, shards(): jnp.einsum('thd,hde->the', query_heads, bucket, preferred_element_type=jn...  48.1 us
    dot_general x1, matrix products, shards(): jnp.einsum('hts,shd->thd', weighted, value_heads, preferred_element_type=...  23.5 us
    ppermute x7, starting transfers between devices, from_partner(): return lax.ppermute(value, axis, pairs)  16.3 us
    dot_general x1, matrix products, shards(): jnp.dot(normed, whole_weight, preferred_element_type=jnp.float32)  14 us
    reshape x1, local copies, waits for them, and re-layouts, shards(): key_heads = keys.reshape(rows_here, HEADS, HEAD)  6.4 us
    convert_element_type x1, other arithmetic, shards(): normed = normed.reshape(rows_here, HEADS * HEAD).astype(jnp.bfloat16)  5.29 us
    dot_general x1, matrix products, shards(): jnp.einsum('shd,she->hde', key_heads, value_heads, preferred_element_type...  4.83 us
  transfers between devices with their start and end apart: 8, of which 7 were waited for; matrix products, arithmetic and copies ran while one was open for 41% of the time, Pallas kernels for 0%

commit v1 on v0

v1 whole, which is shorter than its diff:
```python
import functools

import jax
import jax.numpy as jnp
from jax import lax
from jax.experimental import pallas as pl
from jax.experimental.pallas import tpu as pltpu
from jax.sharding import PartitionSpec as P

HEADS = 16
HEAD = 128
GATES = 8
HALF = HEADS // 2
ROWS = 1024
CHUNK = 256
CHUNKS = ROWS // CHUNK
EPSILON = 1e-06
VMEM_MIB = 60
F32 = jnp.float32
BF16 = jnp.bfloat16


def params(mib, **more):
    return pltpu.CompilerParams(vmem_limit_bytes=mib << 20, **more)


def cost(flops, moved):
    return pl.CostEstimate(flops=int(flops), bytes_accessed=int(moved), transcendentals=0)


def dot(a, b, contract=((1,), (0,))):
    return lax.dot_general(a, b, (contract, ((), ())), preferred_element_type=F32)


def state_body(k_ref, v_ref, total_ref, sent_ref, prefix_ref):
    for pair in range(2):
        cols = slice(pair * HEAD, (pair + 1) * HEAD)
        total = None
        for c in range(CHUNKS):
            rows = slice(c * CHUNK, (c + 1) * CHUNK)
            part = dot(k_ref[rows, cols], v_ref[rows, cols], ((0,), (0,)))
            total = part if total is None else total + part
            if c + 1 < CHUNKS:
                prefix_ref[pair, c] = total.astype(BF16)
        total_ref[pair] = total
        sent_ref[pair] = total.astype(BF16)


def states(keys, values):
    block = pl.BlockSpec((ROWS, 2 * HEAD), lambda i: (0, i))
    square = pl.BlockSpec((2, HEAD, HEAD), lambda i: (i, 0, 0))
    return pl.pallas_call(
        state_body,
        grid=(HEADS // 2,),
        in_specs=[block, block],
        out_specs=[square, square, pl.BlockSpec((2, CHUNKS - 1, HEAD, HEAD), lambda i: (i, 0, 0, 0))],
        out_shape=[
            jax.ShapeDtypeStruct((HEADS, HEAD, HEAD), F32),
            jax.ShapeDtypeStruct((HEADS, HEAD, HEAD), BF16),
            jax.ShapeDtypeStruct((HEADS, CHUNKS - 1, HEAD, HEAD), BF16),
        ],
        compiler_params=params(VMEM_MIB),
        cost_estimate=cost(2 * ROWS * HEAD * HEAD * HEADS, 10 << 20),
        name="states",
    )(keys, values)


def local_body(side, s_ref, q_ref, k_ref, v_ref, prefix_ref, gate_ref, out_ref):
    core = s_ref[0] if side == 0 else 1 - s_ref[0]
    first = core * HALF + 2 * pl.program_id(0)
    causal = lax.broadcasted_iota(jnp.int32, (CHUNK, CHUNK), 0) >= lax.broadcasted_iota(
        jnp.int32, (CHUNK, CHUNK), 1
    )
    for pair in range(2):
        cols = slice(pair * HEAD, (pair + 1) * HEAD)
        shift = lax.rem(HEAD - (first + pair), HEAD)
        for c in range(CHUNKS):
            rows = slice(c * CHUNK, (c + 1) * CHUNK)
            q = q_ref[rows, cols]
            scores = dot(q, k_ref[rows, cols], ((1,), (1,)))
            scores = jnp.where(causal, scores, 0.0).astype(BF16)
            mixed = dot(scores, v_ref[rows, cols])
            if c:
                mixed = mixed + dot(q, prefix_ref[pair, c - 1])
            weight = pltpu.roll(gate_ref[rows, :].astype(F32), shift, 1)[:, 0:1]
            out_ref[rows, cols] = mixed * weight


def local(side, scalars, queries, keys, values, prefix, level_gate):
    quarter = HALF // 2
    where = lambda i, s: (s[0] if side == 0 else 1 - s[0]) * quarter + i
    block = pl.BlockSpec((ROWS, 2 * HEAD), lambda i, s: (0, where(i, s)))
    return pl.pallas_call(
        functools.partial(local_body, side),
        grid_spec=pltpu.PrefetchScalarGridSpec(
            num_scalar_prefetch=1,
            grid=(quarter,),
            in_specs=[
                block,
                block,
                block,
                pl.BlockSpec((2, CHUNKS - 1, HEAD, HEAD), lambda i, s: (where(i, s), 0, 0, 0)),
                pl.BlockSpec((ROWS, GATES * HEADS), lambda i, s: (0, 0)),
            ],
            out_specs=pl.BlockSpec((ROWS, 2 * HEAD), lambda i, s: (0, i)),
        ),
        out_shape=jax.ShapeDtypeStruct((ROWS, HALF * HEAD), F32),
        compiler_params=params(VMEM_MIB),
        cost_estimate=cost(4e9, 11 << 20),
        name=f"local{side}",
    )(scalars, queries, keys, values, prefix, level_gate)


def add_levels(scalars, head, q, gate, attended, levels, buckets):
    shift = lax.rem(HEAD - head, HEAD)
    rolled = pltpu.roll(gate, shift, 1)
    at = 0
    while at < len(levels):
        group = levels[at : at + 2]
        square = jnp.concatenate(buckets[at : at + 2], axis=1)
        product = dot(q, square)
        for n, level in enumerate(group):
            flag = scalars[1 + level].astype(F32)
            column = (level + 1) * HEADS
            weight = rolled[:, column : column + 1] * flag
            attended = attended + product[:, n * HEAD : (n + 1) * HEAD] * weight
        at += 2
    return attended


def head_maps():
    mine = lambda i, s: s[0] * HALF + i
    yours = lambda i, s: (1 - s[0]) * HALF + i
    return mine, yours


def final_body(levels, s_ref, q0, q1, a0, a1, gate_ref, gain_ref, *refs):
    buckets = refs[: 2 * len(levels)]
    weight_ref, out_ref, normed_ref = refs[2 * len(levels) :]
    i = pl.program_id(0)
    core = s_ref[0]

    @pl.when(i < HALF)
    def _():
        for side, (q, a) in enumerate(((q0, a0), (q1, a1))):
            head = (core if side == 0 else 1 - core) * HALF + i
            squares = [buckets[2 * n + side][0] for n in range(len(levels))]
            gain = gain_ref[pl.ds(head, 1), :]
            cols = pl.ds(pl.multiple_of(head * HEAD, HEAD), HEAD)
            for c in range(CHUNKS):
                rows = slice(c * CHUNK, (c + 1) * CHUNK)
                x = add_levels(
                    s_ref, head, q[rows, :], gate_ref[rows, :].astype(F32), a[rows, :], levels, squares
                )
                squares_mean = jnp.mean(x * x, axis=1, keepdims=True)
                normed_ref[rows, cols] = (x * lax.rsqrt(squares_mean + EPSILON) * gain).astype(BF16)

    @pl.when(i >= HALF)
    def _():
        out_ref[...] = dot(normed_ref[...], weight_ref[...]).astype(BF16)


def final(scalars, queries, attended, level_gate, gain, levels, buckets, weight):
    mine, yours = head_maps()
    clip = lambda i: jnp.minimum(i, HALF - 1)
    tile = HEADS * HEAD // HALF
    col0 = lambda i, s: (0, mine(clip(i), s))
    col1 = lambda i, s: (0, yours(clip(i), s))
    own = pl.BlockSpec((1, HEAD, HEAD), lambda i, s: (clip(i), 0, 0))
    specs = []
    for level in levels:
        if level == 0:
            specs += [
                pl.BlockSpec((1, HEAD, HEAD), lambda i, s: (mine(clip(i), s), 0, 0)),
                pl.BlockSpec((1, HEAD, HEAD), lambda i, s: (yours(clip(i), s), 0, 0)),
            ]
        else:
            specs += [own, own]
    late = lambda i, s: (0, jnp.maximum(i - HALF, 0))
    return pl.pallas_call(
        functools.partial(final_body, levels),
        grid_spec=pltpu.PrefetchScalarGridSpec(
            num_scalar_prefetch=1,
            grid=(2 * HALF,),
            in_specs=[
                pl.BlockSpec((ROWS, HEAD), col0),
                pl.BlockSpec((ROWS, HEAD), col1),
                pl.BlockSpec((ROWS, HEAD), lambda i, s: (0, clip(i))),
                pl.BlockSpec((ROWS, HEAD), lambda i, s: (0, clip(i))),
                pl.BlockSpec((ROWS, GATES * HEADS), lambda i, s: (0, 0)),
                pl.BlockSpec((HEADS, HEAD), lambda i, s: (0, 0)),
                *specs,
                pl.BlockSpec((HEADS * HEAD, tile), late),
            ],
            out_specs=pl.BlockSpec((ROWS, tile), late),
            scratch_shapes=[pltpu.VMEM((ROWS, HEADS * HEAD), BF16)],
        ),
        out_shape=jax.ShapeDtypeStruct((ROWS, HEADS * HEAD), BF16),
        compiler_params=params(VMEM_MIB),
        cost_estimate=cost(13e9, 30 << 20),
        name="final",
    )(scalars, queries, queries, *attended, level_gate, gain, *buckets, weight)


def from_partner(value, axis, bit):
    mask = 2**bit
    pairs = [(source, source ^ mask) for source in range(lax.axis_size(axis))]
    return lax.ppermute(value, axis, pairs)


def shards(queries, keys, values, level_gate, norm_gain, out_weight):
    position = lax.axis_index("ctx")
    levels = lax.axis_size("ctx").bit_length() - 1
    core = position & 1
    scalars = jnp.stack([core] + [position >> level & 1 for level in range(levels)]).astype(jnp.int32)
    whole_weight = lax.all_gather(out_weight, "ctx", axis=0, tiled=True)
    total, sent, prefix = states(keys, values)
    first = from_partner(sent, "ctx", 0)
    attended = [None, None]
    buckets = [first, first]
    running = lax.dynamic_slice_in_dim(total, core * HALF, HALF) + lax.dynamic_slice_in_dim(
        first, core * HALF, HALF
    ).astype(F32)
    for level in range(1, levels):
        outgoing = running.astype(BF16)
        if level == 1:
            outgoing, q_a = lax.optimization_barrier((outgoing, queries))
            attended[0] = local(0, scalars, q_a, keys, values, prefix, level_gate)
        if level == 3:
            outgoing, q_b, attended[0] = lax.optimization_barrier((outgoing, queries, attended[0]))
            attended[1] = local(1, scalars, q_b, keys, values, prefix, level_gate)
        if level == 5:
            outgoing, attended[1] = lax.optimization_barrier((outgoing, attended[1]))
        received = from_partner(outgoing, "ctx", level)
        other = from_partner(received, "ctx", 0)
        buckets += [received, other]
        if level + 1 < levels:
            running = running + received.astype(F32)
    gain = norm_gain.reshape(HEADS, HEAD)
    return final(
        scalars, queries, attended, level_gate, gain, list(range(levels)), buckets, whole_weight
    )


def solution(mesh):
    placed = (P("ctx", None), P("ctx", None), P("ctx", None), P("ctx", None), P(), P("ctx", None))
    return jax.shard_map(
        shards, mesh=mesh, in_specs=placed, out_specs=P("ctx", None), check_vma=False
    )
```

time: 223 us -> 147 us (0.66); the launches traced: 220 us -> 147 us
  matrix products: 90.4 us -> 0 us
  Pallas kernels: 0 us -> 73.7 us
  waiting for transfers between devices: 84.3 us -> 14.6 us
  starting transfers between devices: 16.3 us -> 40.9 us
  local copies, waits for them, and re-layouts: 7.53 us -> 1.32 us
  other arithmetic: 7.6 us -> 2.92 us
    dot_general x10 -> x0, matrix products: 90.4 us -> none  [the longest x7 48.1 us: shards(): jnp.einsum('thd,hde->the', query_heads, bucket, preferred_element_type=jn...]
    pallas_call x0 -> x4, Pallas kernels: none -> 73.7 us  [the longest x1 47.7 us: final(): pl.pallas_call(functools.partial(final_body, levels), grid_spec=pltpu.Pre...]
    ppermute x7 -> x13, waiting for transfers between devices: 83.6 us -> 13.9 us  [from_partner(): return lax.ppermute(value, axis, pairs)]
    ppermute x7 -> x13, starting transfers between devices: 16.3 us -> 40.9 us  [from_partner(): return lax.ppermute(value, axis, pairs)]
    reshape x1 -> x0, local copies, waits for them, and re-layouts: 6.4 us -> none  [shards(): key_heads = keys.reshape(rows_here, HEADS, HEAD)]
    convert_element_type x2 -> x6, other arithmetic: 5.33 us -> 2.92 us  [shards(): outgoing = running.astype(BF16)]
  transfers between devices with their start and end apart: 8 -> 14, of which waited for: 7 -> 4; matrix products, arithmetic and copies ran while one was open for 41% -> 2% of each run, Pallas kernels for 0% -> 18%
where the time goes in v1:
time: 147 us
  Pallas kernels  73.7 us (50%)
  starting transfers between devices  40.9 us (28%)
  waiting for transfers between devices  14.6 us (10%)
  between operations  13.6 us (9%)
  other arithmetic  2.92 us (2%)
    pallas_call x1, Pallas kernels, final(): pl.pallas_call(functools.partial(final_body, levels), grid_spec=pltpu.Pre...  47.7 us
    ppermute x13, starting transfers between devices, from_partner(): return lax.ppermute(value, axis, pairs)  40.9 us
    pallas_call x2, Pallas kernels, local(): pl.pallas_call(functools.partial(local_body, side), grid_spec=pltpu.Prefe...  17.6 us
    ppermute x13, waiting for transfers between devices, from_partner(): return lax.ppermute(value, axis, pairs)  13.9 us
    pallas_call x1, Pallas kernels, states(): pl.pallas_call(state_body, grid=(HEADS // 2,), in_specs=[block, block], o...  8.29 us
  transfers between devices with their start and end apart: 14, of which 4 were waited for; matrix products, arithmetic and copies ran while one was open for 2% of the time, Pallas kernels for 18%

profile of v1, /device:TPU:1, one launch (start us, length us, event | category | flops | bytes accessed | tf_op | source)
XLA Modules:
  0.0 146.9 jit_solution(762240448095185644)
XLA Ops:
  6.5 0.7 all-gather.2.cloned.1.call-update
  7.3 8.3 %states.1 = (f32[16,128,128]{2,1,0:T(8,128)}, bf16[16,128,128]{2,1,0:T(8,128)(2,1)}, bf16[16,3,128,128]{3,2,1,0:T(8,128)(2,1)}) custom-call(bf16[1024,2048]{1,0:T(8,128)(2,1)} %k_ref.5, bf16[1024,2048]{1,0:T(8,128)(2,1)} %v_ref.5), custom_call_target="tpu_custom_call" | custom-call | flops 536870912 | bytes 10485760 | tf_op jit(solution)/shard_map/states/pallas_call | solution.py:52
  15.5 1.4 collective-permute-start
  16.9 1.7 %collective-permute-done.refs_0_.refs_1_ = bf16[16,128,128]{2,1,0:T(8,128)(2,1)S(1)} collective-permute-done((bf16[16,128,128]{2,1,0:T(8,128)(2,1)}, bf16[16,128,128]{2,1,0:T(8,128)(2,1)S(1)}, u32[]{:S(2)}, u32[]{:S(2)}) %collective-permute-start) | collective-permute-done | bytes 524320 | tf_op jit(solution)/shard_map/ppermute | solution.py:208
  18.7 1.3 fusion.3
  20.0 1.4 collective-permute-start.1
  21.4 0.6 stack.35.s_ref
  22.0 5.9 %collective-permute-done.1.refs_2_ = bf16[8,128,128]{2,1,0:T(8,128)(2,1)S(1)} collective-permute-done((bf16[8,128,128]{2,1,0:T(8,128)(2,1)S(1)}, bf16[8,128,128]{2,1,0:T(8,128)(2,1)S(1)}, u32[]{:S(2)}, u32[]{:S(2)}) %collective-permute-start.1) | collective-permute-done | bytes 262176 | tf_op jit(solution)/shard_map/ppermute | solution.py:208
  27.9 1.2 fusion
  29.1 3.0 %collective-permute-start.2 = (bf16[8,128,128]{2,1,0:T(8,128)(2,1)S(1)}, bf16[8,128,128]{2,1,0:T(8,128)(2,1)S(1)}, u32[]{:S(2)}, u32[]{:S(2)}) collective-permute-start(bf16[8,128,128]{2,1,0:T(8,128)(2,1)S(1)} %fusion), channel_id=1, source_target_pairs={{0,4},{1,5},{2,6},{3,7},{4,0},{5,1},{6,2},{7,3},{8,12},{9,13},{10,... | collective-permute-start | bytes 786440 | tf_op jit(solution)/shard_map/ppermute | solution.py:208
  32.1 8.9 %local0.1.a0 = f32[1024,1024]{1,0:T(8,128)} custom-call(s32[8]{0:T(128)} %stack.35.s_ref, bf16[1024,2048]{1,0:T(8,128)(2,1)} %q1.1, bf16[1024,2048]{1,0:T(8,128)(2,1)} %k_ref.5, bf16[1024,2048]{1,0:T(8,128)(2,1)} %v_ref.5, bf16[16,3,128,128]{3,2,1,0:T(8,128)(2,1)} %get-tuple-element.19.prefix_ref, bf16[1024,128]{1,0:T(8,128)(2,1)} %gate_ref.5), custom_call_target="tpu_custom_call" | custom-call | flops 4000000000 | bytes 11534336 | tf_op jit(solution)/shard_map/local0/pallas_call | solution.py:93
  41.0 0.1 fusion.4
  41.1 1.7 %collective-permute-start.3 = (bf16[8,128,128]{2,1,0:T(8,128)(2,1)S(1)}, bf16[8,128,128]{2,1,0:T(8,128)(2,1)S(1)}, u32[]{:S(2)}, u32[]{:S(2)}) collective-permute-start(bf16[8,128,128]{2,1,0:T(8,128)(2,1)S(1)} %get-tuple-element.21), channel_id=1, source_target_pairs={{0,8},{1,9},{2,10},{3,11},{4,12},{5,13},{6,14},{7,15},{8,0},{9,1},... | collective-permute-start | bytes 786440 | tf_op jit(solution)/shard_map/ppermute | solution.py:208
  42.8 5.1 %collective-permute-done.3.refs_6_ = bf16[8,128,128]{2,1,0:T(8,128)(2,1)S(1)} collective-permute-done((bf16[8,128,128]{2,1,0:T(8,128)(2,1)S(1)}, bf16[8,128,128]{2,1,0:T(8,128)(2,1)S(1)}, u32[]{:S(2)}, u32[]{:S(2)}) %collective-permute-start.3) | collective-permute-done | bytes 262176 | tf_op jit(solution)/shard_map/ppermute | solution.py:208
  48.0 0.1 fusion.1
  48.0 3.4 %collective-permute-start.4 = (bf16[8,128,128]{2,1,0:T(8,128)(2,1)S(1)}, bf16[8,128,128]{2,1,0:T(8,128)(2,1)S(1)}, u32[]{:S(2)}, u32[]{:S(2)}) collective-permute-start(bf16[8,128,128]{2,1,0:T(8,128)(2,1)S(1)} %fusion.1), channel_id=1, source_target_pairs={{0,16},{1,17},{2,18},{3,19},{4,20},{5,21},{6,22},{7,23},{8,24},{9,... | collective-permute-start | bytes 786440 | tf_op jit(solution)/shard_map/ppermute | solution.py:208
  51.5 8.8 %local1.1.a1 = f32[1024,1024]{1,0:T(8,128)} custom-call(s32[8]{0:T(128)} %stack.35.s_ref, bf16[1024,2048]{1,0:T(8,128)(2,1)} %q1.1, bf16[1024,2048]{1,0:T(8,128)(2,1)} %k_ref.5, bf16[1024,2048]{1,0:T(8,128)(2,1)} %v_ref.5, bf16[16,3,128,128]{3,2,1,0:T(8,128)(2,1)} %get-tuple-element.19.prefix_ref, bf16[1024,128]{1,0:T(8,128)(2,1)} %gate_ref.5), custom_call_target="tpu_custom_call" | custom-call | flops 4000000000 | bytes 11534336 | tf_op jit(solution)/shard_map/local1/pallas_call | solution.py:93
  60.2 0.1 fusion.2
  60.3 1.1 collective-permute-start.9
  61.5 5.2 %collective-permute-start.5 = (bf16[8,128,128]{2,1,0:T(8,128)(2,1)S(1)}, bf16[8,128,128]{2,1,0:T(8,128)(2,1)S(1)}, u32[]{:S(2)}, u32[]{:S(2)}) collective-permute-start(bf16[8,128,128]{2,1,0:T(8,128)(2,1)S(1)} %collective-permute-done.1.refs_2_), channel_id=1, source_target_pairs={{0,1},{1,0},{2,3},{3,2},{4,5},{5,4},{6,7},{7,6},{8,9},{9,8},{10,11... | collective-permute-start | bytes 786440 | tf_op jit(solution)/shard_map/ppermute | solution.py:208
  66.7 0.0 collective-permute-done.9.refs_10_
  66.7 0.1 add_convert_fusion
  66.8 2.9 %collective-permute-start.11 = (bf16[8,128,128]{2,1,0:T(8,128)(2,1)S(1)}, bf16[8,128,128]{2,1,0:T(8,128)(2,1)S(1)}, u32[]{:S(2)}, u32[]{:S(2)}) collective-permute-start(bf16[8,128,128]{2,1,0:T(8,128)(2,1)S(1)} %add_convert_fusion), channel_id=1, source_target_pairs={{0,64},{1,65},{2,66},{3,67},{4,68},{5,69},{6,70},{7,71},{8,72},{9,... | collective-permute-start | bytes 786440 | tf_op jit(solution)/shard_map/ppermute | solution.py:208
  69.7 10.6 %collective-permute-start.6 = (bf16[8,128,128]{2,1,0:T(8,128)(2,1)S(1)}, bf16[8,128,128]{2,1,0:T(8,128)(2,1)S(1)}, u32[]{:S(2)}, u32[]{:S(2)}) collective-permute-start(bf16[8,128,128]{2,1,0:T(8,128)(2,1)S(1)} %collective-permute-done.2.refs_4_), channel_id=1, source_target_pairs={{0,1},{1,0},{2,3},{3,2},{4,5},{5,4},{6,7},{7,6},{8,9},{9,8},{10,11... | collective-permute-start | bytes 786440 | tf_op jit(solution)/shard_map/ppermute | solution.py:208
  80.4 0.1 collective-permute-start.7
  80.5 0.4 collective-permute-start.8
  80.9 0.1 collective-permute-start.10
  81.0 9.5 %collective-permute-start.12 = (bf16[8,128,128]{2,1,0:T(8,128)(2,1)S(1)}, bf16[8,128,128]{2,1,0:T(8,128)(2,1)S(1)}, u32[]{:S(2)}, u32[]{:S(2)}) collective-permute-start(bf16[8,128,128]{2,1,0:T(8,128)(2,1)S(1)} %collective-permute-done.11.refs_12_), channel_id=1, source_target_pairs={{0,1},{1,0},{2,3},{3,2},{4,5},{5,4},{6,7},{7,6},{8,9},{9,8},{10,11... | collective-permute-start | bytes 786440 | tf_op jit(solution)/shard_map/ppermute | solution.py:208
  90.5 0.0 collective-permute-done.6.refs_5_
  90.5 1.1 collective-permute-done.12.refs_13_
  91.7 0.6 copy-done.13
  92.3 47.7 %final.1 = bf16[1024,2048]{1,0:T(8,128)(2,1)} custom-call(s32[8]{0:T(128)} %stack.35.s_ref, bf16[1024,2048]{1,0:T(8,128)(2,1)} %q1.1, bf16[1024,2048]{1,0:T(8,128)(2,1)} %q1.1, f32[1024,1024]{1,0:T(8,128)} %local0.1.a0, f32[1024,1024]{1,0:T(8,128)} %local1.1.a1, bf16[1024,128]{1,0:T(8,128)(2,1)} %gate_ref.5, f32[16,128]{1,0:T(8,128)} %bitcast.9, ...), custom_call_target="tpu_custom_call" | custom-call | flops 12999999488 | bytes 31457280 | tf_op jit(solution)/shard_map/final/pallas_call | solution.py:180
  (36 shorter events, 0.1 us)
Async XLA Ops:
  6.5 85.1 %all-gather.2.cloned.1.call-start = ((), (), s32[]{:S(2)}) async-start(), calls=%async_computation | async-start | bytes 8454144 | tf_op jit(solution)/shard_map/all_gather | solution.py:216
  15.5 3.1 %collective-permute-start = (bf16[16,128,128]{2,1,0:T(8,128)(2,1)}, bf16[16,128,128]{2,1,0:T(8,128)(2,1)S(1)}, u32[]{:S(2)}, u32[]{:S(2)}) collective-permute-start(bf16[16,128,128]{2,1,0:T(8,128)(2,1)} %get-tuple-element.16), channel_id=1, source_target_pairs={{0,1},{1,0},{2,3},{3,2},{4,5},{5,4},{6,7},{7,6},{8,9},{9,8},{10,11... | collective-permute-start | bytes 1572872 | tf_op jit(solution)/shard_map/ppermute | solution.py:208
  18.7 22.3 %copy-start.2 = (bf16[16,128,128]{2,1,0:T(8,128)(2,1)}, bf16[16,128,128]{2,1,0:T(8,128)(2,1)S(1)}, u32[]{:S(2)}) copy-start(bf16[16,128,128]{2,1,0:T(8,128)(2,1)S(1)} %collective-permute-done.refs_0_.refs_1_) | copy-start | bytes 1572868
  20.0 7.9 %collective-permute-start.1 = (bf16[8,128,128]{2,1,0:T(8,128)(2,1)S(1)}, bf16[8,128,128]{2,1,0:T(8,128)(2,1)S(1)}, u32[]{:S(2)}, u32[]{:S(2)}) collective-permute-start(bf16[8,128,128]{2,1,0:T(8,128)(2,1)S(1)} %fusion.3), channel_id=1, source_target_pairs={{0,2},{1,3},{2,0},{3,1},{4,6},{5,7},{6,4},{7,5},{8,10},{9,11},{10,... | collective-permute-start | bytes 786440 | tf_op jit(solution)/shard_map/ppermute | solution.py:208
  27.9 33.6 %copy-start.3 = (bf16[8,128,128]{2,1,0:T(8,128)(2,1)}, bf16[8,128,128]{2,1,0:T(8,128)(2,1)S(1)}, u32[]{:S(2)}) copy-start(bf16[8,128,128]{2,1,0:T(8,128)(2,1)S(1)} %collective-permute-done.1.refs_2_) | copy-start | bytes 786436
  29.1 11.8 %collective-permute-start.2 = (bf16[8,128,128]{2,1,0:T(8,128)(2,1)S(1)}, bf16[8,128,128]{2,1,0:T(8,128)(2,1)S(1)}, u32[]{:S(2)}, u32[]{:S(2)}) collective-permute-start(bf16[8,128,128]{2,1,0:T(8,128)(2,1)S(1)} %fusion), channel_id=1, source_target_pairs={{0,4},{1,5},{2,6},{3,7},{4,0},{5,1},{6,2},{7,3},{8,12},{9,13},{10,... | collective-permute-start | bytes 786440 | tf_op jit(solution)/shard_map/ppermute | solution.py:208
  32.1 8.9 %copy-start = (f32[16,128,128]{2,1,0:T(8,128)S(1)}, f32[16,128,128]{2,1,0:T(8,128)}, u32[]{:S(2)}) copy-start(f32[16,128,128]{2,1,0:T(8,128)} %get-tuple-element.15) | copy-start | bytes 3145732
  41.0 28.8 %copy-start.5 = (bf16[8,128,128]{2,1,0:T(8,128)(2,1)}, bf16[8,128,128]{2,1,0:T(8,128)(2,1)S(1)}, u32[]{:S(2)}) copy-start(bf16[8,128,128]{2,1,0:T(8,128)(2,1)S(1)} %collective-permute-done.2.refs_4_) | copy-start | bytes 786436
  41.1 6.9 %collective-permute-start.3 = (bf16[8,128,128]{2,1,0:T(8,128)(2,1)S(1)}, bf16[8,128,128]{2,1,0:T(8,128)(2,1)S(1)}, u32[]{:S(2)}, u32[]{:S(2)}) collective-permute-start(bf16[8,128,128]{2,1,0:T(8,128)(2,1)S(1)} %get-tuple-element.21), channel_id=1, source_target_pairs={{0,8},{1,9},{2,10},{3,11},{4,12},{5,13},{6,14},{7,15},{8,0},{9,1},... | collective-permute-start | bytes 786440 | tf_op jit(solution)/shard_map/ppermute | solution.py:208
  48.0 32.4 %copy-start.1 = (bf16[8,128,128]{2,1,0:T(8,128)(2,1)}, bf16[8,128,128]{2,1,0:T(8,128)(2,1)S(1)}, u32[]{:S(2)}) copy-start(bf16[8,128,128]{2,1,0:T(8,128)(2,1)S(1)} %collective-permute-done.3.refs_6_) | copy-start | bytes 786436
  48.0 12.2 %collective-permute-start.4 = (bf16[8,128,128]{2,1,0:T(8,128)(2,1)S(1)}, bf16[8,128,128]{2,1,0:T(8,128)(2,1)S(1)}, u32[]{:S(2)}, u32[]{:S(2)}) collective-permute-start(bf16[8,128,128]{2,1,0:T(8,128)(2,1)S(1)} %fusion.1), channel_id=1, source_target_pairs={{0,16},{1,17},{2,18},{3,19},{4,20},{5,21},{6,22},{7,23},{8,24},{9,... | collective-permute-start | bytes 786440 | tf_op jit(solution)/shard_map/ppermute | solution.py:208
  60.2 31.4 %copy-start.4 = (bf16[8,128,128]{2,1,0:T(8,128)(2,1)}, bf16[8,128,128]{2,1,0:T(8,128)(2,1)S(1)}, u32[]{:S(2)}) copy-start(bf16[8,128,128]{2,1,0:T(8,128)(2,1)S(1)} %collective-permute-done.4.refs_8_) | copy-start | bytes 786436
  60.3 6.4 %collective-permute-start.9 = (bf16[8,128,128]{2,1,0:T(8,128)(2,1)S(1)}, bf16[8,128,128]{2,1,0:T(8,128)(2,1)S(1)}, u32[]{:S(2)}, u32[]{:S(2)}) collective-permute-start(bf16[8,128,128]{2,1,0:T(8,128)(2,1)S(1)} %fusion.2), channel_id=1, source_target_pairs={{0,32},{1,33},{2,34},{3,35},{4,36},{5,37},{6,38},{7,39},{8,40},{9,... | collective-permute-start | bytes 786440 | tf_op jit(solution)/shard_map/ppermute | solution.py:208
  61.5 19.4 %collective-permute-start.5 = (bf16[8,128,128]{2,1,0:T(8,128)(2,1)S(1)}, bf16[8,128,128]{2,1,0:T(8,128)(2,1)S(1)}, u32[]{:S(2)}, u32[]{:S(2)}) collective-permute-start(bf16[8,128,128]{2,1,0:T(8,128)(2,1)S(1)} %collective-permute-done.1.refs_2_), channel_id=1, source_target_pairs={{0,1},{1,0},{2,3},{3,2},{4,5},{5,4},{6,7},{7,6},{8,9},{9,8},{10,11... | collective-permute-start | bytes 786440 | tf_op jit(solution)/shard_map/ppermute | solution.py:208
  66.7 24.9 %copy-start.6 = (bf16[8,128,128]{2,1,0:T(8,128)(2,1)}, bf16[8,128,128]{2,1,0:T(8,128)(2,1)S(1)}, u32[]{:S(2)}) copy-start(bf16[8,128,128]{2,1,0:T(8,128)(2,1)S(1)} %collective-permute-done.9.refs_10_) | copy-start | bytes 786436
  66.8 14.1 %collective-permute-start.11 = (bf16[8,128,128]{2,1,0:T(8,128)(2,1)S(1)}, bf16[8,128,128]{2,1,0:T(8,128)(2,1)S(1)}, u32[]{:S(2)}, u32[]{:S(2)}) collective-permute-start(bf16[8,128,128]{2,1,0:T(8,128)(2,1)S(1)} %add_convert_fusion), channel_id=1, source_target_pairs={{0,64},{1,65},{2,66},{3,67},{4,68},{5,69},{6,70},{7,71},{8,72},{9,... | collective-permute-start | bytes 786440 | tf_op jit(solution)/shard_map/ppermute | solution.py:208
  69.7 20.7 %collective-permute-start.6 = (bf16[8,128,128]{2,1,0:T(8,128)(2,1)S(1)}, bf16[8,128,128]{2,1,0:T(8,128)(2,1)S(1)}, u32[]{:S(2)}, u32[]{:S(2)}) collective-permute-start(bf16[8,128,128]{2,1,0:T(8,128)(2,1)S(1)} %collective-permute-done.2.refs_4_), channel_id=1, source_target_pairs={{0,1},{1,0},{2,3},{3,2},{4,5},{5,4},{6,7},{7,6},{8,9},{9,8},{10,11... | collective-permute-start | bytes 786440 | tf_op jit(solution)/shard_map/ppermute | solution.py:208
  80.4 10.1 %collective-permute-start.7 = (bf16[8,128,128]{2,1,0:T(8,128)(2,1)S(1)}, bf16[8,128,128]{2,1,0:T(8,128)(2,1)S(1)}, u32[]{:S(2)}, u32[]{:S(2)}) collective-permute-start(bf16[8,128,128]{2,1,0:T(8,128)(2,1)S(1)} %collective-permute-done.3.refs_6_), channel_id=1, source_target_pairs={{0,1},{1,0},{2,3},{3,2},{4,5},{5,4},{6,7},{7,6},{8,9},{9,8},{10,11... | collective-permute-start | bytes 786440 | tf_op jit(solution)/shard_map/ppermute | solution.py:208
  80.5 10.0 %collective-permute-start.8 = (bf16[8,128,128]{2,1,0:T(8,128)(2,1)S(1)}, bf16[8,128,128]{2,1,0:T(8,128)(2,1)S(1)}, u32[]{:S(2)}, u32[]{:S(2)}) collective-permute-start(bf16[8,128,128]{2,1,0:T(8,128)(2,1)S(1)} %collective-permute-done.4.refs_8_), channel_id=1, source_target_pairs={{0,1},{1,0},{2,3},{3,2},{4,5},{5,4},{6,7},{7,6},{8,9},{9,8},{10,11... | collective-permute-start | bytes 786440 | tf_op jit(solution)/shard_map/ppermute | solution.py:208
  80.9 10.8 %copy-start.7 = (bf16[8,128,128]{2,1,0:T(8,128)(2,1)}, bf16[8,128,128]{2,1,0:T(8,128)(2,1)S(1)}, u32[]{:S(2)}) copy-start(bf16[8,128,128]{2,1,0:T(8,128)(2,1)S(1)} %collective-permute-done.5.refs_3_) | copy-start | bytes 786436
  80.9 9.6 %collective-permute-start.10 = (bf16[8,128,128]{2,1,0:T(8,128)(2,1)S(1)}, bf16[8,128,128]{2,1,0:T(8,128)(2,1)S(1)}, u32[]{:S(2)}, u32[]{:S(2)}) collective-permute-start(bf16[8,128,128]{2,1,0:T(8,128)(2,1)S(1)} %collective-permute-done.9.refs_10_), channel_id=1, source_target_pairs={{0,1},{1,0},{2,3},{3,2},{4,5},{5,4},{6,7},{7,6},{8,9},{9,8},{10,11... | collective-permute-start | bytes 786440 | tf_op jit(solution)/shard_map/ppermute | solution.py:208
  81.0 10.7 %copy-start.8 = (bf16[8,128,128]{2,1,0:T(8,128)(2,1)}, bf16[8,128,128]{2,1,0:T(8,128)(2,1)S(1)}, u32[]{:S(2)}) copy-start(bf16[8,128,128]{2,1,0:T(8,128)(2,1)S(1)} %collective-permute-done.11.refs_12_) | copy-start | bytes 786436
  81.0 10.6 %collective-permute-start.12 = (bf16[8,128,128]{2,1,0:T(8,128)(2,1)S(1)}, bf16[8,128,128]{2,1,0:T(8,128)(2,1)S(1)}, u32[]{:S(2)}, u32[]{:S(2)}) collective-permute-start(bf16[8,128,128]{2,1,0:T(8,128)(2,1)S(1)} %collective-permute-done.11.refs_12_), channel_id=1, source_target_pairs={{0,1},{1,0},{2,3},{3,2},{4,5},{5,4},{6,7},{7,6},{8,9},{9,8},{10,11... | collective-permute-start | bytes 786440 | tf_op jit(solution)/shard_map/ppermute | solution.py:208
  90.5 1.2 copy-start.9
  90.5 1.2 copy-start.10
  90.5 1.2 copy-start.11
  90.5 1.2 copy-start.12
  91.6 0.7 copy-start.13
Sparse Core Ops, SparseCore 0:
  10.3 79.9 all-gather.1

commit v2 on v1

v2 whole, which is shorter than its diff:
```python
import functools

import jax
import jax.numpy as jnp
from jax import lax
from jax.experimental import pallas as pl
from jax.experimental.pallas import tpu as pltpu
from jax.sharding import PartitionSpec as P

HEADS = 16
HEAD = 128
GATES = 8
HALF = HEADS // 2
QUARTER = HEADS // 4
ROWS = 1024
CHUNK = 256
CHUNKS = ROWS // CHUNK
EPSILON = 1e-06
VMEM_MIB = 60
F32 = jnp.float32
BF16 = jnp.bfloat16
NN = ((1,), (0,))
NT = ((1,), (1,))


def params():
    return pltpu.CompilerParams(vmem_limit_bytes=VMEM_MIB << 20)


def cost(flops, moved):
    return pl.CostEstimate(flops=int(flops), bytes_accessed=int(moved), transcendentals=0)


def dot(a, b, contract=NN):
    return lax.dot_general(a, b, (contract, ((), ())), preferred_element_type=F32)


def state_body(k_ref, v_ref, total_ref, sent_ref, prefix_ref, vt_ref):
    for pair in range(2):
        cols = slice(pair * HEAD, (pair + 1) * HEAD)
        vt = jnp.transpose(v_ref[:, cols])
        vt_ref[cols, :] = vt
        total = None
        for c in range(CHUNKS):
            rows = slice(c * CHUNK, (c + 1) * CHUNK)
            part = dot(vt[:, rows], k_ref[rows, cols])
            total = part if total is None else total + part
            if c + 1 < CHUNKS:
                prefix_ref[pair, c] = total.astype(BF16)
        total_ref[pair] = total
        sent_ref[pair] = total.astype(BF16)


def states(keys, values):
    block = pl.BlockSpec((ROWS, 2 * HEAD), lambda i: (0, i))
    square = pl.BlockSpec((2, HEAD, HEAD), lambda i: (i, 0, 0))
    return pl.pallas_call(
        state_body,
        grid=(HEADS // 2,),
        in_specs=[block, block],
        out_specs=[
            square,
            square,
            pl.BlockSpec((2, CHUNKS - 1, HEAD, HEAD), lambda i: (i, 0, 0, 0)),
            pl.BlockSpec((2 * HEAD, ROWS), lambda i: (i, 0)),
        ],
        out_shape=[
            jax.ShapeDtypeStruct((HEADS, HEAD, HEAD), F32),
            jax.ShapeDtypeStruct((HEADS, HEAD, HEAD), BF16),
            jax.ShapeDtypeStruct((HEADS, CHUNKS - 1, HEAD, HEAD), BF16),
            jax.ShapeDtypeStruct((HEADS * HEAD, ROWS), BF16),
        ],
        compiler_params=params(),
        cost_estimate=cost(1e9, 14 << 20),
        name="states",
    )(keys, values)


def side_of(side, core):
    return core if side == 0 else 1 - core


def local_body(side, s_ref, q_ref, k_ref, vt_ref, prefix_ref, first_ref, gate_ref, out_ref):
    head0 = side_of(side, s_ref[0]) * HALF + 2 * pl.program_id(0)
    causal = lax.broadcasted_iota(jnp.int32, (CHUNK, CHUNK), 0) <= lax.broadcasted_iota(
        jnp.int32, (CHUNK, CHUNK), 1
    )
    for pair in range(2):
        cols = slice(pair * HEAD, (pair + 1) * HEAD)
        w0 = gate_ref[pl.ds(head0 + pair, 1), :]
        w1 = gate_ref[pl.ds(HEADS + head0 + pair, 1), :]
        for c in range(CHUNKS):
            rows = slice(c * CHUNK, (c + 1) * CHUNK)
            q = q_ref[rows, cols]
            scores = dot(k_ref[rows, cols], q, NT)
            scores = jnp.where(causal, scores, 0.0).astype(BF16)
            mixed = dot(vt_ref[cols, rows], scores)
            if c:
                both = jnp.concatenate([prefix_ref[pair, c - 1], first_ref[pair]], axis=0)
                both = dot(both, q, NT)
                mixed = mixed + both[:HEAD]
                level = both[HEAD:]
            else:
                level = dot(first_ref[pair], q, NT)
            out_ref[cols, rows] = mixed * w0[:, rows] + level * w1[:, rows]


def local(side, scalars, queries, keys, vt, prefix, first, gate):
    where = lambda i, s: side_of(side, s[0]) * QUARTER + i
    block = pl.BlockSpec((ROWS, 2 * HEAD), lambda i, s: (0, where(i, s)))
    return pl.pallas_call(
        functools.partial(local_body, side),
        grid_spec=pltpu.PrefetchScalarGridSpec(
            num_scalar_prefetch=1,
            grid=(QUARTER,),
            in_specs=[
                block,
                block,
                pl.BlockSpec((2 * HEAD, ROWS), lambda i, s: (where(i, s), 0)),
                pl.BlockSpec((2, CHUNKS - 1, HEAD, HEAD), lambda i, s: (where(i, s), 0, 0, 0)),
                pl.BlockSpec((2, HEAD, HEAD), lambda i, s: (where(i, s), 0, 0)),
                pl.BlockSpec((GATES * HEADS, ROWS), lambda i, s: (0, 0)),
            ],
            out_specs=pl.BlockSpec((2 * HEAD, ROWS), lambda i, s: (i, 0)),
        ),
        out_shape=jax.ShapeDtypeStruct((HALF * HEAD, ROWS), F32),
        compiler_params=params(),
        cost_estimate=cost(4e9, 11 << 20),
        name=f"local{side}",
    )(scalars, queries, keys, vt, prefix, first, gate)


def with_levels(head, levels, squares, q, gate_ref, rows, attended):
    products = dot(squares, q, NT)
    for n, level in enumerate(levels):
        weight = gate_ref[pl.ds((level + 1) * HEADS + head, 1), rows]
        attended = attended + products[n * HEAD : (n + 1) * HEAD] * weight
    return attended


def partial_body(side, levels, s_ref, q_ref, a_ref, gate_ref, *refs):
    *buckets, out_ref = refs
    head0 = side_of(side, s_ref[0]) * HALF + 2 * pl.program_id(0)
    for pair in range(2):
        cols = slice(pair * HEAD, (pair + 1) * HEAD)
        squares = jnp.concatenate([b[pair] for b in buckets], axis=0)
        for c in range(CHUNKS):
            rows = slice(c * CHUNK, (c + 1) * CHUNK)
            out_ref[cols, rows] = with_levels(
                head0 + pair, levels, squares, q_ref[rows, cols], gate_ref, rows, a_ref[cols, rows]
            )


def side_specs(side, levels):
    where = lambda i, s: side_of(side, s[0]) * QUARTER + i
    return [
        pl.BlockSpec((ROWS, 2 * HEAD), lambda i, s: (0, where(i, s))),
        pl.BlockSpec((2 * HEAD, ROWS), lambda i, s: (i, 0)),
        pl.BlockSpec((GATES * HEADS, ROWS), lambda i, s: (0, 0)),
        *[pl.BlockSpec((2, HEAD, HEAD), lambda i, s: (i, 0, 0)) for _ in levels],
    ]


def partial_levels(side, levels, scalars, queries, attended, gate, buckets):
    return pl.pallas_call(
        functools.partial(partial_body, side, levels),
        grid_spec=pltpu.PrefetchScalarGridSpec(
            num_scalar_prefetch=1,
            grid=(QUARTER,),
            in_specs=side_specs(side, levels),
            out_specs=pl.BlockSpec((2 * HEAD, ROWS), lambda i, s: (i, 0)),
        ),
        out_shape=jax.ShapeDtypeStruct((HALF * HEAD, ROWS), F32),
        compiler_params=params(),
        cost_estimate=cost(2e9, 10 << 20),
        name=f"levels{side}",
    )(scalars, queries, attended, gate, *buckets)


def norm_body(levels, s_ref, *refs):
    count = len(levels)
    gain_ref, out0_ref, out1_ref = refs[-3:]
    step = pl.program_id(0)
    core = s_ref[0]
    for side, out_ref in ((0, out0_ref), (1, out1_ref)):
        q_ref, a_ref, gate_ref, *buckets = refs[side * (3 + count) : (side + 1) * (3 + count)]
        for pair in range(2):
            head = side_of(side, core) * HALF + 2 * step + pair
            cols = slice(pair * HEAD, (pair + 1) * HEAD)
            squares = jnp.concatenate([b[pair] for b in buckets], axis=0)
            gain = gain_ref[pl.ds(head, 1), :]
            for c in range(CHUNKS):
                rows = slice(c * CHUNK, (c + 1) * CHUNK)
                x = with_levels(head, levels, squares, q_ref[rows, cols], gate_ref, rows, a_ref[cols, rows])
                mean = jnp.mean(x * x, axis=0, keepdims=True)
                x = jnp.transpose(x * lax.rsqrt(mean + EPSILON))
                out_ref[rows, cols] = (x * gain).astype(BF16)


def normed(levels, scalars, queries, attended, gate, buckets, gain):
    half = jax.ShapeDtypeStruct((ROWS, HALF * HEAD), BF16)
    out = pl.BlockSpec((ROWS, 2 * HEAD), lambda i, s: (0, i))
    operands = []
    for side in range(2):
        operands += [queries, attended[side], gate, *buckets[side]]
    return pl.pallas_call(
        functools.partial(norm_body, levels),
        grid_spec=pltpu.PrefetchScalarGridSpec(
            num_scalar_prefetch=1,
            grid=(QUARTER,),
            in_specs=[
                *side_specs(0, levels),
                *side_specs(1, levels),
                pl.BlockSpec((HEADS, HEAD), lambda i, s: (0, 0)),
            ],
            out_specs=[out, out],
        ),
        out_shape=[half, half],
        compiler_params=params(),
        cost_estimate=cost(4e9, 18 << 20),
        name="normed",
    )(scalars, *operands, gain)


def project_body(s_ref, n0_ref, n1_ref, w0_ref, w1_ref, out_ref):
    out_ref[...] = (dot(n0_ref[...], w0_ref[...]) + dot(n1_ref[...], w1_ref[...])).astype(BF16)


def project(scalars, halves, weight):
    tile = 256
    depth = HALF * HEAD
    whole = pl.BlockSpec((ROWS, depth), lambda i, s: (0, 0))
    return pl.pallas_call(
        project_body,
        grid_spec=pltpu.PrefetchScalarGridSpec(
            num_scalar_prefetch=1,
            grid=(HEADS * HEAD // tile,),
            in_specs=[
                whole,
                whole,
                pl.BlockSpec((depth, tile), lambda i, s: (s[0], i)),
                pl.BlockSpec((depth, tile), lambda i, s: (1 - s[0], i)),
            ],
            out_specs=pl.BlockSpec((ROWS, tile), lambda i, s: (0, i)),
        ),
        out_shape=jax.ShapeDtypeStruct((ROWS, HEADS * HEAD), BF16),
        compiler_params=params(),
        cost_estimate=cost(8e9, 16 << 20),
        name="project",
    )(scalars, *halves, weight, weight)


def from_partner(value, axis, bit):
    mask = 2**bit
    pairs = [(source, source ^ mask) for source in range(lax.axis_size(axis))]
    return lax.ppermute(value, axis, pairs)


def shards(queries, keys, values, level_gate, norm_gain, out_weight):
    position = lax.axis_index("ctx")
    levels = lax.axis_size("ctx").bit_length() - 1
    core = position & 1
    scalars = core.astype(jnp.int32).reshape(1)
    whole_weight = lax.all_gather(out_weight, "ctx", axis=0, tiled=True)
    bits = position >> jnp.arange(levels, dtype=jnp.int32) & 1
    present = jnp.concatenate([jnp.ones((1,), F32), bits.astype(F32)])
    gate = level_gate.T.astype(F32) * jnp.repeat(present, HEADS)[:, None]
    total, sent, prefix, vt = states(keys, values)
    first = from_partner(sent, "ctx", 0)
    attended = [None, None]
    mine, yours = {}, {}
    running = lax.dynamic_slice_in_dim(total, core * HALF, HALF) + lax.dynamic_slice_in_dim(
        first, core * HALF, HALF
    ).astype(F32)
    early = [1, 2, 3]
    late = [4, 5, 6]
    for level in range(1, levels):
        outgoing = running.astype(BF16)
        if level == 1:
            outgoing, q = lax.optimization_barrier((outgoing, queries))
            attended[0] = local(0, scalars, q, keys, vt, prefix, first, gate)
        if level == 2:
            outgoing, q = lax.optimization_barrier((outgoing, queries))
            attended[1] = local(1, scalars, q, keys, vt, prefix, first, gate)
        if level == 3:
            outgoing, attended[0] = lax.optimization_barrier((outgoing, attended[0]))
        if level == 4:
            outgoing, attended[1] = lax.optimization_barrier((outgoing, attended[1]))
        if level == 5:
            outgoing, q = lax.optimization_barrier((outgoing, queries))
            attended[0] = partial_levels(0, early, scalars, q, attended[0], gate, [mine[l] for l in early])
        if level == 6:
            outgoing, q, attended[0] = lax.optimization_barrier((outgoing, queries, attended[0]))
            attended[1] = partial_levels(1, early, scalars, q, attended[1], gate, [yours[l] for l in early])
        received = from_partner(outgoing, "ctx", level)
        mine[level] = received
        yours[level] = from_partner(received, "ctx", 0)
        if level + 1 < levels:
            running = running + received.astype(F32)
    gain = norm_gain.reshape(HEADS, HEAD)
    buckets = [[mine[l] for l in late], [yours[l] for l in late]]
    halves = normed(late, scalars, queries, attended, gate, buckets, gain)
    return project(scalars, halves, whole_weight)


def solution(mesh):
    placed = (P("ctx", None), P("ctx", None), P("ctx", None), P("ctx", None), P(), P("ctx", None))
    return jax.shard_map(
        shards, mesh=mesh, in_specs=placed, out_specs=P("ctx", None), check_vma=False
    )
```

time: 147 us -> 131 us (0.89)
  starting transfers between devices: 40.9 us -> 19.2 us
  waiting for transfers between devices: 14.6 us -> 24.4 us
  Pallas kernels: 73.7 us -> 64.6 us
  other arithmetic: 2.92 us -> 6 us
    ppermute x13, starting transfers between devices: 40.9 us -> 19.2 us  [from_partner(): return lax.ppermute(value, axis, pairs)]
    ppermute x13, waiting for transfers between devices: 13.9 us -> 23.7 us  [from_partner(): return lax.ppermute(value, axis, pairs)]
    pallas_call x1 -> x4, Pallas kernels: 47.7 us -> 38 us  [the longest x1 14 us: project(): pl.pallas_call(project_body, grid_spec=pltpu.PrefetchScalarGridSpec(num_s...]
    convert_element_type x6, other arithmetic: 2.92 us -> 5.03 us  [shards(): outgoing = running.astype(BF16)]
    unnamed x28 -> x33, local copies, waits for them, and re-layouts: 0.69 us -> 2.44 us
  transfers between devices with their start and end apart: 14 -> 14, of which waited for: 4 -> 4; matrix products, arithmetic and copies ran while one was open for 2% -> 5% of each run, Pallas kernels for 18% -> 39%
where the time goes in v2:
time: 131 us; the launch traced here: 130 us
  Pallas kernels  64.6 us (49%)
  waiting for transfers between devices  24.4 us (19%)
  starting transfers between devices  19.2 us (15%)
  between operations  13.6 us (10%)
  other arithmetic  6 us (5%)
  local copies, waits for them, and re-layouts  2.6 us (2%)
    ppermute x13, waiting for transfers between devices, from_partner(): return lax.ppermute(value, axis, pairs)  23.7 us
    ppermute x13, starting transfers between devices, from_partner(): return lax.ppermute(value, axis, pairs)  19.2 us
    pallas_call x2, Pallas kernels, local(): pl.pallas_call(functools.partial(local_body, side), grid_spec=pltpu.Prefe...  17.6 us
    pallas_call x1, Pallas kernels, project(): pl.pallas_call(project_body, grid_spec=pltpu.PrefetchScalarGridSpec(num_s...  14 us
    pallas_call x2, Pallas kernels, partial_levels(): pl.pallas_call(functools.partial(partial_body, side, levels), grid_spec=p...  13.7 us
    pallas_call x1, Pallas kernels, normed(): pl.pallas_call(functools.partial(norm_body, levels), grid_spec=pltpu.Pref...  10.3 us
    pallas_call x1, Pallas kernels, states(): pl.pallas_call(state_body, grid=(HEADS // 2,), in_specs=[block, block], o...  9.05 us
    convert_element_type x6, other arithmetic, shards(): outgoing = running.astype(BF16)  5.03 us
  transfers between devices with their start and end apart: 14, of which 4 were waited for; matrix products, arithmetic and copies ran while one was open for 5% of the time, Pallas kernels for 39%

profile of v2, /device:TPU:1, one launch (start us, length us, event | category | flops | bytes accessed | tf_op | source)
XLA Modules:
  0.0 130.4 jit_solution(9639361188081366335)
XLA Ops:
  6.5 0.7 all-gather.2.cloned.1.call-update
  7.3 9.1 %states.1 = (f32[16,128,128]{2,1,0:T(8,128)}, bf16[16,128,128]{2,1,0:T(8,128)(2,1)}, bf16[16,3,128,128]{3,2,1,0:T(8,128)(2,1)}, bf16[2048,1024]{1,0:T(8,128)(2,1)}) custom-call(bf16[1024,2048]{1,0:T(8,128)(2,1)} %k_ref.5, bf16[1024,2048]{1,0:T(8,128)(2,1)} %v_ref.1), custom_call_target="tpu_custom_call" | custom-call | flops 1000000000 | bytes 14680064 | tf_op jit(solution)/shard_map/states/pallas_call | solution.py:57
  16.3 1.4 %collective-permute-start = (bf16[16,128,128]{2,1,0:T(8,128)(2,1)}, bf16[16,128,128]{2,1,0:T(8,128)(2,1)S(1)}, u32[]{:S(2)}, u32[]{:S(2)}) collective-permute-start(bf16[16,128,128]{2,1,0:T(8,128)(2,1)} %get-tuple-element.25), channel_id=1, source_target_pairs={{0,1},{1,0},{2,3},{3,2},{4,5},{5,4},{6,7},{7,6},{8,9},{9,8},{10,11... | collective-permute-start | bytes 1572872 | tf_op jit(solution)/shard_map/ppermute | solution.py:256
  17.7 1.7 %collective-permute-done.first_ref = bf16[16,128,128]{2,1,0:T(8,128)(2,1)S(1)} collective-permute-done((bf16[16,128,128]{2,1,0:T(8,128)(2,1)}, bf16[16,128,128]{2,1,0:T(8,128)(2,1)S(1)}, u32[]{:S(2)}, u32[]{:S(2)}) %collective-permute-start) | collective-permute-done | bytes 524320 | tf_op jit(solution)/shard_map/ppermute | solution.py:256
  19.4 1.3 fusion.3
  20.7 1.4 %collective-permute-start.1 = (bf16[8,128,128]{2,1,0:T(8,128)(2,1)S(1)}, bf16[8,128,128]{2,1,0:T(8,128)(2,1)S(1)}, u32[]{:S(2)}, u32[]{:S(2)}) collective-permute-start(bf16[8,128,128]{2,1,0:T(8,128)(2,1)S(1)} %fusion.3), channel_id=1, source_target_pairs={{0,2},{1,3},{2,0},{3,1},{4,6},{5,7},{6,4},{7,5},{8,10},{9,11},{10,... | collective-permute-start | bytes 786440 | tf_op jit(solution)/shard_map/ppermute | solution.py:256
  22.5 0.9 multiply_bitcast_fusion.gate_ref.refs_2_.refs_8_
  23.4 5.2 %collective-permute-done.1.refs_0_ = bf16[8,128,128]{2,1,0:T(8,128)(2,1)S(1)} collective-permute-done((bf16[8,128,128]{2,1,0:T(8,128)(2,1)S(1)}, bf16[8,128,128]{2,1,0:T(8,128)(2,1)S(1)}, u32[]{:S(2)}, u32[]{:S(2)}) %collective-permute-start.1) | collective-permute-done | bytes 262176 | tf_op jit(solution)/shard_map/ppermute | solution.py:256
  28.7 1.2 fusion
  29.9 2.9 %collective-permute-start.2 = (bf16[8,128,128]{2,1,0:T(8,128)(2,1)S(1)}, bf16[8,128,128]{2,1,0:T(8,128)(2,1)S(1)}, u32[]{:S(2)}, u32[]{:S(2)}) collective-permute-start(bf16[8,128,128]{2,1,0:T(8,128)(2,1)S(1)} %fusion), channel_id=1, source_target_pairs={{0,4},{1,5},{2,6},{3,7},{4,0},{5,1},{6,2},{7,3},{8,12},{9,13},{10,... | collective-permute-start | bytes 786440 | tf_op jit(solution)/shard_map/ppermute | solution.py:256
  32.8 8.8 %local0.1.a_ref = f32[1024,1024]{1,0:T(8,128)} custom-call(s32[1]{0:T(128)} %bitcast.s_ref, bf16[1024,2048]{1,0:T(8,128)(2,1)} %refs_6_.1, bf16[1024,2048]{1,0:T(8,128)(2,1)} %k_ref.5, bf16[2048,1024]{1,0:T(8,128)(2,1)} %get-tuple-element.29.vt_ref, bf16[16,3,128,128]{3,2,1,0:T(8,128)(2,1)} %get-tuple-element.30.prefix_ref, bf16[16,128,128]{2,1,0:T(8,128)(2,1)} %copy-done, ...), custom_call_target="tpu_custom_call" | custom-call | flops 4000000000 | bytes 11534336 | tf_op jit(solution)/shard_map/local0/pallas_call | solution.py:111
  41.7 1.2 fusion.4
  42.9 1.7 %collective-permute-start.3 = (bf16[8,128,128]{2,1,0:T(8,128)(2,1)S(1)}, bf16[8,128,128]{2,1,0:T(8,128)(2,1)S(1)}, u32[]{:S(2)}, u32[]{:S(2)}) collective-permute-start(bf16[8,128,128]{2,1,0:T(8,128)(2,1)S(1)} %get-tuple-element.31), channel_id=1, source_target_pairs={{0,8},{1,9},{2,10},{3,11},{4,12},{5,13},{6,14},{7,15},{8,0},{9,1},... | collective-permute-start | bytes 786440 | tf_op jit(solution)/shard_map/ppermute | solution.py:256
  44.6 8.8 %local1.1.a_ref = f32[1024,1024]{1,0:T(8,128)} custom-call(s32[1]{0:T(128)} %bitcast.s_ref, bf16[1024,2048]{1,0:T(8,128)(2,1)} %refs_6_.1, bf16[1024,2048]{1,0:T(8,128)(2,1)} %k_ref.5, bf16[2048,1024]{1,0:T(8,128)(2,1)} %get-tuple-element.29.vt_ref, bf16[16,3,128,128]{3,2,1,0:T(8,128)(2,1)} %get-tuple-element.30.prefix_ref, bf16[16,128,128]{2,1,0:T(8,128)(2,1)} %copy-done, ...), custom_call_target="tpu_custom_call" | custom-call | flops 4000000000 | bytes 11534336 | tf_op jit(solution)/shard_map/local1/pallas_call | solution.py:111
  53.4 3.3 %collective-permute-start.4 = (bf16[8,128,128]{2,1,0:T(8,128)(2,1)S(1)}, bf16[8,128,128]{2,1,0:T(8,128)(2,1)S(1)}, u32[]{:S(2)}, u32[]{:S(2)}) collective-permute-start(bf16[8,128,128]{2,1,0:T(8,128)(2,1)S(1)} %fusion.1), channel_id=1, source_target_pairs={{0,16},{1,17},{2,18},{3,19},{4,20},{5,21},{6,22},{7,23},{8,24},{9,... | collective-permute-start | bytes 786440 | tf_op jit(solution)/shard_map/ppermute | solution.py:256
  56.7 5.3 %collective-permute-done.4.refs_3_ = bf16[8,128,128]{2,1,0:T(8,128)(2,1)S(1)} collective-permute-done((bf16[8,128,128]{2,1,0:T(8,128)(2,1)S(1)}, bf16[8,128,128]{2,1,0:T(8,128)(2,1)S(1)}, u32[]{:S(2)}, u32[]{:S(2)}) %collective-permute-start.4) | collective-permute-done | bytes 262176 | tf_op jit(solution)/shard_map/ppermute | solution.py:256
  62.2 1.1 collective-permute-start.5
  63.3 2.6 %collective-permute-start.7 = (bf16[8,128,128]{2,1,0:T(8,128)(2,1)S(1)}, bf16[8,128,128]{2,1,0:T(8,128)(2,1)S(1)}, u32[]{:S(2)}, u32[]{:S(2)}) collective-permute-start(bf16[8,128,128]{2,1,0:T(8,128)(2,1)S(1)} %collective-permute-done.1.refs_0_), channel_id=1, source_target_pairs={{0,1},{1,0},{2,3},{3,2},{4,5},{5,4},{6,7},{7,6},{8,9},{9,8},{10,11... | collective-permute-start | bytes 786440 | tf_op jit(solution)/shard_map/ppermute | solution.py:256
  66.0 6.8 %levels0.1.refs_1_ = f32[1024,1024]{1,0:T(8,128)} custom-call(s32[1]{0:T(128)} %bitcast.s_ref, bf16[1024,2048]{1,0:T(8,128)(2,1)} %refs_6_.1, f32[1024,1024]{1,0:T(8,128)} %local0.1.a_ref, f32[128,1024]{1,0:T(8,128)} %multiply_bitcast_fusion.gate_ref.refs_2_.refs_8_, bf16[8,128,128]{2,1,0:T(8,128)(2,1)} %copy-done.2, bf16[8,128,128]{2,1,0:T(8,128)(2,1)} %copy-done.5, ...), custom_call_target="tpu_custom_call" | custom-call | flops 2000000000 | bytes 10485760 | tf_op jit(solution)/shard_map/levels0/pallas_call | solution.py:165
  72.8 1.2 add_convert_fusion
  74.0 2.8 %collective-permute-start.6 = (bf16[8,128,128]{2,1,0:T(8,128)(2,1)S(1)}, bf16[8,128,128]{2,1,0:T(8,128)(2,1)S(1)}, u32[]{:S(2)}, u32[]{:S(2)}) collective-permute-start(bf16[8,128,128]{2,1,0:T(8,128)(2,1)S(1)} %add_convert_fusion), channel_id=1, source_target_pairs={{0,64},{1,65},{2,66},{3,67},{4,68},{5,69},{6,70},{7,71},{8,72},{9,... | collective-permute-start | bytes 786440 | tf_op jit(solution)/shard_map/ppermute | solution.py:256
  76.8 0.3 collective-permute-start.8
  77.1 0.2 collective-permute-start.9
  77.3 0.3 collective-permute-start.10
  77.8 11.3 %collective-permute-done.6.refs_5_ = bf16[8,128,128]{2,1,0:T(8,128)(2,1)S(1)} collective-permute-done((bf16[8,128,128]{2,1,0:T(8,128)(2,1)S(1)}, bf16[8,128,128]{2,1,0:T(8,128)(2,1)S(1)}, u32[]{:S(2)}, u32[]{:S(2)}) %collective-permute-start.6) | collective-permute-done | bytes 262176 | tf_op jit(solution)/shard_map/ppermute | solution.py:256
  89.1 0.9 collective-permute-start.12
  90.0 0.7 copy-done.9
  90.7 0.7 copy-done.10
  91.4 6.8 %levels1.1.refs_7_ = f32[1024,1024]{1,0:T(8,128)} custom-call(s32[1]{0:T(128)} %bitcast.s_ref, bf16[1024,2048]{1,0:T(8,128)(2,1)} %refs_6_.1, f32[1024,1024]{1,0:T(8,128)} %local1.1.a_ref, f32[128,1024]{1,0:T(8,128)} %multiply_bitcast_fusion.gate_ref.refs_2_.refs_8_, bf16[8,128,128]{2,1,0:T(8,128)(2,1)} %copy-done.8, bf16[8,128,128]{2,1,0:T(8,128)(2,1)} %copy-done.9, ...), custom_call_target="tpu_custom_call" | custom-call | flops 2000000000 | bytes 10485760 | tf_op jit(solution)/shard_map/levels1/pallas_call | solution.py:165
  98.3 0.6 copy-done.13
  99.2 10.3 %normed.1 = (bf16[1024,1024]{1,0:T(8,128)(2,1)}, bf16[1024,1024]{1,0:T(8,128)(2,1)}) custom-call(s32[1]{0:T(128)} %bitcast.s_ref, bf16[1024,2048]{1,0:T(8,128)(2,1)} %refs_6_.1, f32[1024,1024]{1,0:T(8,128)} %levels0.1.refs_1_, f32[128,1024]{1,0:T(8,128)} %multiply_bitcast_fusion.gate_ref.refs_2_.refs_8_, bf16[8,128,128]{2,1,0:T(8,128)(2,1)} %copy-done.4, ...), custom_call_target="tpu_custom_call" | custom-call | flops 4000000000 | bytes 18874368 | tf_op jit(solution)/shard_map/normed/pallas_call | solution.py:206
  109.5 14.0 %project.1 = bf16[1024,2048]{1,0:T(8,128)(2,1)} custom-call(s32[1]{0:T(128)} %bitcast.s_ref, bf16[1024,1024]{1,0:T(8,128)(2,1)} %get-tuple-element.41.n0_ref, bf16[1024,1024]{1,0:T(8,128)(2,1)} %get-tuple-element.42.n1_ref, bf16[2048,2048]{1,0:T(8,128)(2,1)} %all-gather.2.cloned.1.call-done.w0_ref.w1_ref, ...), custom_call_target="tpu_custom_call" | custom-call | flops 8000000000 | bytes 16777216 | tf_op jit(solution)/shard_map/project/pallas_call | solution.py:233
  (48 shorter events, 1.1 us)
Async XLA Ops:
  6.5 103.0 %all-gather.2.cloned.1.call-start = ((), (), s32[]{:S(2)}) async-start(), calls=%async_computation | async-start | bytes 8454144 | tf_op jit(solution)/shard_map/all_gather | solution.py:264
  7.3 15.1 %copy-start.11 = (bf16[1024,128]{1,0:T(8,128)(2,1)S(1)}, bf16[1024,128]{1,0:T(8,128)(2,1)}, u32[]{:S(2)}) copy-start(bf16[1024,128]{1,0:T(8,128)(2,1)} %param.9) | copy-start | bytes 786436
  16.3 3.1 %collective-permute-start = (bf16[16,128,128]{2,1,0:T(8,128)(2,1)}, bf16[16,128,128]{2,1,0:T(8,128)(2,1)S(1)}, u32[]{:S(2)}, u32[]{:S(2)}) collective-permute-start(bf16[16,128,128]{2,1,0:T(8,128)(2,1)} %get-tuple-element.25), channel_id=1, source_target_pairs={{0,1},{1,0},{2,3},{3,2},{4,5},{5,4},{6,7},{7,6},{8,9},{9,8},{10,11... | collective-permute-start | bytes 1572872 | tf_op jit(solution)/shard_map/ppermute | solution.py:256
  19.4 13.4 %copy-start = (bf16[16,128,128]{2,1,0:T(8,128)(2,1)}, bf16[16,128,128]{2,1,0:T(8,128)(2,1)S(1)}, u32[]{:S(2)}) copy-start(bf16[16,128,128]{2,1,0:T(8,128)(2,1)S(1)} %collective-permute-done.first_ref) | copy-start | bytes 1572868
  20.7 7.9 %collective-permute-start.1 = (bf16[8,128,128]{2,1,0:T(8,128)(2,1)S(1)}, bf16[8,128,128]{2,1,0:T(8,128)(2,1)S(1)}, u32[]{:S(2)}, u32[]{:S(2)}) collective-permute-start(bf16[8,128,128]{2,1,0:T(8,128)(2,1)S(1)} %fusion.3), channel_id=1, source_target_pairs={{0,2},{1,3},{2,0},{3,1},{4,6},{5,7},{6,4},{7,5},{8,10},{9,11},{10,... | collective-permute-start | bytes 786440 | tf_op jit(solution)/shard_map/ppermute | solution.py:256
  28.7 34.7 %copy-start.2 = (bf16[8,128,128]{2,1,0:T(8,128)(2,1)}, bf16[8,128,128]{2,1,0:T(8,128)(2,1)S(1)}, u32[]{:S(2)}) copy-start(bf16[8,128,128]{2,1,0:T(8,128)(2,1)S(1)} %collective-permute-done.1.refs_0_) | copy-start | bytes 786436
  29.9 11.8 %collective-permute-start.2 = (bf16[8,128,128]{2,1,0:T(8,128)(2,1)S(1)}, bf16[8,128,128]{2,1,0:T(8,128)(2,1)S(1)}, u32[]{:S(2)}, u32[]{:S(2)}) collective-permute-start(bf16[8,128,128]{2,1,0:T(8,128)(2,1)S(1)} %fusion), channel_id=1, source_target_pairs={{0,4},{1,5},{2,6},{3,7},{4,0},{5,1},{6,2},{7,3},{8,12},{9,13},{10,... | collective-permute-start | bytes 786440 | tf_op jit(solution)/shard_map/ppermute | solution.py:256
  32.8 8.8 %copy-start.3 = (f32[16,128,128]{2,1,0:T(8,128)S(1)}, f32[16,128,128]{2,1,0:T(8,128)}, u32[]{:S(2)}) copy-start(f32[16,128,128]{2,1,0:T(8,128)} %get-tuple-element.24) | copy-start | bytes 3145732
  41.7 11.7 %copy-start.5 = (bf16[8,128,128]{2,1,0:T(8,128)(2,1)}, bf16[8,128,128]{2,1,0:T(8,128)(2,1)S(1)}, u32[]{:S(2)}) copy-start(bf16[8,128,128]{2,1,0:T(8,128)(2,1)S(1)} %collective-permute-done.2.refs_1_) | copy-start | bytes 786436
  42.9 10.5 %collective-permute-start.3 = (bf16[8,128,128]{2,1,0:T(8,128)(2,1)S(1)}, bf16[8,128,128]{2,1,0:T(8,128)(2,1)S(1)}, u32[]{:S(2)}, u32[]{:S(2)}) collective-permute-start(bf16[8,128,128]{2,1,0:T(8,128)(2,1)S(1)} %get-tuple-element.31), channel_id=1, source_target_pairs={{0,8},{1,9},{2,10},{3,11},{4,12},{5,13},{6,14},{7,15},{8,0},{9,1},... | collective-permute-start | bytes 786440 | tf_op jit(solution)/shard_map/ppermute | solution.py:256
  53.4 12.6 %copy-start.1 = (bf16[8,128,128]{2,1,0:T(8,128)(2,1)}, bf16[8,128,128]{2,1,0:T(8,128)(2,1)S(1)}, u32[]{:S(2)}) copy-start(bf16[8,128,128]{2,1,0:T(8,128)(2,1)S(1)} %collective-permute-done.3.refs_2_) | copy-start | bytes 786436
  53.4 8.6 %collective-permute-start.4 = (bf16[8,128,128]{2,1,0:T(8,128)(2,1)S(1)}, bf16[8,128,128]{2,1,0:T(8,128)(2,1)S(1)}, u32[]{:S(2)}, u32[]{:S(2)}) collective-permute-start(bf16[8,128,128]{2,1,0:T(8,128)(2,1)S(1)} %fusion.1), channel_id=1, source_target_pairs={{0,16},{1,17},{2,18},{3,19},{4,20},{5,21},{6,22},{7,23},{8,24},{9,... | collective-permute-start | bytes 786440 | tf_op jit(solution)/shard_map/ppermute | solution.py:256
  62.1 15.2 %copy-start.4 = (bf16[8,128,128]{2,1,0:T(8,128)(2,1)}, bf16[8,128,128]{2,1,0:T(8,128)(2,1)S(1)}, u32[]{:S(2)}) copy-start(bf16[8,128,128]{2,1,0:T(8,128)(2,1)S(1)} %collective-permute-done.4.refs_3_) | copy-start | bytes 786436
  62.2 14.6 %copy-start.6 = (bf16[8,128,128]{2,1,0:T(8,128)(2,1)S(1)}, bf16[8,128,128]{2,1,0:T(8,128)(2,1)}, u32[]{:S(2)}) copy-start(bf16[8,128,128]{2,1,0:T(8,128)(2,1)} %copy-done.5) | copy-start | bytes 786436
  62.2 10.6 %collective-permute-start.5 = (bf16[8,128,128]{2,1,0:T(8,128)(2,1)S(1)}, bf16[8,128,128]{2,1,0:T(8,128)(2,1)S(1)}, u32[]{:S(2)}, u32[]{:S(2)}) collective-permute-start(bf16[8,128,128]{2,1,0:T(8,128)(2,1)S(1)} %fusion.2), channel_id=1, source_target_pairs={{0,32},{1,33},{2,34},{3,35},{4,36},{5,37},{6,38},{7,39},{8,40},{9,... | collective-permute-start | bytes 786440 | tf_op jit(solution)/shard_map/ppermute | solution.py:256
  63.3 14.3 %collective-permute-start.7 = (bf16[8,128,128]{2,1,0:T(8,128)(2,1)S(1)}, bf16[8,128,128]{2,1,0:T(8,128)(2,1)S(1)}, u32[]{:S(2)}, u32[]{:S(2)}) collective-permute-start(bf16[8,128,128]{2,1,0:T(8,128)(2,1)S(1)} %collective-permute-done.1.refs_0_), channel_id=1, source_target_pairs={{0,1},{1,0},{2,3},{3,2},{4,5},{5,4},{6,7},{7,6},{8,9},{9,8},{10,11... | collective-permute-start | bytes 786440 | tf_op jit(solution)/shard_map/ppermute | solution.py:256
  72.8 25.5 %copy-start.7 = (bf16[8,128,128]{2,1,0:T(8,128)(2,1)}, bf16[8,128,128]{2,1,0:T(8,128)(2,1)S(1)}, u32[]{:S(2)}) copy-start(bf16[8,128,128]{2,1,0:T(8,128)(2,1)S(1)} %collective-permute-done.5.refs_4_) | copy-start | bytes 786436
  74.0 15.2 %collective-permute-start.6 = (bf16[8,128,128]{2,1,0:T(8,128)(2,1)S(1)}, bf16[8,128,128]{2,1,0:T(8,128)(2,1)S(1)}, u32[]{:S(2)}, u32[]{:S(2)}) collective-permute-start(bf16[8,128,128]{2,1,0:T(8,128)(2,1)S(1)} %add_convert_fusion), channel_id=1, source_target_pairs={{0,64},{1,65},{2,66},{3,67},{4,68},{5,69},{6,70},{7,71},{8,72},{9,... | collective-permute-start | bytes 786440 | tf_op jit(solution)/shard_map/ppermute | solution.py:256
  76.8 13.2 %collective-permute-start.8 = (bf16[8,128,128]{2,1,0:T(8,128)(2,1)S(1)}, bf16[8,128,128]{2,1,0:T(8,128)(2,1)S(1)}, u32[]{:S(2)}, u32[]{:S(2)}) collective-permute-start(bf16[8,128,128]{2,1,0:T(8,128)(2,1)S(1)} %copy-done.6), channel_id=1, source_target_pairs={{0,1},{1,0},{2,3},{3,2},{4,5},{5,4},{6,7},{7,6},{8,9},{9,8},{10,11... | collective-permute-start | bytes 786440 | tf_op jit(solution)/shard_map/ppermute | solution.py:256
  77.1 12.9 %collective-permute-start.9 = (bf16[8,128,128]{2,1,0:T(8,128)(2,1)}, bf16[8,128,128]{2,1,0:T(8,128)(2,1)S(1)}, u32[]{:S(2)}, u32[]{:S(2)}) collective-permute-start(bf16[8,128,128]{2,1,0:T(8,128)(2,1)} %copy-done.1), channel_id=1, source_target_pairs={{0,1},{1,0},{2,3},{3,2},{4,5},{5,4},{6,7},{7,6},{8,9},{9,8},{10,11... | collective-permute-start | bytes 786440 | tf_op jit(solution)/shard_map/ppermute | solution.py:256
  77.3 20.9 %collective-permute-start.10 = (bf16[8,128,128]{2,1,0:T(8,128)(2,1)S(1)}, bf16[8,128,128]{2,1,0:T(8,128)(2,1)S(1)}, u32[]{:S(2)}, u32[]{:S(2)}) collective-permute-start(bf16[8,128,128]{2,1,0:T(8,128)(2,1)S(1)} %collective-permute-done.4.refs_3_), channel_id=1, source_target_pairs={{0,1},{1,0},{2,3},{3,2},{4,5},{5,4},{6,7},{7,6},{8,9},{9,8},{10,11... | collective-permute-start | bytes 786440 | tf_op jit(solution)/shard_map/ppermute | solution.py:256
  77.6 12.4 %copy-start.8 = (bf16[8,128,128]{2,1,0:T(8,128)(2,1)}, bf16[8,128,128]{2,1,0:T(8,128)(2,1)S(1)}, u32[]{:S(2)}) copy-start(bf16[8,128,128]{2,1,0:T(8,128)(2,1)S(1)} %collective-permute-done.7.refs_0_) | copy-start | bytes 786436
  77.6 20.6 %collective-permute-start.11 = (bf16[8,128,128]{2,1,0:T(8,128)(2,1)S(1)}, bf16[8,128,128]{2,1,0:T(8,128)(2,1)S(1)}, u32[]{:S(2)}, u32[]{:S(2)}) collective-permute-start(bf16[8,128,128]{2,1,0:T(8,128)(2,1)S(1)} %collective-permute-done.5.refs_4_), channel_id=1, source_target_pairs={{0,1},{1,0},{2,3},{3,2},{4,5},{5,4},{6,7},{7,6},{8,9},{9,8},{10,11... | collective-permute-start | bytes 786440 | tf_op jit(solution)/shard_map/ppermute | solution.py:256
  89.1 9.2 %copy-start.12 = (bf16[8,128,128]{2,1,0:T(8,128)(2,1)}, bf16[8,128,128]{2,1,0:T(8,128)(2,1)S(1)}, u32[]{:S(2)}) copy-start(bf16[8,128,128]{2,1,0:T(8,128)(2,1)S(1)} %collective-permute-done.6.refs_5_) | copy-start | bytes 786436
  89.1 9.1 %collective-permute-start.12 = (bf16[8,128,128]{2,1,0:T(8,128)(2,1)S(1)}, bf16[8,128,128]{2,1,0:T(8,128)(2,1)S(1)}, u32[]{:S(2)}, u32[]{:S(2)}) collective-permute-start(bf16[8,128,128]{2,1,0:T(8,128)(2,1)S(1)} %collective-permute-done.6.refs_5_), channel_id=1, source_target_pairs={{0,1},{1,0},{2,3},{3,2},{4,5},{5,4},{6,7},{7,6},{8,9},{9,8},{10,11... | collective-permute-start | bytes 786440 | tf_op jit(solution)/shard_map/ppermute | solution.py:256
  90.0 0.7 copy-start.9
  90.7 0.7 copy-start.10
  98.2 0.7 copy-start.13
  98.3 0.8 copy-start.14
  98.3 0.9 copy-start.15
Sparse Core Ops, SparseCore 0:
  10.3 81.2 all-gather.1

commit v3 on v0

v3 whole, which is shorter than its diff:
```python
import functools

import jax
import jax.numpy as jnp
from jax import lax
from jax.experimental import pallas as pl
from jax.experimental.pallas import tpu as pltpu
from jax.sharding import PartitionSpec as P

HEADS = 16
HEAD = 128
GATES = 8
HALF = HEADS // 2
QUARTER = HEADS // 4
ROWS = 1024
CHUNK = 256
CHUNKS = ROWS // CHUNK
EPSILON = 1e-06
VMEM_MIB = 60
F32 = jnp.float32
BF16 = jnp.bfloat16
NN = ((1,), (0,))
NT = ((1,), (1,))


def params():
    return pltpu.CompilerParams(vmem_limit_bytes=VMEM_MIB << 20)


def cost(flops, moved):
    return pl.CostEstimate(flops=int(flops), bytes_accessed=int(moved), transcendentals=0)


def dot(a, b, contract=NN):
    return lax.dot_general(a, b, (contract, ((), ())), preferred_element_type=F32)


def state_body(k_ref, v_ref, total_ref, sent_ref, prefix_ref, vt_ref):
    for pair in range(2):
        cols = slice(pair * HEAD, (pair + 1) * HEAD)
        vt = jnp.transpose(v_ref[:, cols])
        vt_ref[cols, :] = vt
        total = None
        for c in range(CHUNKS):
            rows = slice(c * CHUNK, (c + 1) * CHUNK)
            part = dot(vt[:, rows], k_ref[rows, cols])
            total = part if total is None else total + part
            if c + 1 < CHUNKS:
                prefix_ref[pair, c] = total.astype(BF16)
        total_ref[pair] = total
        sent_ref[pair] = total.astype(BF16)


def states(keys, values):
    block = pl.BlockSpec((ROWS, 2 * HEAD), lambda i: (0, i))
    square = pl.BlockSpec((2, HEAD, HEAD), lambda i: (i, 0, 0))
    return pl.pallas_call(
        state_body,
        grid=(HEADS // 2,),
        in_specs=[block, block],
        out_specs=[
            square,
            square,
            pl.BlockSpec((2, CHUNKS - 1, HEAD, HEAD), lambda i: (i, 0, 0, 0)),
            pl.BlockSpec((2 * HEAD, ROWS), lambda i: (i, 0)),
        ],
        out_shape=[
            jax.ShapeDtypeStruct((HEADS, HEAD, HEAD), F32),
            jax.ShapeDtypeStruct((HEADS, HEAD, HEAD), BF16),
            jax.ShapeDtypeStruct((HEADS, CHUNKS - 1, HEAD, HEAD), BF16),
            jax.ShapeDtypeStruct((HEADS * HEAD, ROWS), BF16),
        ],
        compiler_params=params(),
        cost_estimate=cost(1e9, 14 << 20),
        name="states",
    )(keys, values)


def quarter_of(number, s):
    side, sub = divmod(number, 2)
    return (s[0] ^ side) * 2 + (s[1] ^ sub)


def local_body(number, s_ref, q_ref, k_ref, vt_ref, prefix_ref, first_ref, gate0_ref, gate1_ref, out_ref):
    within = lax.rem(quarter_of(number, s_ref) * QUARTER + pl.program_id(0), HEADS)
    causal = lax.broadcasted_iota(jnp.int32, (CHUNK, CHUNK), 0) <= lax.broadcasted_iota(
        jnp.int32, (CHUNK, CHUNK), 1
    )
    w0 = gate0_ref[pl.ds(within, 1), :]
    w1 = gate1_ref[pl.ds(within, 1), :]
    for c in range(CHUNKS):
        rows = slice(c * CHUNK, (c + 1) * CHUNK)
        q = q_ref[rows, :]
        scores = dot(k_ref[rows, :], q, NT)
        scores = jnp.where(causal, scores, 0.0).astype(BF16)
        mixed = dot(vt_ref[:, rows], scores)
        if c:
            both = jnp.concatenate([prefix_ref[0, c - 1], first_ref[0]], axis=0)
            both = dot(both, q, NT)
            mixed = mixed + both[:HEAD]
            level = both[HEAD:]
        else:
            level = dot(first_ref[0], q, NT)
        out_ref[:, rows] = mixed * w0[:, rows] + level * w1[:, rows]


def local(number, scalars, queries, keys, vt, prefix, first, gate):
    where = lambda i, s: quarter_of(number, s) * QUARTER + i
    block = pl.BlockSpec((ROWS, HEAD), lambda i, s: (0, where(i, s)))
    return pl.pallas_call(
        functools.partial(local_body, number),
        grid_spec=pltpu.PrefetchScalarGridSpec(
            num_scalar_prefetch=1,
            grid=(QUARTER,),
            in_specs=[
                block,
                block,
                pl.BlockSpec((HEAD, ROWS), lambda i, s: (where(i, s), 0)),
                pl.BlockSpec((1, CHUNKS - 1, HEAD, HEAD), lambda i, s: (where(i, s), 0, 0, 0)),
                pl.BlockSpec((1, HEAD, HEAD), lambda i, s: (where(i, s), 0, 0)),
                pl.BlockSpec((HEADS, ROWS), lambda i, s: (0, 0)),
                pl.BlockSpec((HEADS, ROWS), lambda i, s: (1, 0)),
            ],
            out_specs=pl.BlockSpec((HEAD, ROWS), lambda i, s: (i, 0)),
        ),
        out_shape=jax.ShapeDtypeStruct((QUARTER * HEAD, ROWS), F32),
        compiler_params=params(),
        cost_estimate=cost(2e9, 6 << 20),
        name=f"local{number}",
    )(scalars, queries, keys, vt, prefix, first, gate, gate)


def norm_body(count, s_ref, *refs):
    gate_ref, gain_ref, out_ref = refs[-3:]
    for number in range(4):
        q_ref, a_ref, *buckets = refs[number * (2 + count) : (number + 1) * (2 + count)]
        head = quarter_of(number, s_ref) * QUARTER + pl.program_id(0)
        squares = jnp.concatenate([b[0] for b in buckets], axis=0)
        gain = gain_ref[pl.ds(head, 1), :]
        weights = [gate_ref[pl.ds((n + 2) * HEADS + head, 1), :] for n in range(count)]
        for c in range(CHUNKS):
            rows = slice(c * CHUNK, (c + 1) * CHUNK)
            products = dot(squares, q_ref[rows, :], NT)
            x = a_ref[:, rows]
            for n in range(count):
                x = x + products[n * HEAD : (n + 1) * HEAD] * weights[n][:, rows]
            mean = jnp.mean(x * x, axis=0, keepdims=True)
            x = jnp.transpose(x * lax.rsqrt(mean + EPSILON))
            cols = pl.ds(pl.multiple_of(head * HEAD, HEAD), HEAD)
            out_ref[rows, cols] = (x * gain).astype(BF16)


def normed(scalars, queries, attended, buckets, gate, gain):
    count = len(buckets[0])
    operands, specs = [], []
    for number in range(4):
        head = lambda i, s, number=number: (0, quarter_of(number, s) * QUARTER + i)
        operands += [queries, attended[number]]
        specs += [pl.BlockSpec((ROWS, HEAD), head), pl.BlockSpec((HEAD, ROWS), lambda i, s: (i, 0))]
        for array, index in buckets[number]:
            operands.append(array)
            specs.append(pl.BlockSpec((1, HEAD, HEAD), lambda i, s, index=index: (index(i, s), 0, 0)))
    return pl.pallas_call(
        functools.partial(norm_body, count),
        grid_spec=pltpu.PrefetchScalarGridSpec(
            num_scalar_prefetch=1,
            grid=(QUARTER,),
            in_specs=[
                *specs,
                pl.BlockSpec((GATES * HEADS, ROWS), lambda i, s: (0, 0)),
                pl.BlockSpec((HEADS, HEAD), lambda i, s: (0, 0)),
            ],
            out_specs=pl.BlockSpec((ROWS, HEADS * HEAD), lambda i, s: (0, 0)),
        ),
        out_shape=jax.ShapeDtypeStruct((ROWS, HEADS * HEAD), BF16),
        compiler_params=params(),
        cost_estimate=cost(4e9, 18 << 20),
        name="normed",
    )(scalars, *operands, gate, gain)


def project_body(n_ref, w_ref, out_ref):
    out_ref[...] = dot(n_ref[...], w_ref[...]).astype(BF16)


def project(rows, weight):
    tile = 256
    return pl.pallas_call(
        project_body,
        grid=(HEADS * HEAD // tile,),
        in_specs=[
            pl.BlockSpec((ROWS, HEADS * HEAD), lambda i: (0, 0)),
            pl.BlockSpec((HEADS * HEAD, tile), lambda i: (0, i)),
        ],
        out_specs=pl.BlockSpec((ROWS, tile), lambda i: (0, i)),
        out_shape=jax.ShapeDtypeStruct((ROWS, HEADS * HEAD), BF16),
        compiler_params=params(),
        cost_estimate=cost(8e9, 16 << 20),
        name="project",
    )(rows, weight)


def from_partner(value, axis, bit):
    mask = 2**bit
    pairs = [(source, source ^ mask) for source in range(lax.axis_size(axis))]
    return lax.ppermute(value, axis, pairs)


def plain_bucket(array, number):
    return array, lambda i, s: (s[1] ^ (number % 2)) * QUARTER + i


def batch_bucket(array, number, at, size):
    return array, lambda i, s: (number % 2) * size * QUARTER + at * QUARTER + i


def shards(queries, keys, values, level_gate, norm_gain, out_weight):
    position = lax.axis_index("ctx")
    levels = lax.axis_size("ctx").bit_length() - 1
    core = position & 1
    near = position >> 1 & 1
    scalars = jnp.stack([core, near]).astype(jnp.int32)
    whole_weight = lax.all_gather(out_weight, "ctx", axis=0, tiled=True)
    bits = position >> jnp.arange(levels, dtype=jnp.int32) & 1
    present = jnp.concatenate([jnp.ones((1,), F32), bits.astype(F32)])
    gate = level_gate.T.astype(F32) * jnp.repeat(present, HEADS)[:, None]
    total, sent, prefix, vt = states(keys, values)
    first = from_partner(sent, "ctx", 0)
    running = lax.dynamic_slice_in_dim(total, core * HALF, HALF) + lax.dynamic_slice_in_dim(
        first, core * HALF, HALF
    ).astype(F32)
    attended = []
    buckets = [[] for _ in range(4)]
    batch = []
    for level in range(1, levels):
        outgoing = running.astype(BF16)
        if level <= 4:
            if level > 2:
                outgoing, q, attended[level - 3] = lax.optimization_barrier(
                    (outgoing, queries, attended[level - 3])
                )
            else:
                outgoing, q = lax.optimization_barrier((outgoing, queries))
            attended.append(local(level - 1, scalars, q, keys, vt, prefix, first, gate))
        elif level - 3 < 4:
            outgoing, attended[level - 3] = lax.optimization_barrier((outgoing, attended[level - 3]))
        received = from_partner(outgoing, "ctx", level)
        if level == 1:
            other = from_partner(received, "ctx", 0)
            for number in range(4):
                buckets[number].append(plain_bucket((received, other)[number // 2], number))
            running = lax.dynamic_slice_in_dim(running, near * QUARTER, QUARTER) + lax.dynamic_slice_in_dim(
                received, near * QUARTER, QUARTER
            ).astype(F32)
            continue
        batch.append(received)
        if level % 2 or level + 1 == levels:
            size = len(batch)
            here = jnp.concatenate(batch) if size > 1 else batch[0]
            chip = jnp.concatenate([here, from_partner(here, "ctx", 1)])
            other = from_partner(chip, "ctx", 0)
            for at in range(size):
                for number in range(4):
                    buckets[number].append(batch_bucket((chip, other)[number // 2], number, at, size))
            batch = []
        if level + 1 < levels:
            running = running + received.astype(F32)
    gain = norm_gain.reshape(HEADS, HEAD)
    rows = normed(scalars, queries, attended, buckets, gate, gain)
    return project(rows, whole_weight)


def solution(mesh):
    placed = (P("ctx", None), P("ctx", None), P("ctx", None), P("ctx", None), P(), P("ctx", None))
    return jax.shard_map(
        shards, mesh=mesh, in_specs=placed, out_specs=P("ctx", None), check_vma=False
    )
```

time: 223 us -> 121 us (0.54); the launches traced: 220 us -> 120 us
  matrix products: 90.4 us -> 0 us
  waiting for transfers between devices: 84.3 us -> 11.1 us
  Pallas kernels: 0 us -> 61.7 us
  starting transfers between devices: 16.3 us -> 29.3 us
  local copies, waits for them, and re-layouts: 7.53 us -> 1.5 us
  other arithmetic: 7.6 us -> 3.21 us
    dot_general x10 -> x0, matrix products: 90.4 us -> none  [the longest x7 48.1 us: shards(): jnp.einsum('thd,hde->the', query_heads, bucket, preferred_element_type=jn...]
    ppermute x7 -> x14, waiting for transfers between devices: 83.6 us -> 10.3 us  [from_partner(): return lax.ppermute(value, axis, pairs)]
    pallas_call x0 -> x7, Pallas kernels: none -> 61.7 us  [the longest x4 24.7 us: local(): pl.pallas_call(functools.partial(local_body, number), grid_spec=pltpu.Pre...]
    ppermute x7 -> x14, starting transfers between devices: 16.3 us -> 29.3 us  [from_partner(): return lax.ppermute(value, axis, pairs)]
    reshape x1 -> x0, local copies, waits for them, and re-layouts: 6.4 us -> none  [shards(): key_heads = keys.reshape(rows_here, HEADS, HEAD)]
    convert_element_type x2 -> x7, other arithmetic: 5.33 us -> 1.55 us  [the longest x6 1.55 us: shards(): outgoing = running.astype(BF16)]
  transfers between devices with their start and end apart: 8 -> 15, of which waited for: 7 -> 4; matrix products, arithmetic and copies ran while one was open for 41% -> 3% of each run, Pallas kernels for 0% -> 40%
where the time goes in v3:
time: 121 us; the launch traced here: 120 us
  Pallas kernels  61.7 us (51%)
  starting transfers between devices  29.3 us (24%)
  between operations  13.6 us (11%)
  waiting for transfers between devices  11.1 us (9%)
  other arithmetic  3.21 us (3%)
  local copies, waits for them, and re-layouts  1.5 us (1%)
    ppermute x14, starting transfers between devices, from_partner(): return lax.ppermute(value, axis, pairs)  29.3 us
    pallas_call x4, Pallas kernels, local(): pl.pallas_call(functools.partial(local_body, number), grid_spec=pltpu.Pre...  24.7 us
    pallas_call x1, Pallas kernels, project(): pl.pallas_call(project_body, grid=(HEADS * HEAD // tile,), in_specs=[pl.B...  14 us
    pallas_call x1, Pallas kernels, normed(): pl.pallas_call(functools.partial(norm_body, count), grid_spec=pltpu.Prefe...  13.9 us
    ppermute x14, waiting for transfers between devices, from_partner(): return lax.ppermute(value, axis, pairs)  10.3 us
    pallas_call x1, Pallas kernels, states(): pl.pallas_call(state_body, grid=(HEADS // 2,), in_specs=[block, block], o...  9.06 us
  transfers between devices with their start and end apart: 15, of which 4 were waited for; matrix products, arithmetic and copies ran while one was open for 3% of the time, Pallas kernels for 40%

profile of v3, /device:TPU:1, one launch (start us, length us, event | category | flops | bytes accessed | tf_op | source)
XLA Modules:
  0.0 120.4 jit_solution(9308664767283714211)
XLA Ops:
  6.5 0.7 all-gather.2.cloned.1.call-update
  7.3 9.1 %states.1 = (f32[16,128,128]{2,1,0:T(8,128)}, bf16[16,128,128]{2,1,0:T(8,128)(2,1)}, bf16[16,3,128,128]{3,2,1,0:T(8,128)(2,1)}, bf16[2048,1024]{1,0:T(8,128)(2,1)}) custom-call(bf16[1024,2048]{1,0:T(8,128)(2,1)} %k_ref.9, bf16[1024,2048]{1,0:T(8,128)(2,1)} %v_ref.1), custom_call_target="tpu_custom_call" | custom-call | flops 1000000000 | bytes 14680064 | tf_op jit(solution)/shard_map/states/pallas_call | solution.py:57
  16.3 1.4 %collective-permute-start = (bf16[16,128,128]{2,1,0:T(8,128)(2,1)}, bf16[16,128,128]{2,1,0:T(8,128)(2,1)S(1)}, u32[]{:S(2)}, u32[]{:S(2)}) collective-permute-start(bf16[16,128,128]{2,1,0:T(8,128)(2,1)} %get-tuple-element.24), channel_id=1, source_target_pairs={{0,1},{1,0},{2,3},{3,2},{4,5},{5,4},{6,7},{7,6},{8,9},{9,8},{10,11... | collective-permute-start | bytes 1572872 | tf_op jit(solution)/shard_map/ppermute | solution.py:206
  18.1 0.9 multiply_bitcast_fusion.gate0_ref.gate1_ref.refs_32_
  19.0 0.4 collective-permute-done.first_ref
  19.5 1.3 %fusion.4 = (bf16[8,128,128]{2,1,0:T(8,128)(2,1)S(1)}, f32[8,128,128]{2,1,0:T(8,128)S(1)}) fusion(bf16[16,128,128]{2,1,0:T(8,128)(2,1)S(1)} %collective-permute-done.first_ref, s32[]{:T(128)S(6)} %select_n.8, f32[16,128,128]{2,1,0:T(8,128)} %get-tuple-element.23), kind=kLoop, calls=%fused_computation.24 | loop fusion | flops 393216 | bytes 1572868 | tf_op jit(solution)/shard_map/convert_element_type | solution.py:236
  20.8 1.4 %collective-permute-start.1 = (bf16[8,128,128]{2,1,0:T(8,128)(2,1)S(1)}, bf16[8,128,128]{2,1,0:T(8,128)(2,1)S(1)}, u32[]{:S(2)}, u32[]{:S(2)}) collective-permute-start(bf16[8,128,128]{2,1,0:T(8,128)(2,1)S(1)} %get-tuple-element.25), channel_id=1, source_target_pairs={{0,2},{1,3},{2,0},{3,1},{4,6},{5,7},{6,4},{7,5},{8,10},{9,11},{10,... | collective-permute-start | bytes 786440 | tf_op jit(solution)/shard_map/ppermute | solution.py:206
  22.2 0.6 pad_add_fusion.s_ref
  22.8 6.2 %local0.1.refs_1_ = f32[512,1024]{1,0:T(8,128)} custom-call(s32[2]{0:T(128)} %pad_add_fusion.s_ref, bf16[1024,2048]{1,0:T(8,128)(2,1)} %refs_24_.1, bf16[1024,2048]{1,0:T(8,128)(2,1)} %k_ref.9, bf16[2048,1024]{1,0:T(8,128)(2,1)} %get-tuple-element.28.vt_ref, bf16[16,3,128,128]{3,2,1,0:T(8,128)(2,1)} %get-tuple-element.29.prefix_ref, ...), custom_call_target="tpu_custom_call" | custom-call | flops 2000000000 | bytes 6291456 | tf_op jit(solution)/shard_map/local0/pallas_call | solution.py:110
  29.1 2.6 %collective-permute-start.2 = (bf16[4,128,128]{2,1,0:T(8,128)(2,1)S(1)}, bf16[4,128,128]{2,1,0:T(8,128)(2,1)S(1)}, u32[]{:S(2)}, u32[]{:S(2)}) collective-permute-start(bf16[4,128,128]{2,1,0:T(8,128)(2,1)S(1)} %fusion.2), channel_id=1, source_target_pairs={{0,4},{1,5},{2,6},{3,7},{4,0},{5,1},{6,2},{7,3},{8,12},{9,13},{10,... | collective-permute-start | bytes 393224 | tf_op jit(solution)/shard_map/ppermute | solution.py:206
  31.7 6.2 %local1.1.refs_9_ = f32[512,1024]{1,0:T(8,128)} custom-call(s32[2]{0:T(128)} %pad_add_fusion.s_ref, bf16[1024,2048]{1,0:T(8,128)(2,1)} %refs_24_.1, bf16[1024,2048]{1,0:T(8,128)(2,1)} %k_ref.9, bf16[2048,1024]{1,0:T(8,128)(2,1)} %get-tuple-element.28.vt_ref, bf16[16,3,128,128]{3,2,1,0:T(8,128)(2,1)} %get-tuple-element.29.prefix_ref, ...), custom_call_target="tpu_custom_call" | custom-call | flops 2000000000 | bytes 6291456 | tf_op jit(solution)/shard_map/local1/pallas_call | solution.py:110
  37.9 1.7 %collective-permute-start.3 = (bf16[4,128,128]{2,1,0:T(8,128)(2,1)S(1)}, bf16[4,128,128]{2,1,0:T(8,128)(2,1)S(1)}, u32[]{:S(2)}, u32[]{:S(2)}) collective-permute-start(bf16[4,128,128]{2,1,0:T(8,128)(2,1)S(1)} %fusion), channel_id=1, source_target_pairs={{0,8},{1,9},{2,10},{3,11},{4,12},{5,13},{6,14},{7,15},{8,0},{9,1},... | collective-permute-start | bytes 393224 | tf_op jit(solution)/shard_map/ppermute | solution.py:206
  39.6 6.2 %local2.1.refs_17_ = f32[512,1024]{1,0:T(8,128)} custom-call(s32[2]{0:T(128)} %pad_add_fusion.s_ref, bf16[1024,2048]{1,0:T(8,128)(2,1)} %refs_24_.1, bf16[1024,2048]{1,0:T(8,128)(2,1)} %k_ref.9, bf16[2048,1024]{1,0:T(8,128)(2,1)} %get-tuple-element.28.vt_ref, bf16[16,3,128,128]{3,2,1,0:T(8,128)(2,1)} %get-tuple-element.29.prefix_ref, ...), custom_call_target="tpu_custom_call" | custom-call | flops 2000000000 | bytes 6291456 | tf_op jit(solution)/shard_map/local2/pallas_call | solution.py:110
  45.9 3.5 %collective-permute-start.5 = (bf16[4,128,128]{2,1,0:T(8,128)(2,1)S(1)}, bf16[4,128,128]{2,1,0:T(8,128)(2,1)S(1)}, u32[]{:S(2)}, u32[]{:S(2)}) collective-permute-start(bf16[4,128,128]{2,1,0:T(8,128)(2,1)S(1)} %get-tuple-element.33), channel_id=1, source_target_pairs={{0,16},{1,17},{2,18},{3,19},{4,20},{5,21},{6,22},{7,23},{8,24},{9,... | collective-permute-start | bytes 393224 | tf_op jit(solution)/shard_map/ppermute | solution.py:206
  49.4 0.2 collective-permute-start.4
  49.6 6.2 %local3.1.refs_25_ = f32[512,1024]{1,0:T(8,128)} custom-call(s32[2]{0:T(128)} %pad_add_fusion.s_ref, bf16[1024,2048]{1,0:T(8,128)(2,1)} %refs_24_.1, bf16[1024,2048]{1,0:T(8,128)(2,1)} %k_ref.9, bf16[2048,1024]{1,0:T(8,128)(2,1)} %get-tuple-element.28.vt_ref, bf16[16,3,128,128]{3,2,1,0:T(8,128)(2,1)} %get-tuple-element.29.prefix_ref, ...), custom_call_target="tpu_custom_call" | custom-call | flops 2000000000 | bytes 6291456 | tf_op jit(solution)/shard_map/local3/pallas_call | solution.py:110
  55.8 1.6 %collective-permute-start.6 = (bf16[4,128,128]{2,1,0:T(8,128)(2,1)S(1)}, bf16[4,128,128]{2,1,0:T(8,128)(2,1)S(1)}, u32[]{:S(2)}, u32[]{:S(2)}) collective-permute-start(bf16[4,128,128]{2,1,0:T(8,128)(2,1)S(1)} %fusion.1), channel_id=1, source_target_pairs={{0,32},{1,33},{2,34},{3,35},{4,36},{5,37},{6,38},{7,39},{8,40},{9,... | collective-permute-start | bytes 393224 | tf_op jit(solution)/shard_map/ppermute | solution.py:206
  57.5 2.3 %collective-permute-done.6 = bf16[4,128,128]{2,1,0:T(8,128)(2,1)S(1)} collective-permute-done((bf16[4,128,128]{2,1,0:T(8,128)(2,1)S(1)}, bf16[4,128,128]{2,1,0:T(8,128)(2,1)S(1)}, u32[]{:S(2)}, u32[]{:S(2)}) %collective-permute-start.6) | collective-permute-done | bytes 131104 | tf_op jit(solution)/shard_map/ppermute | solution.py:206
  59.8 1.3 %collective-permute-start.7 = (bf16[8,128,128]{2,1,0:T(8,128)(2,1)S(1)}, bf16[8,128,128]{2,1,0:T(8,128)(2,1)S(1)}, u32[]{:S(2)}, u32[]{:S(2)}) collective-permute-start(bf16[8,128,128]{2,1,0:T(8,128)(2,1)S(1)} %pad_maximum_fusion.1), channel_id=1, source_target_pairs={{0,2},{1,3},{2,0},{3,1},{4,6},{5,7},{6,4},{7,5},{8,10},{9,11},{10,... | collective-permute-start | bytes 786440 | tf_op jit(solution)/shard_map/ppermute | solution.py:206
  61.2 3.1 %collective-permute-start.8 = (bf16[4,128,128]{2,1,0:T(8,128)(2,1)S(1)}, bf16[4,128,128]{2,1,0:T(8,128)(2,1)S(1)}, u32[]{:S(2)}, u32[]{:S(2)}) collective-permute-start(bf16[4,128,128]{2,1,0:T(8,128)(2,1)S(1)} %add_convert_fusion), channel_id=1, source_target_pairs={{0,64},{1,65},{2,66},{3,67},{4,68},{5,69},{6,70},{7,71},{8,72},{9,... | collective-permute-start | bytes 393224 | tf_op jit(solution)/shard_map/ppermute | solution.py:206
  64.4 4.1 %collective-permute-start.11 = (bf16[16,128,128]{2,1,0:T(8,128)(2,1)S(1)}, bf16[16,128,128]{2,1,0:T(8,128)(2,1)S(1)}, u32[]{:S(2)}, u32[]{:S(2)}) collective-permute-start(bf16[16,128,128]{2,1,0:T(8,128)(2,1)S(1)} %constant_dynamic-update-slice_fusion.refs_3_.refs_4_.refs_11_.refs_12_), channel_id=1, source_target_pairs={{0,1},{1,0},{2,3},{3,2},{4,5},{5,4},{6,7},{7,6},{8,9},{9,8},{10,11... | collective-permute-start | bytes 1572872 | tf_op jit(solution)/shard_map/ppermute | solution.py:206
  68.6 5.9 %collective-permute-start.12 = (bf16[16,128,128]{2,1,0:T(8,128)(2,1)S(1)}, bf16[16,128,128]{2,1,0:T(8,128)(2,1)S(1)}, u32[]{:S(2)}, u32[]{:S(2)}) collective-permute-start(bf16[16,128,128]{2,1,0:T(8,128)(2,1)S(1)} %constant_dynamic-update-slice_fusion.3.refs_5_.refs_6_.refs_13_.refs_14_), channel_id=1, source_target_pairs={{0,1},{1,0},{2,3},{3,2},{4,5},{5,4},{6,7},{7,6},{8,9},{9,8},{10,11... | collective-permute-start | bytes 1572872 | tf_op jit(solution)/shard_map/ppermute | solution.py:206
  74.5 1.4 %collective-permute-start.9 = (bf16[4,128,128]{2,1,0:T(8,128)(2,1)S(1)}, bf16[4,128,128]{2,1,0:T(8,128)(2,1)S(1)}, u32[]{:S(2)}, u32[]{:S(2)}) collective-permute-start(bf16[4,128,128]{2,1,0:T(8,128)(2,1)S(1)} %collective-permute-done.8), channel_id=1, source_target_pairs={{0,2},{1,3},{2,0},{3,1},{4,6},{5,7},{6,4},{7,5},{8,10},{9,11},{10,... | collective-permute-start | bytes 393224 | tf_op jit(solution)/shard_map/ppermute | solution.py:206
  75.9 0.4 collective-permute-start.10
  76.3 6.4 %collective-permute-done.9 = bf16[4,128,128]{2,1,0:T(8,128)(2,1)S(1)} collective-permute-done((bf16[4,128,128]{2,1,0:T(8,128)(2,1)S(1)}, bf16[4,128,128]{2,1,0:T(8,128)(2,1)S(1)}, u32[]{:S(2)}, u32[]{:S(2)}) %collective-permute-start.9) | collective-permute-done | bytes 131104 | tf_op jit(solution)/shard_map/ppermute | solution.py:206
  82.7 0.6 collective-permute-start.13
  83.4 1.2 collective-permute-done.13.refs_23_.refs_31_
  84.6 0.6 copy-done.8
  85.2 0.2 copy-done.3
  85.4 0.2 copy-done.4
  85.6 13.9 %normed.1.n_ref = bf16[1024,2048]{1,0:T(8,128)(2,1)} custom-call(s32[2]{0:T(128)} %pad_add_fusion.s_ref, bf16[1024,2048]{1,0:T(8,128)(2,1)} %refs_24_.1, f32[512,1024]{1,0:T(8,128)} %local0.1.refs_1_, bf16[8,128,128]{2,1,0:T(8,128)(2,1)} %copy-done.5, bf16[16,128,128]{2,1,0:T(8,128)(2,1)} %copy-done.1, bf16[16,128,128]{2,1,0:T(8,128)(2,1)} %copy-done.1, ...), custom_call_target="tpu_custom_call" | custom-call | flops 4000000000 | bytes 18874368 | tf_op jit(solution)/shard_map/normed/pallas_call | solution.py:163
  99.5 14.0 %project.1 = bf16[1024,2048]{1,0:T(8,128)(2,1)} custom-call(bf16[1024,2048]{1,0:T(8,128)(2,1)} %normed.1.n_ref, bf16[2048,2048]{1,0:T(8,128)(2,1)} %all-gather.2.cloned.1.call-done.w_ref), custom_call_target="tpu_custom_call" | custom-call | flops 8000000000 | bytes 16777216 | tf_op jit(solution)/shard_map/project/pallas_call | solution.py:188
  (49 shorter events, 0.9 us)
Async XLA Ops:
  6.5 93.0 %all-gather.2.cloned.1.call-start = ((), (), s32[]{:S(2)}) async-start(), calls=%async_computation | async-start | bytes 8454144 | tf_op jit(solution)/shard_map/all_gather | solution.py:223
  7.3 10.7 %copy-start.9 = (bf16[1024,128]{1,0:T(8,128)(2,1)S(1)}, bf16[1024,128]{1,0:T(8,128)(2,1)}, u32[]{:S(2)}) copy-start(bf16[1024,128]{1,0:T(8,128)(2,1)} %param.9) | copy-start | bytes 786436
  16.3 3.1 %collective-permute-start = (bf16[16,128,128]{2,1,0:T(8,128)(2,1)}, bf16[16,128,128]{2,1,0:T(8,128)(2,1)S(1)}, u32[]{:S(2)}, u32[]{:S(2)}) collective-permute-start(bf16[16,128,128]{2,1,0:T(8,128)(2,1)} %get-tuple-element.24), channel_id=1, source_target_pairs={{0,1},{1,0},{2,3},{3,2},{4,5},{5,4},{6,7},{7,6},{8,9},{9,8},{10,11... | collective-permute-start | bytes 1572872 | tf_op jit(solution)/shard_map/ppermute | solution.py:206
  19.5 3.3 %copy-start = (bf16[16,128,128]{2,1,0:T(8,128)(2,1)}, bf16[16,128,128]{2,1,0:T(8,128)(2,1)S(1)}, u32[]{:S(2)}) copy-start(bf16[16,128,128]{2,1,0:T(8,128)(2,1)S(1)} %collective-permute-done.first_ref) | copy-start | bytes 1572868
  20.8 8.2 %collective-permute-start.1 = (bf16[8,128,128]{2,1,0:T(8,128)(2,1)S(1)}, bf16[8,128,128]{2,1,0:T(8,128)(2,1)S(1)}, u32[]{:S(2)}, u32[]{:S(2)}) collective-permute-start(bf16[8,128,128]{2,1,0:T(8,128)(2,1)S(1)} %get-tuple-element.25), channel_id=1, source_target_pairs={{0,2},{1,3},{2,0},{3,1},{4,6},{5,7},{6,4},{7,5},{8,10},{9,11},{10,... | collective-permute-start | bytes 786440 | tf_op jit(solution)/shard_map/ppermute | solution.py:206
  29.0 46.9 %copy-start.5 = (bf16[8,128,128]{2,1,0:T(8,128)(2,1)}, bf16[8,128,128]{2,1,0:T(8,128)(2,1)S(1)}, u32[]{:S(2)}) copy-start(bf16[8,128,128]{2,1,0:T(8,128)(2,1)S(1)} %collective-permute-done.1.refs_2_.refs_10_) | copy-start | bytes 786436
  29.1 8.8 %collective-permute-start.2 = (bf16[4,128,128]{2,1,0:T(8,128)(2,1)S(1)}, bf16[4,128,128]{2,1,0:T(8,128)(2,1)S(1)}, u32[]{:S(2)}, u32[]{:S(2)}) collective-permute-start(bf16[4,128,128]{2,1,0:T(8,128)(2,1)S(1)} %fusion.2), channel_id=1, source_target_pairs={{0,4},{1,5},{2,6},{3,7},{4,0},{5,1},{6,2},{7,3},{8,12},{9,13},{10,... | collective-permute-start | bytes 393224 | tf_op jit(solution)/shard_map/ppermute | solution.py:206
  37.9 7.9 %collective-permute-start.3 = (bf16[4,128,128]{2,1,0:T(8,128)(2,1)S(1)}, bf16[4,128,128]{2,1,0:T(8,128)(2,1)S(1)}, u32[]{:S(2)}, u32[]{:S(2)}) collective-permute-start(bf16[4,128,128]{2,1,0:T(8,128)(2,1)S(1)} %fusion), channel_id=1, source_target_pairs={{0,8},{1,9},{2,10},{3,11},{4,12},{5,13},{6,14},{7,15},{8,0},{9,1},... | collective-permute-start | bytes 393224 | tf_op jit(solution)/shard_map/ppermute | solution.py:206
  45.9 9.9 %collective-permute-start.5 = (bf16[4,128,128]{2,1,0:T(8,128)(2,1)S(1)}, bf16[4,128,128]{2,1,0:T(8,128)(2,1)S(1)}, u32[]{:S(2)}, u32[]{:S(2)}) collective-permute-start(bf16[4,128,128]{2,1,0:T(8,128)(2,1)S(1)} %get-tuple-element.33), channel_id=1, source_target_pairs={{0,16},{1,17},{2,18},{3,19},{4,20},{5,21},{6,22},{7,23},{8,24},{9,... | collective-permute-start | bytes 393224 | tf_op jit(solution)/shard_map/ppermute | solution.py:206
  49.4 15.0 %collective-permute-start.4 = (bf16[8,128,128]{2,1,0:T(8,128)(2,1)S(1)}, bf16[8,128,128]{2,1,0:T(8,128)(2,1)S(1)}, u32[]{:S(2)}, u32[]{:S(2)}) collective-permute-start(bf16[8,128,128]{2,1,0:T(8,128)(2,1)S(1)} %pad_maximum_fusion), channel_id=1, source_target_pairs={{0,2},{1,3},{2,0},{3,1},{4,6},{5,7},{6,4},{7,5},{8,10},{9,11},{10,... | collective-permute-start | bytes 786440 | tf_op jit(solution)/shard_map/ppermute | solution.py:206
  55.8 4.0 %collective-permute-start.6 = (bf16[4,128,128]{2,1,0:T(8,128)(2,1)S(1)}, bf16[4,128,128]{2,1,0:T(8,128)(2,1)S(1)}, u32[]{:S(2)}, u32[]{:S(2)}) collective-permute-start(bf16[4,128,128]{2,1,0:T(8,128)(2,1)S(1)} %fusion.1), channel_id=1, source_target_pairs={{0,32},{1,33},{2,34},{3,35},{4,36},{5,37},{6,38},{7,39},{8,40},{9,... | collective-permute-start | bytes 393224 | tf_op jit(solution)/shard_map/ppermute | solution.py:206
  59.8 8.7 %collective-permute-start.7 = (bf16[8,128,128]{2,1,0:T(8,128)(2,1)S(1)}, bf16[8,128,128]{2,1,0:T(8,128)(2,1)S(1)}, u32[]{:S(2)}, u32[]{:S(2)}) collective-permute-start(bf16[8,128,128]{2,1,0:T(8,128)(2,1)S(1)} %pad_maximum_fusion.1), channel_id=1, source_target_pairs={{0,2},{1,3},{2,0},{3,1},{4,6},{5,7},{6,4},{7,5},{8,10},{9,11},{10,... | collective-permute-start | bytes 786440 | tf_op jit(solution)/shard_map/ppermute | solution.py:206
  61.2 13.2 %collective-permute-start.8 = (bf16[4,128,128]{2,1,0:T(8,128)(2,1)S(1)}, bf16[4,128,128]{2,1,0:T(8,128)(2,1)S(1)}, u32[]{:S(2)}, u32[]{:S(2)}) collective-permute-start(bf16[4,128,128]{2,1,0:T(8,128)(2,1)S(1)} %add_convert_fusion), channel_id=1, source_target_pairs={{0,64},{1,65},{2,66},{3,67},{4,68},{5,69},{6,70},{7,71},{8,72},{9,... | collective-permute-start | bytes 393224 | tf_op jit(solution)/shard_map/ppermute | solution.py:206
  64.4 20.1 %copy-start.1 = (bf16[16,128,128]{2,1,0:T(8,128)(2,1)}, bf16[16,128,128]{2,1,0:T(8,128)(2,1)S(1)}, u32[]{:S(2)}) copy-start(bf16[16,128,128]{2,1,0:T(8,128)(2,1)S(1)} %constant_dynamic-update-slice_fusion.refs_3_.refs_4_.refs_11_.refs_12_) | copy-start | bytes 1572868
  64.4 20.1 %collective-permute-start.11 = (bf16[16,128,128]{2,1,0:T(8,128)(2,1)S(1)}, bf16[16,128,128]{2,1,0:T(8,128)(2,1)S(1)}, u32[]{:S(2)}, u32[]{:S(2)}) collective-permute-start(bf16[16,128,128]{2,1,0:T(8,128)(2,1)S(1)} %constant_dynamic-update-slice_fusion.refs_3_.refs_4_.refs_11_.refs_12_), channel_id=1, source_target_pairs={{0,1},{1,0},{2,3},{3,2},{4,5},{5,4},{6,7},{7,6},{8,9},{9,8},{10,11... | collective-permute-start | bytes 1572872 | tf_op jit(solution)/shard_map/ppermute | solution.py:206
  68.5 16.0 %copy-start.2 = (bf16[16,128,128]{2,1,0:T(8,128)(2,1)}, bf16[16,128,128]{2,1,0:T(8,128)(2,1)S(1)}, u32[]{:S(2)}) copy-start(bf16[16,128,128]{2,1,0:T(8,128)(2,1)S(1)} %constant_dynamic-update-slice_fusion.3.refs_5_.refs_6_.refs_13_.refs_14_) | copy-start | bytes 1572868
  68.6 16.0 %collective-permute-start.12 = (bf16[16,128,128]{2,1,0:T(8,128)(2,1)S(1)}, bf16[16,128,128]{2,1,0:T(8,128)(2,1)S(1)}, u32[]{:S(2)}, u32[]{:S(2)}) collective-permute-start(bf16[16,128,128]{2,1,0:T(8,128)(2,1)S(1)} %constant_dynamic-update-slice_fusion.3.refs_5_.refs_6_.refs_13_.refs_14_), channel_id=1, source_target_pairs={{0,1},{1,0},{2,3},{3,2},{4,5},{5,4},{6,7},{7,6},{8,9},{9,8},{10,11... | collective-permute-start | bytes 1572872 | tf_op jit(solution)/shard_map/ppermute | solution.py:206
  74.5 8.2 %collective-permute-start.9 = (bf16[4,128,128]{2,1,0:T(8,128)(2,1)S(1)}, bf16[4,128,128]{2,1,0:T(8,128)(2,1)S(1)}, u32[]{:S(2)}, u32[]{:S(2)}) collective-permute-start(bf16[4,128,128]{2,1,0:T(8,128)(2,1)S(1)} %collective-permute-done.8), channel_id=1, source_target_pairs={{0,2},{1,3},{2,0},{3,1},{4,6},{5,7},{6,4},{7,5},{8,10},{9,11},{10,... | collective-permute-start | bytes 393224 | tf_op jit(solution)/shard_map/ppermute | solution.py:206
  75.9 7.5 %collective-permute-start.10 = (bf16[8,128,128]{2,1,0:T(8,128)(2,1)S(1)}, bf16[8,128,128]{2,1,0:T(8,128)(2,1)S(1)}, u32[]{:S(2)}, u32[]{:S(2)}) collective-permute-start(bf16[8,128,128]{2,1,0:T(8,128)(2,1)S(1)} %collective-permute-done.1.refs_2_.refs_10_), channel_id=1, source_target_pairs={{0,1},{1,0},{2,3},{3,2},{4,5},{5,4},{6,7},{7,6},{8,9},{9,8},{10,11... | collective-permute-start | bytes 786440 | tf_op jit(solution)/shard_map/ppermute | solution.py:206
  82.7 1.9 %copy-start.6 = (bf16[8,128,128]{2,1,0:T(8,128)(2,1)}, bf16[8,128,128]{2,1,0:T(8,128)(2,1)S(1)}, u32[]{:S(2)}) copy-start(bf16[8,128,128]{2,1,0:T(8,128)(2,1)S(1)} %constant_dynamic-update-slice_fusion.6.refs_7_.refs_15_) | copy-start | bytes 786436
  82.7 1.8 %collective-permute-start.13 = (bf16[8,128,128]{2,1,0:T(8,128)(2,1)S(1)}, bf16[8,128,128]{2,1,0:T(8,128)(2,1)S(1)}, u32[]{:S(2)}, u32[]{:S(2)}) collective-permute-start(bf16[8,128,128]{2,1,0:T(8,128)(2,1)S(1)} %constant_dynamic-update-slice_fusion.6.refs_7_.refs_15_), channel_id=1, source_target_pairs={{0,1},{1,0},{2,3},{3,2},{4,5},{5,4},{6,7},{7,6},{8,9},{9,8},{10,11... | collective-permute-start | bytes 786440 | tf_op jit(solution)/shard_map/ppermute | solution.py:206
  83.4 1.2 %copy-start.7 = (bf16[8,128,128]{2,1,0:T(8,128)(2,1)}, bf16[8,128,128]{2,1,0:T(8,128)(2,1)S(1)}, u32[]{:S(2)}) copy-start(bf16[8,128,128]{2,1,0:T(8,128)(2,1)S(1)} %collective-permute-done.10.refs_18_.refs_26_) | copy-start | bytes 786436
  84.5 0.7 copy-start.8
  84.5 0.9 copy-start.3
  84.5 1.1 copy-start.4
Sparse Core Ops, SparseCore 0:
  10.3 74.8 all-gather.1

commit v4 on v3

--- a/solution.py
+++ b/solution.py
@@ -6,6 +6,7 @@
 from jax.experimental import pallas as pl
 from jax.experimental.pallas import tpu as pltpu
 from jax.sharding import PartitionSpec as P
+
 
 HEADS = 16
 HEAD = 128
@@ -126,12 +127,23 @@
         out_shape=jax.ShapeDtypeStruct((QUARTER * HEAD, ROWS), F32),
         compiler_params=params(),
         cost_estimate=cost(2e9, 6 << 20),
-        name=f"local{number}",
     )(scalars, queries, keys, vt, prefix, first, gate, gate)
 
 
-def norm_body(count, s_ref, *refs):
-    gate_ref, gain_ref, out_ref = refs[-3:]
+def final_body(count, s_ref, *refs):
+    gate_ref, gain_ref, weight_ref, out_ref, normed_ref = refs[-5:]
+    step = pl.program_id(0)
+
+    @pl.when(step < QUARTER)
+    def _():
+        norm_heads(count, s_ref, refs[:-5], gate_ref, gain_ref, normed_ref)
+
+    @pl.when(step >= QUARTER)
+    def _():
+        out_ref[...] = dot(normed_ref[...], weight_ref[...]).astype(BF16)
+
+
+def norm_heads(count, s_ref, refs, gate_ref, gain_ref, out_ref):
     for number in range(4):
         q_ref, a_ref, *buckets = refs[number * (2 + count) : (number + 1) * (2 + count)]
         head = quarter_of(number, s_ref) * QUARTER + pl.program_id(0)
@@ -150,54 +162,38 @@
             out_ref[rows, cols] = (x * gain).astype(BF16)
 
 
-def normed(scalars, queries, attended, buckets, gate, gain):
+def final(scalars, queries, attended, buckets, gate, gain, weight):
     count = len(buckets[0])
+    tile = 256
+    early = lambda i: jnp.minimum(i, QUARTER - 1)
+    late = lambda i, s: (0, jnp.maximum(i - QUARTER, 0))
     operands, specs = [], []
     for number in range(4):
-        head = lambda i, s, number=number: (0, quarter_of(number, s) * QUARTER + i)
+        head = lambda i, s, number=number: (0, quarter_of(number, s) * QUARTER + early(i))
         operands += [queries, attended[number]]
-        specs += [pl.BlockSpec((ROWS, HEAD), head), pl.BlockSpec((HEAD, ROWS), lambda i, s: (i, 0))]
+        specs += [pl.BlockSpec((ROWS, HEAD), head), pl.BlockSpec((HEAD, ROWS), lambda i, s: (early(i), 0))]
         for array, index in buckets[number]:
             operands.append(array)
-            specs.append(pl.BlockSpec((1, HEAD, HEAD), lambda i, s, index=index: (index(i, s), 0, 0)))
+            specs.append(pl.BlockSpec((1, HEAD, HEAD), lambda i, s, index=index: (index(early(i), s), 0, 0)))
     return pl.pallas_call(
-        functools.partial(norm_body, count),
+        functools.partial(final_body, count),
         grid_spec=pltpu.PrefetchScalarGridSpec(
             num_scalar_prefetch=1,
-            grid=(QUARTER,),
+            grid=(QUARTER + HEADS * HEAD // tile,),
             in_specs=[
                 *specs,
                 pl.BlockSpec((GATES * HEADS, ROWS), lambda i, s: (0, 0)),
                 pl.BlockSpec((HEADS, HEAD), lambda i, s: (0, 0)),
+                pl.BlockSpec((HEADS * HEAD, tile), late),
             ],
-            out_specs=pl.BlockSpec((ROWS, HEADS * HEAD), lambda i, s: (0, 0)),
+            out_specs=pl.BlockSpec((ROWS, tile), late),
+            scratch_shapes=[pltpu.VMEM((ROWS, HEADS * HEAD), BF16)],
         ),
         out_shape=jax.ShapeDtypeStruct((ROWS, HEADS * HEAD), BF16),
         compiler_params=params(),
-        cost_estimate=cost(4e9, 18 << 20),
-        name="normed",
-    )(scalars, *operands, gate, gain)
-
-
-def project_body(n_ref, w_ref, out_ref):
-    out_ref[...] = dot(n_ref[...], w_ref[...]).astype(BF16)
-
-
-def project(rows, weight):
-    tile = 256
-    return pl.pallas_call(
-        project_body,
-        grid=(HEADS * HEAD // tile,),
-        in_specs=[
-            pl.BlockSpec((ROWS, HEADS * HEAD), lambda i: (0, 0)),
-            pl.BlockSpec((HEADS * HEAD, tile), lambda i: (0, i)),
-        ],
-        out_specs=pl.BlockSpec((ROWS, tile), lambda i: (0, i)),
-        out_shape=jax.ShapeDtypeStruct((ROWS, HEADS * HEAD), BF16),
-        compiler_params=params(),
-        cost_estimate=cost(8e9, 16 << 20),
-        name="project",
-    )(rows, weight)
+        cost_estimate=cost(12e9, 30 << 20),
+        name="final",
+    )(scalars, *operands, gate, gain, weight)
 
 
 def from_partner(value, axis, bit):
@@ -254,7 +250,7 @@
             ).astype(F32)
             continue
         batch.append(received)
-        if level % 2 or level + 1 == levels:
+        if level in (4, levels - 1):
             size = len(batch)
             here = jnp.concatenate(batch) if size > 1 else batch[0]
             chip = jnp.concatenate([here, from_partner(here, "ctx", 1)])
@@ -266,12 +262,10 @@
         if level + 1 < levels:
             running = running + received.astype(F32)
     gain = norm_gain.reshape(HEADS, HEAD)
-    rows = normed(scalars, queries, attended, buckets, gate, gain)
-    return project(rows, whole_weight)
+    return final(scalars, queries, attended, buckets, gate, gain, whole_weight)
 
 
 def solution(mesh):
     placed = (P("ctx", None), P("ctx", None), P("ctx", None), P("ctx", None), P(), P("ctx", None))
-    return jax.shard_map(
-        shards, mesh=mesh, in_specs=placed, out_specs=P("ctx", None), check_vma=False
-    )
+
+    return jax.shard_map(shards, mesh=mesh, in_specs=placed, out_specs=P("ctx", None), check_vma=False)

time: 121 us -> 129 us (1.066)
  waiting for transfers between devices: 11.1 us -> 23.9 us
  starting transfers between devices: 29.3 us -> 25.6 us
  Pallas kernels: 61.7 us -> 60 us
    ppermute x14 -> x12, waiting for transfers between devices: 10.3 us -> 23.2 us  [from_partner(): return lax.ppermute(value, axis, pairs)]
    ppermute x14 -> x12, starting transfers between devices: 29.3 us -> 25.6 us  [from_partner(): return lax.ppermute(value, axis, pairs)]
    pallas_call x2 -> x1, Pallas kernels: 27.9 us -> 26.2 us  [final(): pl.pallas_call(functools.partial(final_body, count), grid_spec=pltpu.Pref...]
  transfers between devices with their start and end apart: 15 -> 13, of which waited for: 4 -> 6; matrix products, arithmetic and copies ran while one was open for 3% -> 3% of each run, Pallas kernels for 40% -> 26%
where the time goes in v4:
time: 129 us; the launch traced here: 128 us
  Pallas kernels  60 us (47%)
  starting transfers between devices  25.6 us (20%)
  waiting for transfers between devices  23.9 us (19%)
  between operations  13.6 us (11%)
  other arithmetic  3.22 us (2%)
  local copies, waits for them, and re-layouts  1.59 us (1%)
    pallas_call x1, Pallas kernels, final(): pl.pallas_call(functools.partial(final_body, count), grid_spec=pltpu.Pref...  26.2 us
    ppermute x12, starting transfers between devices, from_partner(): return lax.ppermute(value, axis, pairs)  25.6 us
    pallas_call x4, Pallas kernels, local(): pl.pallas_call(functools.partial(local_body, number), grid_spec=pltpu.Pre...  24.8 us
    ppermute x12, waiting for transfers between devices, from_partner(): return lax.ppermute(value, axis, pairs)  23.2 us
    pallas_call x1, Pallas kernels, states(): pl.pallas_call(state_body, grid=(HEADS // 2,), in_specs=[block, block], o...  9.05 us
  transfers between devices with their start and end apart: 13, of which 6 were waited for; matrix products, arithmetic and copies ran while one was open for 3% of the time, Pallas kernels for 26%

profile of v4, /device:TPU:1, one launch (start us, length us, event | category | flops | bytes accessed | tf_op | source)
XLA Modules:
  0.0 127.9 jit_solution(8693053926515826275)
XLA Ops:
  6.5 0.7 all-gather.2.cloned.1.call-update
  7.3 9.0 %states.1 = (f32[16,128,128]{2,1,0:T(8,128)}, bf16[16,128,128]{2,1,0:T(8,128)(2,1)}, bf16[16,3,128,128]{3,2,1,0:T(8,128)(2,1)}, bf16[2048,1024]{1,0:T(8,128)(2,1)}) custom-call(bf16[1024,2048]{1,0:T(8,128)(2,1)} %k_ref.9, bf16[1024,2048]{1,0:T(8,128)(2,1)} %v_ref.1), custom_call_target="tpu_custom_call" | custom-call | flops 1000000000 | bytes 14680064 | tf_op jit(solution)/shard_map/states/pallas_call | solution.py:58
  16.3 1.4 %collective-permute-start = (bf16[16,128,128]{2,1,0:T(8,128)(2,1)}, bf16[16,128,128]{2,1,0:T(8,128)(2,1)S(1)}, u32[]{:S(2)}, u32[]{:S(2)}) collective-permute-start(bf16[16,128,128]{2,1,0:T(8,128)(2,1)} %get-tuple-element.24), channel_id=1, source_target_pairs={{0,1},{1,0},{2,3},{3,2},{4,5},{5,4},{6,7},{7,6},{8,9},{9,8},{10,11... | collective-permute-start | bytes 1572872 | tf_op jit(solution)/shard_map/ppermute | solution.py:202
  17.7 0.6 pad_add_fusion.s_ref
  18.3 1.1 collective-permute-done.first_ref
  19.4 1.3 %fusion.4 = (bf16[8,128,128]{2,1,0:T(8,128)(2,1)S(1)}, f32[8,128,128]{2,1,0:T(8,128)S(1)}) fusion(bf16[16,128,128]{2,1,0:T(8,128)(2,1)S(1)} %collective-permute-done.first_ref, s32[]{:T(128)S(6)} %select_n.8, f32[16,128,128]{2,1,0:T(8,128)} %get-tuple-element.23), kind=kLoop, calls=%fused_computation.23 | loop fusion | flops 393216 | bytes 1572868 | tf_op jit(solution)/shard_map/convert_element_type | solution.py:232
  20.8 1.4 %collective-permute-start.1 = (bf16[8,128,128]{2,1,0:T(8,128)(2,1)S(1)}, bf16[8,128,128]{2,1,0:T(8,128)(2,1)S(1)}, u32[]{:S(2)}, u32[]{:S(2)}) collective-permute-start(bf16[8,128,128]{2,1,0:T(8,128)(2,1)S(1)} %get-tuple-element.25), channel_id=1, source_target_pairs={{0,2},{1,3},{2,0},{3,1},{4,6},{5,7},{6,4},{7,5},{8,10},{9,11},{10,... | collective-permute-start | bytes 786440 | tf_op jit(solution)/shard_map/ppermute | solution.py:202
  22.4 0.2 copy.7
  22.6 0.9 multiply_bitcast_fusion.gate0_ref.gate1_ref.refs_32_
  23.4 5.2 %collective-permute-done.1.refs_2_.refs_10_ = bf16[8,128,128]{2,1,0:T(8,128)(2,1)S(1)} collective-permute-done((bf16[8,128,128]{2,1,0:T(8,128)(2,1)S(1)}, bf16[8,128,128]{2,1,0:T(8,128)(2,1)S(1)}, u32[]{:S(2)}, u32[]{:S(2)}) %collective-permute-start.1) | collective-permute-done | bytes 262176 | tf_op jit(solution)/shard_map/ppermute | solution.py:202
  28.7 2.9 %collective-permute-start.2 = (bf16[4,128,128]{2,1,0:T(8,128)(2,1)S(1)}, bf16[4,128,128]{2,1,0:T(8,128)(2,1)S(1)}, u32[]{:S(2)}, u32[]{:S(2)}) collective-permute-start(bf16[4,128,128]{2,1,0:T(8,128)(2,1)S(1)} %fusion.2), channel_id=1, source_target_pairs={{0,4},{1,5},{2,6},{3,7},{4,0},{5,1},{6,2},{7,3},{8,12},{9,13},{10,... | collective-permute-start | bytes 393224 | tf_op jit(solution)/shard_map/ppermute | solution.py:202
  31.7 6.2 %shard_map.64.refs_1_ = f32[512,1024]{1,0:T(8,128)} custom-call(s32[2]{0:T(128)} %pad_add_fusion.s_ref, bf16[1024,2048]{1,0:T(8,128)(2,1)} %refs_24_.1, bf16[1024,2048]{1,0:T(8,128)(2,1)} %k_ref.9, bf16[2048,1024]{1,0:T(8,128)(2,1)} %get-tuple-element.28.vt_ref, bf16[16,3,128,128]{3,2,1,0:T(8,128)(2,1)} %get-tuple-element.29.prefix_ref, ...), custom_call_target="tpu_custom_call" | custom-call | flops 2000000000 | bytes 6291456 | tf_op jit(solution)/shard_map/pallas_call | solution.py:111
  37.9 1.7 %collective-permute-start.3 = (bf16[4,128,128]{2,1,0:T(8,128)(2,1)S(1)}, bf16[4,128,128]{2,1,0:T(8,128)(2,1)S(1)}, u32[]{:S(2)}, u32[]{:S(2)}) collective-permute-start(bf16[4,128,128]{2,1,0:T(8,128)(2,1)S(1)} %fusion), channel_id=1, source_target_pairs={{0,8},{1,9},{2,10},{3,11},{4,12},{5,13},{6,14},{7,15},{8,0},{9,1},... | collective-permute-start | bytes 393224 | tf_op jit(solution)/shard_map/ppermute | solution.py:202
  39.7 6.2 %shard_map.65.refs_9_ = f32[512,1024]{1,0:T(8,128)} custom-call(s32[2]{0:T(128)} %pad_add_fusion.s_ref, bf16[1024,2048]{1,0:T(8,128)(2,1)} %refs_24_.1, bf16[1024,2048]{1,0:T(8,128)(2,1)} %k_ref.9, bf16[2048,1024]{1,0:T(8,128)(2,1)} %get-tuple-element.28.vt_ref, bf16[16,3,128,128]{3,2,1,0:T(8,128)(2,1)} %get-tuple-element.29.prefix_ref, ...), custom_call_target="tpu_custom_call" | custom-call | flops 2000000000 | bytes 6291456 | tf_op jit(solution)/shard_map/pallas_call | solution.py:111
  45.9 3.3 %collective-permute-start.4 = (bf16[4,128,128]{2,1,0:T(8,128)(2,1)S(1)}, bf16[4,128,128]{2,1,0:T(8,128)(2,1)S(1)}, u32[]{:S(2)}, u32[]{:S(2)}) collective-permute-start(bf16[4,128,128]{2,1,0:T(8,128)(2,1)S(1)} %get-tuple-element.33), channel_id=1, source_target_pairs={{0,16},{1,17},{2,18},{3,19},{4,20},{5,21},{6,22},{7,23},{8,24},{9,... | collective-permute-start | bytes 393224 | tf_op jit(solution)/shard_map/ppermute | solution.py:202
  49.2 6.2 %shard_map.66.refs_17_ = f32[512,1024]{1,0:T(8,128)} custom-call(s32[2]{0:T(128)} %pad_add_fusion.s_ref, bf16[1024,2048]{1,0:T(8,128)(2,1)} %refs_24_.1, bf16[1024,2048]{1,0:T(8,128)(2,1)} %k_ref.9, bf16[2048,1024]{1,0:T(8,128)(2,1)} %get-tuple-element.28.vt_ref, bf16[16,3,128,128]{3,2,1,0:T(8,128)(2,1)} %get-tuple-element.29.prefix_ref, ...), custom_call_target="tpu_custom_call" | custom-call | flops 2000000000 | bytes 6291456 | tf_op jit(solution)/shard_map/pallas_call | solution.py:111
  55.5 1.6 %collective-permute-start.6 = (bf16[4,128,128]{2,1,0:T(8,128)(2,1)S(1)}, bf16[4,128,128]{2,1,0:T(8,128)(2,1)S(1)}, u32[]{:S(2)}, u32[]{:S(2)}) collective-permute-start(bf16[4,128,128]{2,1,0:T(8,128)(2,1)S(1)} %fusion.1), channel_id=1, source_target_pairs={{0,32},{1,33},{2,34},{3,35},{4,36},{5,37},{6,38},{7,39},{8,40},{9,... | collective-permute-start | bytes 393224 | tf_op jit(solution)/shard_map/ppermute | solution.py:202
  57.1 6.2 %shard_map.67.refs_25_ = f32[512,1024]{1,0:T(8,128)} custom-call(s32[2]{0:T(128)} %pad_add_fusion.s_ref, bf16[1024,2048]{1,0:T(8,128)(2,1)} %refs_24_.1, bf16[1024,2048]{1,0:T(8,128)(2,1)} %k_ref.9, bf16[2048,1024]{1,0:T(8,128)(2,1)} %get-tuple-element.28.vt_ref, bf16[16,3,128,128]{3,2,1,0:T(8,128)(2,1)} %get-tuple-element.29.prefix_ref, ...), custom_call_target="tpu_custom_call" | custom-call | flops 2000000000 | bytes 6291456 | tf_op jit(solution)/shard_map/pallas_call | solution.py:111
  63.4 0.4 collective-permute-start.5
  63.8 2.8 %collective-permute-start.7 = (bf16[4,128,128]{2,1,0:T(8,128)(2,1)S(1)}, bf16[4,128,128]{2,1,0:T(8,128)(2,1)S(1)}, u32[]{:S(2)}, u32[]{:S(2)}) collective-permute-start(bf16[4,128,128]{2,1,0:T(8,128)(2,1)S(1)} %add_convert_fusion), channel_id=1, source_target_pairs={{0,64},{1,65},{2,66},{3,67},{4,68},{5,69},{6,70},{7,71},{8,72},{9,... | collective-permute-start | bytes 393224 | tf_op jit(solution)/shard_map/ppermute | solution.py:202
  66.6 4.2 %collective-permute-done.7 = bf16[4,128,128]{2,1,0:T(8,128)(2,1)S(1)} collective-permute-done((bf16[4,128,128]{2,1,0:T(8,128)(2,1)S(1)}, bf16[4,128,128]{2,1,0:T(8,128)(2,1)S(1)}, u32[]{:S(2)}, u32[]{:S(2)}) %collective-permute-start.7) | collective-permute-done | bytes 131104 | tf_op jit(solution)/shard_map/ppermute | solution.py:202
  70.8 1.3 %collective-permute-start.8 = (bf16[8,128,128]{2,1,0:T(8,128)(2,1)S(1)}, bf16[8,128,128]{2,1,0:T(8,128)(2,1)S(1)}, u32[]{:S(2)}, u32[]{:S(2)}) collective-permute-start(bf16[8,128,128]{2,1,0:T(8,128)(2,1)S(1)} %pad_maximum_fusion.1), channel_id=1, source_target_pairs={{0,2},{1,3},{2,0},{3,1},{4,6},{5,7},{6,4},{7,5},{8,10},{9,11},{10,... | collective-permute-start | bytes 786440 | tf_op jit(solution)/shard_map/ppermute | solution.py:202
  72.1 7.5 %collective-permute-done.5 = bf16[12,128,128]{2,1,0:T(8,128)(2,1)S(1)} collective-permute-done((bf16[12,128,128]{2,1,0:T(8,128)(2,1)S(1)}, bf16[12,128,128]{2,1,0:T(8,128)(2,1)S(1)}, u32[]{:S(2)}, u32[]{:S(2)}) %collective-permute-start.5) | collective-permute-done | bytes 393248 | tf_op jit(solution)/shard_map/ppermute | solution.py:202
  79.6 6.6 %collective-permute-start.10 = (bf16[24,128,128]{2,1,0:T(8,128)(2,1)S(1)}, bf16[24,128,128]{2,1,0:T(8,128)(2,1)S(1)}, u32[]{:S(2)}, u32[]{:S(2)}) collective-permute-start(bf16[24,128,128]{2,1,0:T(8,128)(2,1)S(1)} %constant_dynamic-update-slice_fusion.refs_3_.refs_4_.refs_5_.refs_11_.refs_12_.refs_13_), channel_id=1, source_target_pairs={{0,1},{1,0},{2,3},{3,2},{4,5},{5,4},{6,7},{7,6},{8,9},{9,8},{10,11... | collective-permute-start | bytes 2359304 | tf_op jit(solution)/shard_map/ppermute | solution.py:202
  86.3 3.4 %collective-permute-done.8 = bf16[8,128,128]{2,1,0:T(8,128)(2,1)S(1)} collective-permute-done((bf16[8,128,128]{2,1,0:T(8,128)(2,1)S(1)}, bf16[8,128,128]{2,1,0:T(8,128)(2,1)S(1)}, u32[]{:S(2)}, u32[]{:S(2)}) %collective-permute-start.8) | collective-permute-done | bytes 262176 | tf_op jit(solution)/shard_map/ppermute | solution.py:202
  89.7 2.0 %collective-permute-start.11 = (bf16[16,128,128]{2,1,0:T(8,128)(2,1)S(1)}, bf16[16,128,128]{2,1,0:T(8,128)(2,1)S(1)}, u32[]{:S(2)}, u32[]{:S(2)}) collective-permute-start(bf16[16,128,128]{2,1,0:T(8,128)(2,1)S(1)} %constant_dynamic-update-slice_fusion.4.refs_6_.refs_7_.refs_14_.refs_15_), channel_id=1, source_target_pairs={{0,1},{1,0},{2,3},{3,2},{4,5},{5,4},{6,7},{7,6},{8,9},{9,8},{10,11... | collective-permute-start | bytes 1572872 | tf_op jit(solution)/shard_map/ppermute | solution.py:202
  91.8 0.1 collective-permute-start.9
  91.9 1.8 %collective-permute-done.9.refs_18_.refs_26_ = bf16[8,128,128]{2,1,0:T(8,128)(2,1)S(1)} collective-permute-done((bf16[8,128,128]{2,1,0:T(8,128)(2,1)S(1)}, bf16[8,128,128]{2,1,0:T(8,128)(2,1)S(1)}, u32[]{:S(2)}, u32[]{:S(2)}) %collective-permute-start.9) | collective-permute-done | bytes 262176 | tf_op jit(solution)/shard_map/ppermute | solution.py:202
  93.8 0.6 copy-done.6
  94.4 0.2 copy-done.4
  94.6 0.3 copy-done.1
  94.9 26.2 %final.1 = bf16[1024,2048]{1,0:T(8,128)(2,1)} custom-call(s32[2]{0:T(128)} %pad_add_fusion.s_ref, bf16[1024,2048]{1,0:T(8,128)(2,1)} %refs_24_.1, f32[512,1024]{1,0:T(8,128)} %shard_map.64.refs_1_, bf16[8,128,128]{2,1,0:T(8,128)(2,1)} %copy-done.5, bf16[24,128,128]{2,1,0:T(8,128)(2,1)} %copy-done, bf16[24,128,128]{2,1,0:T(8,128)(2,1)} %copy-done, ...), custom_call_target="tpu_custom_call" | custom-call | flops 12000000000 | bytes 31457280 | tf_op jit(solution)/shard_map/final/pallas_call | solution.py:178
  (39 shorter events, 0.8 us)
Async XLA Ops:
  6.5 87.2 %all-gather.2.cloned.1.call-start = ((), (), s32[]{:S(2)}) async-start(), calls=%async_computation | async-start | bytes 8454144 | tf_op jit(solution)/shard_map/all_gather | solution.py:219
  7.3 15.1 %copy-start.7 = (bf16[1024,128]{1,0:T(8,128)(2,1)S(1)}, bf16[1024,128]{1,0:T(8,128)(2,1)}, u32[]{:S(2)}) copy-start(bf16[1024,128]{1,0:T(8,128)(2,1)} %param.9) | copy-start | bytes 786436
  16.3 3.1 %collective-permute-start = (bf16[16,128,128]{2,1,0:T(8,128)(2,1)}, bf16[16,128,128]{2,1,0:T(8,128)(2,1)S(1)}, u32[]{:S(2)}, u32[]{:S(2)}) collective-permute-start(bf16[16,128,128]{2,1,0:T(8,128)(2,1)} %get-tuple-element.24), channel_id=1, source_target_pairs={{0,1},{1,0},{2,3},{3,2},{4,5},{5,4},{6,7},{7,6},{8,9},{9,8},{10,11... | collective-permute-start | bytes 1572872 | tf_op jit(solution)/shard_map/ppermute | solution.py:202
  19.4 12.2 %copy-start.2 = (bf16[16,128,128]{2,1,0:T(8,128)(2,1)}, bf16[16,128,128]{2,1,0:T(8,128)(2,1)S(1)}, u32[]{:S(2)}) copy-start(bf16[16,128,128]{2,1,0:T(8,128)(2,1)S(1)} %collective-permute-done.first_ref) | copy-start | bytes 1572868
  20.8 7.9 %collective-permute-start.1 = (bf16[8,128,128]{2,1,0:T(8,128)(2,1)S(1)}, bf16[8,128,128]{2,1,0:T(8,128)(2,1)S(1)}, u32[]{:S(2)}, u32[]{:S(2)}) collective-permute-start(bf16[8,128,128]{2,1,0:T(8,128)(2,1)S(1)} %get-tuple-element.25), channel_id=1, source_target_pairs={{0,2},{1,3},{2,0},{3,1},{4,6},{5,7},{6,4},{7,5},{8,10},{9,11},{10,... | collective-permute-start | bytes 786440 | tf_op jit(solution)/shard_map/ppermute | solution.py:202
  28.7 63.1 %copy-start.5 = (bf16[8,128,128]{2,1,0:T(8,128)(2,1)}, bf16[8,128,128]{2,1,0:T(8,128)(2,1)S(1)}, u32[]{:S(2)}) copy-start(bf16[8,128,128]{2,1,0:T(8,128)(2,1)S(1)} %collective-permute-done.1.refs_2_.refs_10_) | copy-start | bytes 786436
  28.7 9.1 %collective-permute-start.2 = (bf16[4,128,128]{2,1,0:T(8,128)(2,1)S(1)}, bf16[4,128,128]{2,1,0:T(8,128)(2,1)S(1)}, u32[]{:S(2)}, u32[]{:S(2)}) collective-permute-start(bf16[4,128,128]{2,1,0:T(8,128)(2,1)S(1)} %fusion.2), channel_id=1, source_target_pairs={{0,4},{1,5},{2,6},{3,7},{4,0},{5,1},{6,2},{7,3},{8,12},{9,13},{10,... | collective-permute-start | bytes 393224 | tf_op jit(solution)/shard_map/ppermute | solution.py:202
  37.9 7.9 %collective-permute-start.3 = (bf16[4,128,128]{2,1,0:T(8,128)(2,1)S(1)}, bf16[4,128,128]{2,1,0:T(8,128)(2,1)S(1)}, u32[]{:S(2)}, u32[]{:S(2)}) collective-permute-start(bf16[4,128,128]{2,1,0:T(8,128)(2,1)S(1)} %fusion), channel_id=1, source_target_pairs={{0,8},{1,9},{2,10},{3,11},{4,12},{5,13},{6,14},{7,15},{8,0},{9,1},... | collective-permute-start | bytes 393224 | tf_op jit(solution)/shard_map/ppermute | solution.py:202
  45.9 9.5 %collective-permute-start.4 = (bf16[4,128,128]{2,1,0:T(8,128)(2,1)S(1)}, bf16[4,128,128]{2,1,0:T(8,128)(2,1)S(1)}, u32[]{:S(2)}, u32[]{:S(2)}) collective-permute-start(bf16[4,128,128]{2,1,0:T(8,128)(2,1)S(1)} %get-tuple-element.33), channel_id=1, source_target_pairs={{0,16},{1,17},{2,18},{3,19},{4,20},{5,21},{6,22},{7,23},{8,24},{9,... | collective-permute-start | bytes 393224 | tf_op jit(solution)/shard_map/ppermute | solution.py:202
  55.5 8.2 %collective-permute-start.6 = (bf16[4,128,128]{2,1,0:T(8,128)(2,1)S(1)}, bf16[4,128,128]{2,1,0:T(8,128)(2,1)S(1)}, u32[]{:S(2)}, u32[]{:S(2)}) collective-permute-start(bf16[4,128,128]{2,1,0:T(8,128)(2,1)S(1)} %fusion.1), channel_id=1, source_target_pairs={{0,32},{1,33},{2,34},{3,35},{4,36},{5,37},{6,38},{7,39},{8,40},{9,... | collective-permute-start | bytes 393224 | tf_op jit(solution)/shard_map/ppermute | solution.py:202
  63.4 16.2 %collective-permute-start.5 = (bf16[12,128,128]{2,1,0:T(8,128)(2,1)S(1)}, bf16[12,128,128]{2,1,0:T(8,128)(2,1)S(1)}, u32[]{:S(2)}, u32[]{:S(2)}) collective-permute-start(bf16[12,128,128]{2,1,0:T(8,128)(2,1)S(1)} %pad_maximum_fusion), channel_id=1, source_target_pairs={{0,2},{1,3},{2,0},{3,1},{4,6},{5,7},{6,4},{7,5},{8,10},{9,11},{10,... | collective-permute-start | bytes 1179656 | tf_op jit(solution)/shard_map/ppermute | solution.py:202
  63.8 7.0 %collective-permute-start.7 = (bf16[4,128,128]{2,1,0:T(8,128)(2,1)S(1)}, bf16[4,128,128]{2,1,0:T(8,128)(2,1)S(1)}, u32[]{:S(2)}, u32[]{:S(2)}) collective-permute-start(bf16[4,128,128]{2,1,0:T(8,128)(2,1)S(1)} %add_convert_fusion), channel_id=1, source_target_pairs={{0,64},{1,65},{2,66},{3,67},{4,68},{5,69},{6,70},{7,71},{8,72},{9,... | collective-permute-start | bytes 393224 | tf_op jit(solution)/shard_map/ppermute | solution.py:202
  70.8 18.9 %collective-permute-start.8 = (bf16[8,128,128]{2,1,0:T(8,128)(2,1)S(1)}, bf16[8,128,128]{2,1,0:T(8,128)(2,1)S(1)}, u32[]{:S(2)}, u32[]{:S(2)}) collective-permute-start(bf16[8,128,128]{2,1,0:T(8,128)(2,1)S(1)} %pad_maximum_fusion.1), channel_id=1, source_target_pairs={{0,2},{1,3},{2,0},{3,1},{4,6},{5,7},{6,4},{7,5},{8,10},{9,11},{10,... | collective-permute-start | bytes 786440 | tf_op jit(solution)/shard_map/ppermute | solution.py:202
  79.6 14.1 %copy-start = (bf16[24,128,128]{2,1,0:T(8,128)(2,1)}, bf16[24,128,128]{2,1,0:T(8,128)(2,1)S(1)}, u32[]{:S(2)}) copy-start(bf16[24,128,128]{2,1,0:T(8,128)(2,1)S(1)} %constant_dynamic-update-slice_fusion.refs_3_.refs_4_.refs_5_.refs_11_.refs_12_.refs_13_) | copy-start | bytes 2359300
  79.6 14.1 %collective-permute-start.10 = (bf16[24,128,128]{2,1,0:T(8,128)(2,1)S(1)}, bf16[24,128,128]{2,1,0:T(8,128)(2,1)S(1)}, u32[]{:S(2)}, u32[]{:S(2)}) collective-permute-start(bf16[24,128,128]{2,1,0:T(8,128)(2,1)S(1)} %constant_dynamic-update-slice_fusion.refs_3_.refs_4_.refs_5_.refs_11_.refs_12_.refs_13_), channel_id=1, source_target_pairs={{0,1},{1,0},{2,3},{3,2},{4,5},{5,4},{6,7},{7,6},{8,9},{9,8},{10,11... | collective-permute-start | bytes 2359304 | tf_op jit(solution)/shard_map/ppermute | solution.py:202
  89.7 4.0 %copy-start.3 = (bf16[16,128,128]{2,1,0:T(8,128)(2,1)}, bf16[16,128,128]{2,1,0:T(8,128)(2,1)S(1)}, u32[]{:S(2)}) copy-start(bf16[16,128,128]{2,1,0:T(8,128)(2,1)S(1)} %constant_dynamic-update-slice_fusion.4.refs_6_.refs_7_.refs_14_.refs_15_) | copy-start | bytes 1572868
  89.7 4.0 %collective-permute-start.11 = (bf16[16,128,128]{2,1,0:T(8,128)(2,1)S(1)}, bf16[16,128,128]{2,1,0:T(8,128)(2,1)S(1)}, u32[]{:S(2)}, u32[]{:S(2)}) collective-permute-start(bf16[16,128,128]{2,1,0:T(8,128)(2,1)S(1)} %constant_dynamic-update-slice_fusion.4.refs_6_.refs_7_.refs_14_.refs_15_), channel_id=1, source_target_pairs={{0,1},{1,0},{2,3},{3,2},{4,5},{5,4},{6,7},{7,6},{8,9},{9,8},{10,11... | collective-permute-start | bytes 1572872 | tf_op jit(solution)/shard_map/ppermute | solution.py:202
  91.8 1.9 %collective-permute-start.9 = (bf16[8,128,128]{2,1,0:T(8,128)(2,1)S(1)}, bf16[8,128,128]{2,1,0:T(8,128)(2,1)S(1)}, u32[]{:S(2)}, u32[]{:S(2)}) collective-permute-start(bf16[8,128,128]{2,1,0:T(8,128)(2,1)S(1)} %collective-permute-done.1.refs_2_.refs_10_), channel_id=1, source_target_pairs={{0,1},{1,0},{2,3},{3,2},{4,5},{5,4},{6,7},{7,6},{8,9},{9,8},{10,11... | collective-permute-start | bytes 786440 | tf_op jit(solution)/shard_map/ppermute | solution.py:202
  93.7 0.7 copy-start.6
  93.7 0.9 copy-start.4
  93.7 1.2 copy-start.1
Sparse Core Ops, SparseCore 0:
  10.3 80.2 all-gather.1

commit v5 on v3

--- a/solution.py
+++ b/solution.py
@@ -6,6 +6,7 @@
 from jax.experimental import pallas as pl
 from jax.experimental.pallas import tpu as pltpu
 from jax.sharding import PartitionSpec as P
+
 
 HEADS = 16
 HEAD = 128
@@ -126,7 +127,6 @@
         out_shape=jax.ShapeDtypeStruct((QUARTER * HEAD, ROWS), F32),
         compiler_params=params(),
         cost_estimate=cost(2e9, 6 << 20),
-        name=f"local{number}",
     )(scalars, queries, keys, vt, prefix, first, gate, gate)
 
 
@@ -254,7 +254,13 @@
             ).astype(F32)
             continue
         batch.append(received)
-        if level % 2 or level + 1 == levels:
+        if level + 1 == levels:
+            beside = from_partner(received, "ctx", 1)
+            pieces = [received, beside]
+            pieces += [from_partner(received, "ctx", 0), from_partner(beside, "ctx", 0)]
+            for number in range(4):
+                buckets[number].append((pieces[number], lambda i, s: i))
+        elif level in (3, 4, 5):
             size = len(batch)
             here = jnp.concatenate(batch) if size > 1 else batch[0]
             chip = jnp.concatenate([here, from_partner(here, "ctx", 1)])
@@ -272,6 +278,5 @@
 
 def solution(mesh):
     placed = (P("ctx", None), P("ctx", None), P("ctx", None), P("ctx", None), P(), P("ctx", None))
-    return jax.shard_map(
-        shards, mesh=mesh, in_specs=placed, out_specs=P("ctx", None), check_vma=False
-    )
+
+    return jax.shard_map(shards, mesh=mesh, in_specs=placed, out_specs=P("ctx", None), check_vma=False)

time: 121 us -> 118 us (0.975)
  waiting for transfers between devices: 11.1 us -> 6.91 us
    ppermute x14 -> x17, waiting for transfers between devices: 10.3 us -> 6.18 us  [from_partner(): return lax.ppermute(value, axis, pairs)]
    ppermute x14 -> x17, starting transfers between devices: 29.3 us -> 30.4 us  [from_partner(): return lax.ppermute(value, axis, pairs)]
  transfers between devices with their start and end apart: 15 -> 18, of which waited for: 4 -> 5; matrix products, arithmetic and copies ran while one was open for 3% -> 3% of each run, Pallas kernels for 40% -> 41%
where the time goes in v5:
time: 118 us; the launch traced here: 117 us
  Pallas kernels  61.9 us (52%)
  starting transfers between devices  30.4 us (26%)
  between operations  13.7 us (12%)
  waiting for transfers between devices  6.91 us (6%)
  other arithmetic  3.23 us (3%)
  local copies, waits for them, and re-layouts  1.3 us (1%)
    ppermute x17, starting transfers between devices, from_partner(): return lax.ppermute(value, axis, pairs)  30.4 us
    pallas_call x4, Pallas kernels, local(): pl.pallas_call(functools.partial(local_body, number), grid_spec=pltpu.Pre...  24.8 us
    pallas_call x1, Pallas kernels, normed(): pl.pallas_call(functools.partial(norm_body, count), grid_spec=pltpu.Prefe...  14 us
    pallas_call x1, Pallas kernels, project(): pl.pallas_call(project_body, grid=(HEADS * HEAD // tile,), in_specs=[pl.B...  14 us
    pallas_call x1, Pallas kernels, states(): pl.pallas_call(state_body, grid=(HEADS // 2,), in_specs=[block, block], o...  9.05 us
    ppermute x17, waiting for transfers between devices, from_partner(): return lax.ppermute(value, axis, pairs)  6.18 us
  transfers between devices with their start and end apart: 18, of which 5 were waited for; matrix products, arithmetic and copies ran while one was open for 3% of the time, Pallas kernels for 41%

profile of v5, /device:TPU:1, one launch (start us, length us, event | category | flops | bytes accessed | tf_op | source)
XLA Modules:
  0.0 117.4 jit_solution(16442100369396315444)
XLA Ops:
  6.5 0.7 all-gather.2.cloned.1.call-update
  7.3 9.1 %states.1 = (f32[16,128,128]{2,1,0:T(8,128)}, bf16[16,128,128]{2,1,0:T(8,128)(2,1)}, bf16[16,3,128,128]{3,2,1,0:T(8,128)(2,1)}, bf16[2048,1024]{1,0:T(8,128)(2,1)}) custom-call(bf16[1024,2048]{1,0:T(8,128)(2,1)} %k_ref.9, bf16[1024,2048]{1,0:T(8,128)(2,1)} %v_ref.1), custom_call_target="tpu_custom_call" | custom-call | flops 1000000000 | bytes 14680064 | tf_op jit(solution)/shard_map/states/pallas_call | solution.py:58
  16.3 1.4 %collective-permute-start = (bf16[16,128,128]{2,1,0:T(8,128)(2,1)}, bf16[16,128,128]{2,1,0:T(8,128)(2,1)S(1)}, u32[]{:S(2)}, u32[]{:S(2)}) collective-permute-start(bf16[16,128,128]{2,1,0:T(8,128)(2,1)} %get-tuple-element.24), channel_id=1, source_target_pairs={{0,1},{1,0},{2,3},{3,2},{4,5},{5,4},{6,7},{7,6},{8,9},{9,8},{10,11... | collective-permute-start | bytes 1572872 | tf_op jit(solution)/shard_map/ppermute | solution.py:206
  18.1 0.9 multiply_bitcast_fusion.gate0_ref.gate1_ref.refs_32_
  19.0 0.4 collective-permute-done.first_ref
  19.5 1.3 %fusion.4 = (bf16[8,128,128]{2,1,0:T(8,128)(2,1)S(1)}, f32[8,128,128]{2,1,0:T(8,128)S(1)}) fusion(bf16[16,128,128]{2,1,0:T(8,128)(2,1)S(1)} %collective-permute-done.first_ref, s32[]{:T(128)S(6)} %select_n.8, f32[16,128,128]{2,1,0:T(8,128)} %get-tuple-element.23), kind=kLoop, calls=%fused_computation.22 | loop fusion | flops 393216 | bytes 1572868 | tf_op jit(solution)/shard_map/convert_element_type | solution.py:236
  20.8 1.4 %collective-permute-start.1 = (bf16[8,128,128]{2,1,0:T(8,128)(2,1)S(1)}, bf16[8,128,128]{2,1,0:T(8,128)(2,1)S(1)}, u32[]{:S(2)}, u32[]{:S(2)}) collective-permute-start(bf16[8,128,128]{2,1,0:T(8,128)(2,1)S(1)} %get-tuple-element.25), channel_id=1, source_target_pairs={{0,2},{1,3},{2,0},{3,1},{4,6},{5,7},{6,4},{7,5},{8,10},{9,11},{10,... | collective-permute-start | bytes 786440 | tf_op jit(solution)/shard_map/ppermute | solution.py:206
  22.2 0.7 pad_add_fusion.s_ref
  22.8 6.2 %shard_map.64.refs_1_ = f32[512,1024]{1,0:T(8,128)} custom-call(s32[2]{0:T(128)} %pad_add_fusion.s_ref, bf16[1024,2048]{1,0:T(8,128)(2,1)} %refs_24_.1, bf16[1024,2048]{1,0:T(8,128)(2,1)} %k_ref.9, bf16[2048,1024]{1,0:T(8,128)(2,1)} %get-tuple-element.28.vt_ref, bf16[16,3,128,128]{3,2,1,0:T(8,128)(2,1)} %get-tuple-element.29.prefix_ref, ...), custom_call_target="tpu_custom_call" | custom-call | flops 2000000000 | bytes 6291456 | tf_op jit(solution)/shard_map/pallas_call | solution.py:111
  29.1 2.6 %collective-permute-start.2 = (bf16[4,128,128]{2,1,0:T(8,128)(2,1)S(1)}, bf16[4,128,128]{2,1,0:T(8,128)(2,1)S(1)}, u32[]{:S(2)}, u32[]{:S(2)}) collective-permute-start(bf16[4,128,128]{2,1,0:T(8,128)(2,1)S(1)} %fusion.2), channel_id=1, source_target_pairs={{0,4},{1,5},{2,6},{3,7},{4,0},{5,1},{6,2},{7,3},{8,12},{9,13},{10,... | collective-permute-start | bytes 393224 | tf_op jit(solution)/shard_map/ppermute | solution.py:206
  31.7 1.4 %collective-permute-start.11 = (bf16[8,128,128]{2,1,0:T(8,128)(2,1)S(1)}, bf16[8,128,128]{2,1,0:T(8,128)(2,1)S(1)}, u32[]{:S(2)}, u32[]{:S(2)}) collective-permute-start(bf16[8,128,128]{2,1,0:T(8,128)(2,1)S(1)} %collective-permute-done.1.refs_2_.refs_10_), channel_id=1, source_target_pairs={{0,1},{1,0},{2,3},{3,2},{4,5},{5,4},{6,7},{7,6},{8,9},{9,8},{10,11... | collective-permute-start | bytes 786440 | tf_op jit(solution)/shard_map/ppermute | solution.py:206
  33.1 6.2 %shard_map.65.refs_9_ = f32[512,1024]{1,0:T(8,128)} custom-call(s32[2]{0:T(128)} %pad_add_fusion.s_ref, bf16[1024,2048]{1,0:T(8,128)(2,1)} %refs_24_.1, bf16[1024,2048]{1,0:T(8,128)(2,1)} %k_ref.9, bf16[2048,1024]{1,0:T(8,128)(2,1)} %get-tuple-element.28.vt_ref, bf16[16,3,128,128]{3,2,1,0:T(8,128)(2,1)} %get-tuple-element.29.prefix_ref, ...), custom_call_target="tpu_custom_call" | custom-call | flops 2000000000 | bytes 6291456 | tf_op jit(solution)/shard_map/pallas_call | solution.py:111
  39.3 1.8 %collective-permute-start.3 = (bf16[4,128,128]{2,1,0:T(8,128)(2,1)S(1)}, bf16[4,128,128]{2,1,0:T(8,128)(2,1)S(1)}, u32[]{:S(2)}, u32[]{:S(2)}) collective-permute-start(bf16[4,128,128]{2,1,0:T(8,128)(2,1)S(1)} %fusion), channel_id=1, source_target_pairs={{0,8},{1,9},{2,10},{3,11},{4,12},{5,13},{6,14},{7,15},{8,0},{9,1},... | collective-permute-start | bytes 393224 | tf_op jit(solution)/shard_map/ppermute | solution.py:206
  41.1 6.2 %shard_map.66.refs_17_ = f32[512,1024]{1,0:T(8,128)} custom-call(s32[2]{0:T(128)} %pad_add_fusion.s_ref, bf16[1024,2048]{1,0:T(8,128)(2,1)} %refs_24_.1, bf16[1024,2048]{1,0:T(8,128)(2,1)} %k_ref.9, bf16[2048,1024]{1,0:T(8,128)(2,1)} %get-tuple-element.28.vt_ref, bf16[16,3,128,128]{3,2,1,0:T(8,128)(2,1)} %get-tuple-element.29.prefix_ref, ...), custom_call_target="tpu_custom_call" | custom-call | flops 2000000000 | bytes 6291456 | tf_op jit(solution)/shard_map/pallas_call | solution.py:111
  47.4 3.5 %collective-permute-start.5 = (bf16[4,128,128]{2,1,0:T(8,128)(2,1)S(1)}, bf16[4,128,128]{2,1,0:T(8,128)(2,1)S(1)}, u32[]{:S(2)}, u32[]{:S(2)}) collective-permute-start(bf16[4,128,128]{2,1,0:T(8,128)(2,1)S(1)} %get-tuple-element.33), channel_id=1, source_target_pairs={{0,16},{1,17},{2,18},{3,19},{4,20},{5,21},{6,22},{7,23},{8,24},{9,... | collective-permute-start | bytes 393224 | tf_op jit(solution)/shard_map/ppermute | solution.py:206
  50.9 0.4 collective-permute-start.4
  51.3 6.2 %shard_map.67.refs_25_ = f32[512,1024]{1,0:T(8,128)} custom-call(s32[2]{0:T(128)} %pad_add_fusion.s_ref, bf16[1024,2048]{1,0:T(8,128)(2,1)} %refs_24_.1, bf16[1024,2048]{1,0:T(8,128)(2,1)} %k_ref.9, bf16[2048,1024]{1,0:T(8,128)(2,1)} %get-tuple-element.28.vt_ref, bf16[16,3,128,128]{3,2,1,0:T(8,128)(2,1)} %get-tuple-element.29.prefix_ref, ...), custom_call_target="tpu_custom_call" | custom-call | flops 2000000000 | bytes 6291456 | tf_op jit(solution)/shard_map/pallas_call | solution.py:111
  57.5 1.5 %collective-permute-start.7 = (bf16[4,128,128]{2,1,0:T(8,128)(2,1)S(1)}, bf16[4,128,128]{2,1,0:T(8,128)(2,1)S(1)}, u32[]{:S(2)}, u32[]{:S(2)}) collective-permute-start(bf16[4,128,128]{2,1,0:T(8,128)(2,1)S(1)} %fusion.1), channel_id=1, source_target_pairs={{0,32},{1,33},{2,34},{3,35},{4,36},{5,37},{6,38},{7,39},{8,40},{9,... | collective-permute-start | bytes 393224 | tf_op jit(solution)/shard_map/ppermute | solution.py:206
  59.1 1.2 collective-permute-start.6
  60.3 1.6 %collective-permute-done.7 = bf16[4,128,128]{2,1,0:T(8,128)(2,1)S(1)} collective-permute-done((bf16[4,128,128]{2,1,0:T(8,128)(2,1)S(1)}, bf16[4,128,128]{2,1,0:T(8,128)(2,1)S(1)}, u32[]{:S(2)}, u32[]{:S(2)}) %collective-permute-start.7) | collective-permute-done | bytes 131104 | tf_op jit(solution)/shard_map/ppermute | solution.py:206
  61.9 3.0 %collective-permute-start.9 = (bf16[4,128,128]{2,1,0:T(8,128)(2,1)S(1)}, bf16[4,128,128]{2,1,0:T(8,128)(2,1)S(1)}, u32[]{:S(2)}, u32[]{:S(2)}) collective-permute-start(bf16[4,128,128]{2,1,0:T(8,128)(2,1)S(1)} %add_convert_fusion), channel_id=1, source_target_pairs={{0,64},{1,65},{2,66},{3,67},{4,68},{5,69},{6,70},{7,71},{8,72},{9,... | collective-permute-start | bytes 393224 | tf_op jit(solution)/shard_map/ppermute | solution.py:206
  64.9 1.2 %collective-permute-start.8 = (bf16[4,128,128]{2,1,0:T(8,128)(2,1)S(1)}, bf16[4,128,128]{2,1,0:T(8,128)(2,1)S(1)}, u32[]{:S(2)}, u32[]{:S(2)}) collective-permute-start(bf16[4,128,128]{2,1,0:T(8,128)(2,1)S(1)} %collective-permute-done.7), channel_id=1, source_target_pairs={{0,2},{1,3},{2,0},{3,1},{4,6},{5,7},{6,4},{7,5},{8,10},{9,11},{10,... | collective-permute-start | bytes 393224 | tf_op jit(solution)/shard_map/ppermute | solution.py:206
  66.2 2.3 %collective-permute-start.12 = (bf16[16,128,128]{2,1,0:T(8,128)(2,1)S(1)}, bf16[16,128,128]{2,1,0:T(8,128)(2,1)S(1)}, u32[]{:S(2)}, u32[]{:S(2)}) collective-permute-start(bf16[16,128,128]{2,1,0:T(8,128)(2,1)S(1)} %constant_dynamic-update-slice_fusion.refs_3_.refs_4_.refs_11_.refs_12_), channel_id=1, source_target_pairs={{0,1},{1,0},{2,3},{3,2},{4,5},{5,4},{6,7},{7,6},{8,9},{9,8},{10,11... | collective-permute-start | bytes 1572872 | tf_op jit(solution)/shard_map/ppermute | solution.py:206
  68.7 0.5 collective-permute-start.10
  69.2 2.1 %collective-permute-done.8 = bf16[4,128,128]{2,1,0:T(8,128)(2,1)S(1)} collective-permute-done((bf16[4,128,128]{2,1,0:T(8,128)(2,1)S(1)}, bf16[4,128,128]{2,1,0:T(8,128)(2,1)S(1)}, u32[]{:S(2)}, u32[]{:S(2)}) %collective-permute-start.8) | collective-permute-done | bytes 131104 | tf_op jit(solution)/shard_map/ppermute | solution.py:206
  71.3 4.7 %collective-permute-start.14 = (bf16[8,128,128]{2,1,0:T(8,128)(2,1)S(1)}, bf16[8,128,128]{2,1,0:T(8,128)(2,1)S(1)}, u32[]{:S(2)}, u32[]{:S(2)}) collective-permute-start(bf16[8,128,128]{2,1,0:T(8,128)(2,1)S(1)} %constant_dynamic-update-slice_fusion.5.refs_6_.refs_14_), channel_id=1, source_target_pairs={{0,1},{1,0},{2,3},{3,2},{4,5},{5,4},{6,7},{7,6},{8,9},{9,8},{10,11... | collective-permute-start | bytes 786440 | tf_op jit(solution)/shard_map/ppermute | solution.py:206
  76.1 1.0 collective-permute-done.10.refs_15_
  77.2 3.4 %collective-permute-start.16 = (bf16[4,128,128]{2,1,0:T(8,128)(2,1)S(1)}, bf16[4,128,128]{2,1,0:T(8,128)(2,1)S(1)}, u32[]{:S(2)}, u32[]{:S(2)}) collective-permute-start(bf16[4,128,128]{2,1,0:T(8,128)(2,1)S(1)} %collective-permute-done.10.refs_15_), channel_id=1, source_target_pairs={{0,1},{1,0},{2,3},{3,2},{4,5},{5,4},{6,7},{7,6},{8,9},{9,8},{10,11... | collective-permute-start | bytes 393224 | tf_op jit(solution)/shard_map/ppermute | solution.py:206
  80.6 1.0 collective-permute-done.16.refs_31_
  81.7 0.5 copy-done.13
  82.5 14.0 %normed.1.n_ref = bf16[1024,2048]{1,0:T(8,128)(2,1)} custom-call(s32[2]{0:T(128)} %pad_add_fusion.s_ref, bf16[1024,2048]{1,0:T(8,128)(2,1)} %refs_24_.1, f32[512,1024]{1,0:T(8,128)} %shard_map.64.refs_1_, bf16[8,128,128]{2,1,0:T(8,128)(2,1)} %copy-done.3, bf16[16,128,128]{2,1,0:T(8,128)(2,1)} %copy-done.1, bf16[16,128,128]{2,1,0:T(8,128)(2,1)} %copy-done.1, ...), custom_call_target="tpu_custom_call" | custom-call | flops 4000000000 | bytes 18874368 | tf_op jit(solution)/shard_map/normed/pallas_call | solution.py:163
  96.6 14.0 %project.1 = bf16[1024,2048]{1,0:T(8,128)(2,1)} custom-call(bf16[1024,2048]{1,0:T(8,128)(2,1)} %normed.1.n_ref, bf16[2048,2048]{1,0:T(8,128)(2,1)} %all-gather.2.cloned.1.call-done.w_ref), custom_call_target="tpu_custom_call" | custom-call | flops 8000000000 | bytes 16777216 | tf_op jit(solution)/shard_map/project/pallas_call | solution.py:188
  (61 shorter events, 1.4 us)
Async XLA Ops:
  6.5 90.0 %all-gather.2.cloned.1.call-start = ((), (), s32[]{:S(2)}) async-start(), calls=%async_computation | async-start | bytes 8454144 | tf_op jit(solution)/shard_map/all_gather | solution.py:223
  7.3 10.7 %copy-start.9 = (bf16[1024,128]{1,0:T(8,128)(2,1)S(1)}, bf16[1024,128]{1,0:T(8,128)(2,1)}, u32[]{:S(2)}) copy-start(bf16[1024,128]{1,0:T(8,128)(2,1)} %param.9) | copy-start | bytes 786436
  16.3 3.1 %collective-permute-start = (bf16[16,128,128]{2,1,0:T(8,128)(2,1)}, bf16[16,128,128]{2,1,0:T(8,128)(2,1)S(1)}, u32[]{:S(2)}, u32[]{:S(2)}) collective-permute-start(bf16[16,128,128]{2,1,0:T(8,128)(2,1)} %get-tuple-element.24), channel_id=1, source_target_pairs={{0,1},{1,0},{2,3},{3,2},{4,5},{5,4},{6,7},{7,6},{8,9},{9,8},{10,11... | collective-permute-start | bytes 1572872 | tf_op jit(solution)/shard_map/ppermute | solution.py:206
  19.5 3.4 %copy-start = (bf16[16,128,128]{2,1,0:T(8,128)(2,1)}, bf16[16,128,128]{2,1,0:T(8,128)(2,1)S(1)}, u32[]{:S(2)}) copy-start(bf16[16,128,128]{2,1,0:T(8,128)(2,1)S(1)} %collective-permute-done.first_ref) | copy-start | bytes 1572868
  20.8 8.3 %collective-permute-start.1 = (bf16[8,128,128]{2,1,0:T(8,128)(2,1)S(1)}, bf16[8,128,128]{2,1,0:T(8,128)(2,1)S(1)}, u32[]{:S(2)}, u32[]{:S(2)}) collective-permute-start(bf16[8,128,128]{2,1,0:T(8,128)(2,1)S(1)} %get-tuple-element.25), channel_id=1, source_target_pairs={{0,2},{1,3},{2,0},{3,1},{4,6},{5,7},{6,4},{7,5},{8,10},{9,11},{10,... | collective-permute-start | bytes 786440 | tf_op jit(solution)/shard_map/ppermute | solution.py:206
  29.0 18.3 %copy-start.3 = (bf16[8,128,128]{2,1,0:T(8,128)(2,1)}, bf16[8,128,128]{2,1,0:T(8,128)(2,1)S(1)}, u32[]{:S(2)}) copy-start(bf16[8,128,128]{2,1,0:T(8,128)(2,1)S(1)} %collective-permute-done.1.refs_2_.refs_10_) | copy-start | bytes 786436
  29.1 10.2 %collective-permute-start.2 = (bf16[4,128,128]{2,1,0:T(8,128)(2,1)S(1)}, bf16[4,128,128]{2,1,0:T(8,128)(2,1)S(1)}, u32[]{:S(2)}, u32[]{:S(2)}) collective-permute-start(bf16[4,128,128]{2,1,0:T(8,128)(2,1)S(1)} %fusion.2), channel_id=1, source_target_pairs={{0,4},{1,5},{2,6},{3,7},{4,0},{5,1},{6,2},{7,3},{8,12},{9,13},{10,... | collective-permute-start | bytes 393224 | tf_op jit(solution)/shard_map/ppermute | solution.py:206
  31.7 44.4 %collective-permute-start.11 = (bf16[8,128,128]{2,1,0:T(8,128)(2,1)S(1)}, bf16[8,128,128]{2,1,0:T(8,128)(2,1)S(1)}, u32[]{:S(2)}, u32[]{:S(2)}) collective-permute-start(bf16[8,128,128]{2,1,0:T(8,128)(2,1)S(1)} %collective-permute-done.1.refs_2_.refs_10_), channel_id=1, source_target_pairs={{0,1},{1,0},{2,3},{3,2},{4,5},{5,4},{6,7},{7,6},{8,9},{9,8},{10,11... | collective-permute-start | bytes 786440 | tf_op jit(solution)/shard_map/ppermute | solution.py:206
  39.3 8.0 %collective-permute-start.3 = (bf16[4,128,128]{2,1,0:T(8,128)(2,1)S(1)}, bf16[4,128,128]{2,1,0:T(8,128)(2,1)S(1)}, u32[]{:S(2)}, u32[]{:S(2)}) collective-permute-start(bf16[4,128,128]{2,1,0:T(8,128)(2,1)S(1)} %fusion), channel_id=1, source_target_pairs={{0,8},{1,9},{2,10},{3,11},{4,12},{5,13},{6,14},{7,15},{8,0},{9,1},... | collective-permute-start | bytes 393224 | tf_op jit(solution)/shard_map/ppermute | solution.py:206
  47.4 10.1 %collective-permute-start.5 = (bf16[4,128,128]{2,1,0:T(8,128)(2,1)S(1)}, bf16[4,128,128]{2,1,0:T(8,128)(2,1)S(1)}, u32[]{:S(2)}, u32[]{:S(2)}) collective-permute-start(bf16[4,128,128]{2,1,0:T(8,128)(2,1)S(1)} %get-tuple-element.33), channel_id=1, source_target_pairs={{0,16},{1,17},{2,18},{3,19},{4,20},{5,21},{6,22},{7,23},{8,24},{9,... | collective-permute-start | bytes 393224 | tf_op jit(solution)/shard_map/ppermute | solution.py:206
  50.9 15.3 %collective-permute-start.4 = (bf16[8,128,128]{2,1,0:T(8,128)(2,1)S(1)}, bf16[8,128,128]{2,1,0:T(8,128)(2,1)S(1)}, u32[]{:S(2)}, u32[]{:S(2)}) collective-permute-start(bf16[8,128,128]{2,1,0:T(8,128)(2,1)S(1)} %pad_maximum_fusion), channel_id=1, source_target_pairs={{0,2},{1,3},{2,0},{3,1},{4,6},{5,7},{6,4},{7,5},{8,10},{9,11},{10,... | collective-permute-start | bytes 786440 | tf_op jit(solution)/shard_map/ppermute | solution.py:206
  57.5 4.3 %collective-permute-start.7 = (bf16[4,128,128]{2,1,0:T(8,128)(2,1)S(1)}, bf16[4,128,128]{2,1,0:T(8,128)(2,1)S(1)}, u32[]{:S(2)}, u32[]{:S(2)}) collective-permute-start(bf16[4,128,128]{2,1,0:T(8,128)(2,1)S(1)} %fusion.1), channel_id=1, source_target_pairs={{0,32},{1,33},{2,34},{3,35},{4,36},{5,37},{6,38},{7,39},{8,40},{9,... | collective-permute-start | bytes 393224 | tf_op jit(solution)/shard_map/ppermute | solution.py:206
  59.1 9.4 %collective-permute-start.6 = (bf16[4,128,128]{2,1,0:T(8,128)(2,1)S(1)}, bf16[4,128,128]{2,1,0:T(8,128)(2,1)S(1)}, u32[]{:S(2)}, u32[]{:S(2)}) collective-permute-start(bf16[4,128,128]{2,1,0:T(8,128)(2,1)S(1)} %collective-permute-done.5), channel_id=1, source_target_pairs={{0,2},{1,3},{2,0},{3,1},{4,6},{5,7},{6,4},{7,5},{8,10},{9,11},{10,... | collective-permute-start | bytes 393224 | tf_op jit(solution)/shard_map/ppermute | solution.py:206
  61.9 6.8 %collective-permute-start.9 = (bf16[4,128,128]{2,1,0:T(8,128)(2,1)S(1)}, bf16[4,128,128]{2,1,0:T(8,128)(2,1)S(1)}, u32[]{:S(2)}, u32[]{:S(2)}) collective-permute-start(bf16[4,128,128]{2,1,0:T(8,128)(2,1)S(1)} %add_convert_fusion), channel_id=1, source_target_pairs={{0,64},{1,65},{2,66},{3,67},{4,68},{5,69},{6,70},{7,71},{8,72},{9,... | collective-permute-start | bytes 393224 | tf_op jit(solution)/shard_map/ppermute | solution.py:206
  64.9 6.3 %collective-permute-start.8 = (bf16[4,128,128]{2,1,0:T(8,128)(2,1)S(1)}, bf16[4,128,128]{2,1,0:T(8,128)(2,1)S(1)}, u32[]{:S(2)}, u32[]{:S(2)}) collective-permute-start(bf16[4,128,128]{2,1,0:T(8,128)(2,1)S(1)} %collective-permute-done.7), channel_id=1, source_target_pairs={{0,2},{1,3},{2,0},{3,1},{4,6},{5,7},{6,4},{7,5},{8,10},{9,11},{10,... | collective-permute-start | bytes 393224 | tf_op jit(solution)/shard_map/ppermute | solution.py:206
  66.2 15.4 %copy-start.1 = (bf16[16,128,128]{2,1,0:T(8,128)(2,1)}, bf16[16,128,128]{2,1,0:T(8,128)(2,1)S(1)}, u32[]{:S(2)}) copy-start(bf16[16,128,128]{2,1,0:T(8,128)(2,1)S(1)} %constant_dynamic-update-slice_fusion.refs_3_.refs_4_.refs_11_.refs_12_) | copy-start | bytes 1572868
  66.2 15.4 %collective-permute-start.12 = (bf16[16,128,128]{2,1,0:T(8,128)(2,1)S(1)}, bf16[16,128,128]{2,1,0:T(8,128)(2,1)S(1)}, u32[]{:S(2)}, u32[]{:S(2)}) collective-permute-start(bf16[16,128,128]{2,1,0:T(8,128)(2,1)S(1)} %constant_dynamic-update-slice_fusion.refs_3_.refs_4_.refs_11_.refs_12_), channel_id=1, source_target_pairs={{0,1},{1,0},{2,3},{3,2},{4,5},{5,4},{6,7},{7,6},{8,9},{9,8},{10,11... | collective-permute-start | bytes 1572872 | tf_op jit(solution)/shard_map/ppermute | solution.py:206
  68.5 13.1 %copy-start.4 = (bf16[8,128,128]{2,1,0:T(8,128)(2,1)}, bf16[8,128,128]{2,1,0:T(8,128)(2,1)S(1)}, u32[]{:S(2)}) copy-start(bf16[8,128,128]{2,1,0:T(8,128)(2,1)S(1)} %constant_dynamic-update-slice_fusion.3.refs_5_.refs_13_) | copy-start | bytes 786436
  68.5 12.0 %collective-permute-start.13 = (bf16[8,128,128]{2,1,0:T(8,128)(2,1)S(1)}, bf16[8,128,128]{2,1,0:T(8,128)(2,1)S(1)}, u32[]{:S(2)}, u32[]{:S(2)}) collective-permute-start(bf16[8,128,128]{2,1,0:T(8,128)(2,1)S(1)} %constant_dynamic-update-slice_fusion.3.refs_5_.refs_13_), channel_id=1, source_target_pairs={{0,1},{1,0},{2,3},{3,2},{4,5},{5,4},{6,7},{7,6},{8,9},{9,8},{10,11... | collective-permute-start | bytes 786440 | tf_op jit(solution)/shard_map/ppermute | solution.py:206
  68.7 12.9 %copy-start.10 = (bf16[4,128,128]{2,1,0:T(8,128)(2,1)}, bf16[4,128,128]{2,1,0:T(8,128)(2,1)S(1)}, u32[]{:S(2)}) copy-start(bf16[4,128,128]{2,1,0:T(8,128)(2,1)S(1)} %collective-permute-done.9.refs_7_) | copy-start | bytes 393220
  68.7 8.5 %collective-permute-start.10 = (bf16[4,128,128]{2,1,0:T(8,128)(2,1)S(1)}, bf16[4,128,128]{2,1,0:T(8,128)(2,1)S(1)}, u32[]{:S(2)}, u32[]{:S(2)}) collective-permute-start(bf16[4,128,128]{2,1,0:T(8,128)(2,1)S(1)} %collective-permute-done.9.refs_7_), channel_id=1, source_target_pairs={{0,2},{1,3},{2,0},{3,1},{4,6},{5,7},{6,4},{7,5},{8,10},{9,11},{10,... | collective-permute-start | bytes 393224 | tf_op jit(solution)/shard_map/ppermute | solution.py:206
  71.3 10.3 %copy-start.5 = (bf16[8,128,128]{2,1,0:T(8,128)(2,1)}, bf16[8,128,128]{2,1,0:T(8,128)(2,1)S(1)}, u32[]{:S(2)}) copy-start(bf16[8,128,128]{2,1,0:T(8,128)(2,1)S(1)} %constant_dynamic-update-slice_fusion.5.refs_6_.refs_14_) | copy-start | bytes 786436
  71.3 10.3 %collective-permute-start.14 = (bf16[8,128,128]{2,1,0:T(8,128)(2,1)S(1)}, bf16[8,128,128]{2,1,0:T(8,128)(2,1)S(1)}, u32[]{:S(2)}, u32[]{:S(2)}) collective-permute-start(bf16[8,128,128]{2,1,0:T(8,128)(2,1)S(1)} %constant_dynamic-update-slice_fusion.5.refs_6_.refs_14_), channel_id=1, source_target_pairs={{0,1},{1,0},{2,3},{3,2},{4,5},{5,4},{6,7},{7,6},{8,9},{9,8},{10,11... | collective-permute-start | bytes 786440 | tf_op jit(solution)/shard_map/ppermute | solution.py:206
  76.0 5.6 %copy-start.6 = (bf16[8,128,128]{2,1,0:T(8,128)(2,1)}, bf16[8,128,128]{2,1,0:T(8,128)(2,1)S(1)}, u32[]{:S(2)}) copy-start(bf16[8,128,128]{2,1,0:T(8,128)(2,1)S(1)} %collective-permute-done.11.refs_18_.refs_26_) | copy-start | bytes 786436
  76.0 4.5 %collective-permute-start.15 = (bf16[4,128,128]{2,1,0:T(8,128)(2,1)S(1)}, bf16[4,128,128]{2,1,0:T(8,128)(2,1)S(1)}, u32[]{:S(2)}, u32[]{:S(2)}) collective-permute-start(bf16[4,128,128]{2,1,0:T(8,128)(2,1)S(1)} %collective-permute-done.9.refs_7_), channel_id=1, source_target_pairs={{0,1},{1,0},{2,3},{3,2},{4,5},{5,4},{6,7},{7,6},{8,9},{9,8},{10,11... | collective-permute-start | bytes 393224 | tf_op jit(solution)/shard_map/ppermute | solution.py:206
  77.2 4.5 %copy-start.11 = (bf16[4,128,128]{2,1,0:T(8,128)(2,1)}, bf16[4,128,128]{2,1,0:T(8,128)(2,1)S(1)}, u32[]{:S(2)}) copy-start(bf16[4,128,128]{2,1,0:T(8,128)(2,1)S(1)} %collective-permute-done.10.refs_15_) | copy-start | bytes 393220
  77.2 4.4 %collective-permute-start.16 = (bf16[4,128,128]{2,1,0:T(8,128)(2,1)S(1)}, bf16[4,128,128]{2,1,0:T(8,128)(2,1)S(1)}, u32[]{:S(2)}, u32[]{:S(2)}) collective-permute-start(bf16[4,128,128]{2,1,0:T(8,128)(2,1)S(1)} %collective-permute-done.10.refs_15_), channel_id=1, source_target_pairs={{0,1},{1,0},{2,3},{3,2},{4,5},{5,4},{6,7},{7,6},{8,9},{9,8},{10,11... | collective-permute-start | bytes 393224 | tf_op jit(solution)/shard_map/ppermute | solution.py:206
  80.6 1.1 copy-start.12
  80.6 1.1 copy-start.7
  81.6 0.6 copy-start.13
  81.6 0.8 copy-start.8
  81.6 0.9 copy-start.2
Sparse Core Ops, SparseCore 0:
  10.3 76.1 all-gather.1
